TPU v7x, 32 devices: a whole 2x2x4 slice. The times are simulated.
32 devices in a mesh: rep: 4 (over y, core), fsdp: 8 (over z, x).
Axes of the slice: x: 2, y: 2, z: 4, core: 2. Of those that a mesh axis runs over, the one named last changes fastest.
Arguments:
- visual: bfloat16 [32, 128, 768], P(('rep', 'fsdp')), may hold values from -6 to 6
- text: bfloat16 [32, 1280, 768], P(('rep', 'fsdp')), may hold values from -6 to 6
- visual_valid: int32 [32, 128], P(('rep', 'fsdp')), may hold values from 0 to 1, as said below
- block_owner: int32 [32, 1280], P(('rep', 'fsdp')), may hold values from 0 to 127, as said below
- cross_query: bfloat16 [768, 768], P('fsdp'), may hold values from -0.21875 to 0.21875
- cross_keyval: bfloat16 [768, 1536], P('fsdp'), may hold values from -0.21875 to 0.21875
- cross_output: bfloat16 [768, 768], P('fsdp'), may hold values from -0.625 to 0.625
- gate_weight: bfloat16 [1536, 768], P('fsdp'), may hold values from -0.15625 to 0.15625
- self_qkv: bfloat16 [768, 2304], P('fsdp'), may hold values from -0.21875 to 0.21875
- self_output: bfloat16 [768, 768], P('fsdp'), may hold values from -0.875 to 0.875
- ffn_up: bfloat16 [768, 3072], P('fsdp'), may hold values from -0.21875 to 0.21875
- ffn_down: bfloat16 [3072, 768], P('fsdp'), may hold values from -0.109375 to 0.109375
- norm_gains: float32 [3072], P('fsdp'), may hold values from 0.5 to 1.5
- norm_biases: float32 [3072], P('fsdp'), may hold values from -1.8 to 1.8
- cotangent: bfloat16 [32, 128, 768], P(('rep', 'fsdp')), may hold values from -6 to 6
Outputs:
- layer_out: bfloat16 [32, 128, 768], P(('rep', 'fsdp'))
- grad_visual: float32 [32, 128, 768], P(('rep', 'fsdp'))
- grad_text: float32 [32, 1280, 768], P(('rep', 'fsdp'))
- grad_cross_query: float32 [768, 768], P('fsdp')
- grad_cross_keyval: float32 [768, 1536], P('fsdp')
- grad_cross_output: float32 [768, 768], P('fsdp')
- grad_gate_weight: float32 [1536, 768], P('fsdp')
- grad_self_qkv: float32 [768, 2304], P('fsdp')
- grad_self_output: float32 [768, 768], P('fsdp')
- grad_ffn_up: float32 [768, 3072], P('fsdp')
- grad_ffn_down: float32 [3072, 768], P('fsdp')
- grad_norm_gains: float32 [3072], P('fsdp')
- grad_norm_biases: float32 [3072], P('fsdp')
Inputs may be any that keep to these rules, and one draw needn't show every extreme that they name: `visual_valid`: in every page the real visual blocks come first and the padded ones last; each page has at least a quarter of 128 real blocks and at least one padded block. `block_owner`: each visual block of a page owns exactly 10 of that page's text blocks.
All inputs are finite; a program needn't handle non-finite values.
Results may differ from a plain program's by a relative error of at most 0.04.
Values may be sent and summed in bfloat16 or wider, within the bound.
No kernel may reach another device: no remote copies, remote signals or barrier semaphores. Data moves between devices by JAX's collectives and lax.ppermute only.
A program may use at most 192 MiB of HBM per device.

v0:
```python
import functools

import jax
import jax.numpy as jnp
from jax import lax
from jax.experimental import pallas as pl
from jax.experimental.pallas import tpu as pltpu
from jax.sharding import PartitionSpec as P

H = 12
HD = 64
D = H * HD
HALF = D // 2
QUART = D // 4
WIDE = -(-3 * QUART // 128) * 128
BF = jnp.bfloat16
F32 = jnp.float32

epsilon = 1e-05
filtered_logits = -1000000000.0
shared_sheet_reward = 6.0
SCALE = HD ** (-0.5)
VM = pl.BlockSpec()
SM = pl.BlockSpec(memory_space=pltpu.SMEM)
ANY = pl.BlockSpec(memory_space=pl.ANY)


def sds(shape, dtype=BF):
    return jax.ShapeDtypeStruct(tuple(shape), dtype)


def size_of(a):
    n = jnp.dtype(a.dtype).itemsize
    for d in a.shape:
        n *= d
    return n


class Order:
    def __init__(self):
        self.tokens = []

    def start(self, exchange, a, *args):
        a, *self.tokens = lax.optimization_barrier((a, *self.tokens))
        return exchange(a, *args)

    def wait(self, *arrays):
        self.tokens = self.tokens + list(arrays)

    def run(self, body, outs, where, *ins, name=None, scratch=(), grid=None, in_specs=None, out_specs=None, vmem=None, prefetch=False, far=False):
        moved = sum(size_of(a) for a in ins) + sum(size_of(o) for o in outs)
        held = moved + sum(size_of(s) for s in scratch)
        limit = 66_000_000 if far else vmem << 20 if vmem else min(60 << 20, int(1.25 * held) + (10 << 20))
        ins_specs = ([VM] * len(ins) if in_specs is None else in_specs) + [ANY] * len(self.tokens)
        spec = dict(in_specs=([] if prefetch else [SM]) + ins_specs,
                    out_specs=([VM] * len(outs) if out_specs is None else out_specs) + [pl.BlockSpec((8, 128), lambda *_: (0, 0)) if grid else VM],
                    scratch_shapes=[pltpu.VMEM(s.shape, s.dtype) for s in scratch])
        if prefetch:
            spec = dict(grid_spec=pltpu.PrefetchScalarGridSpec(num_scalar_prefetch=1, grid=grid, **spec))
        elif grid is not None:
            spec["grid"] = grid
        kernel, count, late = body, len(ins), len(self.tokens)
        if far:
            spec["in_specs"] = [SM] + [pl.BlockSpec(memory_space=pltpu.HBM)] * count + [ANY] * late
            spec["scratch_shapes"] = [pltpu.VMEM(a.shape, a.dtype) for a in ins] + [pltpu.SemaphoreType.DMA((count,))]

            def kernel(at, *refs):
                held, sems = refs[-1 - count : -1], refs[-1]
                copies = [pltpu.make_async_copy(refs[i], held[i], sems.at[i]) for i in range(count)]
                for one in copies:
                    one.start()
                for one in copies:
                    one.wait()
                body(at, *held, *refs[count : -1 - count])

        ends = count + late + len(outs)

        def marked(at, *refs):
            refs[ends][...] = jnp.zeros((8, 128), F32)
            kernel(at, *refs[:count], *refs[count + late : ends], *refs[ends + 1 :])

        *got, mark = pl.pallas_call(
            marked,
            out_shape=list(outs) + [sds((8, 128), F32)],
            compiler_params=pltpu.CompilerParams(vmem_limit_bytes=limit),
            cost_estimate=pl.CostEstimate(flops=0, bytes_accessed=1024, transcendentals=0),
            name=name,
            **spec,
        )(where, *ins, *self.tokens)
        self.tokens = [mark]
        return got


T, C, X, Z = 0, 1, 2, 3


class Links:
    def __init__(self, reps, shards):
        self.reps, self.shards = reps, shards
        self.depth = shards // 2
        rank = lax.axis_index("rep")
        shard = lax.axis_index("fsdp")
        self.shard = shard
        self.at = jnp.stack([(rank // 2) % 2, rank % 2, shard % 2, shard // 2]).astype(jnp.int32)

    def core(self, a):
        return lax.ppermute(a, "rep", [(r, r ^ 1) for r in range(self.reps)])

    def y(self, a):
        return lax.ppermute(a, "rep", [(r, r ^ 2) for r in range(self.reps)])

    def rep_bit(self, a, bit):
        return lax.ppermute(a, "rep", [(r, r ^ bit) for r in range(self.reps)])

    def across(self, a):
        return lax.ppermute(a, "fsdp", [(s, s ^ 1) for s in range(self.shards)])

    def along(self, a, k):
        return lax.ppermute(a, "fsdp", [(s, s ^ (2 * k)) for s in range(self.shards)])


def mm(a, b):
    return jnp.dot(a, b, preferred_element_type=F32)


def nt(a, b):
    return lax.dot_general(a, b, (((1,), (1,)), ((), ())), preferred_element_type=F32)


def tn(a, b):
    return lax.dot_general(a, b, (((0,), (0,)), ((), ())), preferred_element_type=F32)


def stats(rows):
    mean = jnp.mean(rows, -1, keepdims=True)
    centred = rows - mean
    factor = lax.rsqrt(jnp.mean(centred * centred, -1, keepdims=True) + epsilon)
    return centred * factor, factor


def norm_back(grad, normal, factor, gain):
    scaled = grad * gain
    dx = scaled - jnp.mean(scaled, -1, keepdims=True) - normal * jnp.mean(scaled * normal, -1, keepdims=True)
    return dx * factor, jnp.sum(grad * normal, 0, keepdims=True), jnp.sum(grad, 0, keepdims=True)


def gain_of(ref, i):
    return ref[:, i * D : (i + 1) * D]


def half(i):
    return pl.ds(pl.multiple_of(i * HALF, 128), HALF)


def pair_masks(rows):
    lane = lax.broadcasted_iota(jnp.int32, (rows, 128), 1)
    return lane < HD


def two_heads(a):
    first = pair_masks(a.shape[0])
    zero = jnp.zeros_like(a)
    return jnp.concatenate([jnp.where(first, a, zero), jnp.where(first, zero, a)], 0)


def one_pair(a):
    n = a.shape[0] // 2
    return jnp.where(pair_masks(n), a[:n], a[n:])


def softmax(scores):
    peak = jnp.max(scores, -1, keepdims=True)
    expo = jnp.exp(scores - peak)
    total = jnp.sum(expo, -1, keepdims=True)
    return expo / total, peak + jnp.log(total)


def pack_a(at, query, keyval, gains, biases, part):
    rows, size = query.shape[0], gains.shape[0]
    part[:rows, :HALF] = keyval[:, pl.ds(pl.multiple_of(at[T] * D + at[C] * HALF, 128), HALF)]
    part[:rows, HALF:] = query[:, half(at[C])]
    part[rows:, :] = jnp.zeros((16, D), BF)
    g, b = gains[...].reshape(1, size), biases[...].reshape(1, size)
    g_hi, b_hi = g.astype(BF), b.astype(BF)
    g_lo, b_lo = (g - g_hi.astype(F32)).astype(BF), (b - b_hi.astype(F32)).astype(BF)
    row = lax.broadcasted_iota(jnp.int32, (16, size), 0)
    out = jnp.zeros((16, size), F32)
    for i, v in enumerate((g_hi, g_lo, b_hi, b_lo)):
        out = jnp.where(row == i, jnp.broadcast_to(v.astype(F32), (16, size)), out)
    part[rows:, HALF : HALF + size] = out.astype(BF)


def pack_rest(at, output, gate, qkv, self_out, up, down, cot, valid, part_b, part_c, part_d, page):
    rows = output.shape[0]
    n = cot.shape[0]
    page[:n] = cot[...]
    page[n:, :n] = jnp.broadcast_to(valid[...], (8, n)).astype(F32).astype(BF)
    page[n:, n:] = jnp.zeros((8, D - n), BF)
    shards = D // rows
    t0, c0 = at[T] == 0, at[C] == 0
    gate_c, out_c, self_c = gate[:, half(at[C])], output[:, half(at[C])], self_out[:, half(at[C])]
    part_b[:, :HALF] = jnp.where(t0, gate_c[:rows], gate_c[rows:])
    part_b[:, HALF:D] = jnp.where(t0, out_c, self_c)
    pieces = []
    for i in range(3):
        v = qkv[:, pl.ds(pl.multiple_of(i * D + at[T] * HALF, 128), HALF)]
        pieces.append(jnp.where(c0, v[:, :QUART], v[:, QUART:]))
    part_c[...] = jnp.concatenate(pieces + [jnp.zeros((rows, WIDE - 3 * QUART), BF)], 1)
    pieces = []
    for s in range(shards):
        v = [up[:, (s * 4 + g) * rows : (s * 4 + g + 1) * rows] for g in range(4)]
        pieces.append(jnp.where(t0, jnp.where(c0, v[0], v[1]), jnp.where(c0, v[2], v[3])))
    part_d[:, :D] = jnp.concatenate(pieces, 1)
    v = [down[g * rows : (g + 1) * rows, :] for g in range(4)]
    part_d[:, D:] = jnp.where(t0, jnp.where(c0, v[0], v[1]), jnp.where(c0, v[2], v[3]))


def column(at, *refs):
    for k, piece in enumerate(refs[:-1]):
        refs[-1][at[Z] ^ k] = piece[...]


def column_a(at, *refs):
    kv, qn = refs[-2:]
    rows = kv.shape[1]
    for k, piece in enumerate(refs[:-2]):
        kv[at[Z] ^ k] = piece[:rows, :HALF]
        qn[at[Z] ^ k] = piece[:, HALF:]


def column_rest(at, *refs):
    whole, rest = refs[-2:]
    for k, piece in enumerate(refs[:-2]):
        whole[at[Z] ^ k] = piece[...]
        if k:
            rest[k - 1] = piece[...]


def join_rest(at, mine, other_own, other_rest, out):
    depth = mine.shape[0]
    for z in range(depth):
        out[z, at[X]] = mine[z]
    for k in range(depth):
        out[at[Z] ^ k, 1 - at[X]] = other_own[...] if k == 0 else other_rest[k - 1]


def join(at, mine, other, out):
    for src, side in ((mine, at[X]), (other, 1 - at[X])):
        for z in range(mine.shape[0]):
            out[z, side] = src[z]


def join_b(at, mine, other, y_mine, y_other, out):
    for i, pair in enumerate(((mine, other), (y_mine, y_other))):
        for src, side in zip(pair, (at[X], 1 - at[X])):
            for z in range(src.shape[0]):
                out[i, z, side] = src[z]


def join_a(at, kvm, kvo, kym, kyo, qm, qo, out, gains, biases):
    _three, depth, _two, rows, _n = out.shape
    size = 4 * D // (2 * depth)
    for i, pair in enumerate(((kvm, kvo), (kym, kyo), (qm, qo))):
        for src, side in zip(pair, (at[X], 1 - at[X])):
            for z in range(depth):
                out[i, z, side] = src[z, :rows]
    first = at[X] == 0
    for z in range(depth):
        a, b = qm[z, rows:, :size].astype(F32), qo[z, rows:, :size].astype(F32)
        for i, v in enumerate((jnp.where(first, a, b), jnp.where(first, b, a))):
            s = (z * 2 + i) * size
            gains[:, s : s + size] = v[0:1] + v[1:2]
            biases[:, s : s + size] = v[2:3] + v[3:4]


def place_b(at, own, came, cross_out, self_out, gate):
    t, c = at[T], at[C]
    for src, cc in ((own, c), (came, 1 - c)):
        for i in range(2):
            gate[:, t ^ i, :, half(cc)] = src[i, :, :, :HALF]
        cross_out[:, :, half(cc)] = src[t, :, :, HALF:]
        self_out[:, :, half(cc)] = src[1 - t, :, :, HALF:]


def normed_kernel(at, text, visual, gains, biases, text_normed, normed):
    normal, _f = stats(text[...].astype(F32))
    text_normed[...] = (normal * gain_of(gains, 1) + gain_of(biases, 1)).astype(BF)
    normal, _f = stats(visual[...].astype(F32))
    normed[...] = (normal * gain_of(gains, 0) + gain_of(biases, 0)).astype(BF)


def keyval_kernel(at, text_normed, normed, own, came, kv, w_kv, w_q, queries):
    t, c = at[T], at[C]

    @pl.when(pl.program_id(0) == 0)
    def _():
        for src, cc in ((own, c), (came, 1 - c)):
            for i in range(2):
                w_kv[:, pl.ds(pl.multiple_of((t ^ i) * D + cc * HALF, 128), HALF)] = src[i]
            w_q[:, half(cc)] = src[2]
        queries[...] = mm(normed[...], w_q[...]).astype(BF)

    kv[...] = mm(text_normed[...], w_kv[...]).astype(BF)


def cross_bias(owner, valid):
    n, m = valid.shape[1], owner.shape[1]
    parent = owner[...] == lax.broadcasted_iota(jnp.int32, (n, m), 0)
    ones = jnp.where(parent, 1.0, 0.0).astype(BF)
    real = jnp.broadcast_to(valid[...].astype(F32), (8, n)).astype(BF)
    present = mm(real, ones)[0:1] > 0.5
    return jnp.where(parent, shared_sheet_reward, 0.0) + jnp.where(present, 0.0, filtered_logits)


def cross_fwd(owner, valid, q, k, v, out, logs, bias):
    @pl.when(pl.program_id(0) == 0)
    def _():
        bias[...] = cross_bias(owner, valid)

    b = bias[...]
    scores = nt(two_heads(q[...]), k[...]) * SCALE + jnp.concatenate([b, b], 0)
    weight, log = softmax(scores)
    logs[0] = log
    out[...] = one_pair(mm(weight.astype(BF), v[...])).astype(BF)


def gate_kernel(at, mixed, normed, visual, gains, biases, w_out, w_gate, cross, gate, joined, second):
    rows = mm(mixed[...], w_out[...]).astype(BF)
    cross[...] = rows
    g = jax.nn.sigmoid(mm(normed[...], w_gate[:D]) + mm(rows, w_gate[D:]))
    gate[...] = g
    j = visual[...].astype(F32) + g * rows.astype(F32)
    joined[...] = j
    normal, _f = stats(j)
    second[...] = (normal * gain_of(gains, 2) + gain_of(biases, 2)).astype(BF)


def head_order(at, a):
    return jnp.where(at[C] == 0, a, jnp.concatenate([a[:, QUART:], a[:, :QUART]], 1))


def self_bias(page):
    n = page.shape[0] - 8
    return jnp.where(page[n : n + 8, :n].astype(F32)[0:1] > 0.5, 0.0, filtered_logits)


def self_fwd(at, second0, second1, valid0, valid1, w_own, w_oth, triple, att0, att1):
    n = second0.shape[0]
    rows = jnp.concatenate([second0[...], second1[...]], 0)
    own, oth = [mm(rows, w[...]).astype(BF) for w in (w_own, w_oth)]
    for i in range(3):
        triple[:, i * HALF : (i + 1) * HALF] = jnp.concatenate(
            [own[:, i * QUART : (i + 1) * QUART], oth[:, i * QUART : (i + 1) * QUART]], 1)
    for page, (valid, att) in enumerate(((valid0, att0), (valid1, att1))):
        bias = self_bias(valid)
        r = slice(page * n, (page + 1) * n)
        outs = []
        for p in range(3):
            q, k, v = [triple[r, i * HALF + p * 128 : i * HALF + (p + 1) * 128] for i in range(3)]
            weight, _l = softmax(nt(two_heads(q), k) * SCALE + bias)
            outs.append(one_pair(mm(weight.astype(BF), v)).astype(BF))
        att[...] = head_order(at, jnp.concatenate(outs, 1))


def carry_kernel(at, mine, came, joined, gains, biases, w, attended, carried, third):
    attended[:, half(at[T])] = mine[...]
    attended[:, half(1 - at[T])] = came[...]
    c = joined[...] + mm(attended[...], w[...])
    carried[...] = c
    normal, _f = stats(c)
    third[...] = (normal * gain_of(gains, 3) + gain_of(biases, 3)).astype(BF)


def ffn_kernel(last, at, third0, third1, cot0, cot1, w, *refs):
    n = third0.shape[0]
    if last:
        y0i, y1i, d0i, d1i, y0, y1, d0, d1, grad = refs
    else:
        y0, y1, d0, d1, grad = refs
    rows = jnp.concatenate([third0[...], third1[...]], 0)
    cot = jnp.concatenate([cot0[:n], cot1[:n]], 0)
    up, down = w[:, :D], w[:, D:]
    v = mm(rows, up)
    k = (2.0 / 3.141592653589793) ** 0.5
    th = jnp.tanh(k * (v + 0.044715 * (v * v * v)))
    act = (0.5 * v * (1.0 + th)).astype(BF)
    slope = 0.5 * (1.0 + th) + 0.5 * v * (1.0 - th * th) * (k * (1.0 + 3.0 * 0.044715 * (v * v)))
    y = mm(act, down)
    grad[:, D:] = tn(act, cot).astype(BF)
    dl = (nt(cot, down) * slope).astype(BF)
    d = nt(dl, up)
    grad[:, :D] = tn(rows, dl).astype(BF)
    if last:
        y0[...] = y[:n] + y0i[...]
        y1[...] = (y[n:] + y1i[...]).astype(BF)
        d0[...] = d[:n] + d0i[...]
        d1[...] = (d[n:] + d1i[...]).astype(BF)
    else:
        y0[...], y1[...], d0[...], d1[...] = y[:n], y[n:], d[:n], d[n:]


def carry_back(at, d0, came, carried, cot, attended, gains, w, d_carried, mine, send, grad, sums):
    normal, factor = stats(carried[...])
    dx, gain, bias = norm_back(d0[...] + came[...].astype(F32), normal, factor, gain_of(gains, 3))
    dc = cot[...].astype(F32) + dx
    d_carried[...] = dc
    low = dc.astype(BF)
    da = nt(low, w[...]).astype(BF)
    t0 = at[T] == 0
    mine[...] = head_order(at, jnp.where(t0, da[:, :HALF], da[:, HALF:]))
    send[...] = head_order(at, jnp.where(t0, da[:, HALF:], da[:, :HALF]))
    grad[...] = tn(attended[...], low).astype(BF)
    sums[0:1], sums[1:2] = gain, bias


def self_back(at, triple, da0, da1, valid0, valid1, second0, second1, w_own, w_oth, d0, d1, g_own, g_oth, dt):
    n = second0.shape[0]

    @pl.loop(0, 3)
    def _(p):
        lanes = [pl.ds(pl.multiple_of(i * HALF + p * 128, 128), 128) for i in range(3)]
        for page, (valid, da) in enumerate(((valid0, da0), (valid1, da1))):
            bias = self_bias(valid)
            r = slice(page * n, (page + 1) * n)
            q, k, v = [triple[r, lane] for lane in lanes]
            qq = two_heads(q)
            dd = two_heads(da[:, lanes[0]])
            weight, _l = softmax(nt(qq, k) * SCALE + bias)
            dp = nt(dd, v)
            ds = (weight * (dp - jnp.sum(weight * dp, -1, keepdims=True))).astype(BF)
            grads = (one_pair(mm(ds, k)) * SCALE, tn(ds, qq) * SCALE, tn(weight.astype(BF), dd))
            for i in range(3):
                dt[r, lanes[i]] = grads[i].astype(BF)

    none = jnp.zeros((2 * n, WIDE - 3 * QUART), BF)
    own = jnp.concatenate([dt[:, i * HALF : i * HALF + QUART] for i in range(3)] + [none], 1)
    oth = jnp.concatenate([dt[:, i * HALF + QUART : (i + 1) * HALF] for i in range(3)] + [none], 1)
    rows = jnp.concatenate([second0[...], second1[...]], 0)
    g_own[...] = tn(rows, own).astype(BF).reshape(g_own.shape)
    g_oth[...] = tn(rows, oth).astype(BF).reshape(g_oth.shape)
    d = nt(own, w_own[...]) + nt(oth, w_oth[...])
    d0[...] = d[:n]
    d1[...] = d[n:].astype(BF)


def gate_back(at, d_carried, d0, came, joined, normed, cross, gate, mixed, gains, w_gate, w_out, g_self,
              d_joined, d_mixed, d_normed, keep, send, sums):
    t, c = at[T], at[C]
    rows = keep.shape[2]
    normal, factor = stats(joined[...])
    dx, gain, bias = norm_back(d0[...] + came[...].astype(F32), normal, factor, gain_of(gains, 2))
    dj = d_carried[...] + dx
    d_joined[...] = dj
    sums[0:1], sums[1:2] = gain, bias
    g = gate[...]
    dg = (dj * cross[...].astype(F32) * g * (1.0 - g)).astype(BF)
    d_normed[...] = nt(dg, w_gate[:D])
    dc = (dj * g + nt(dg, w_gate[D:])).astype(BF)
    d_mixed[...] = nt(dc, w_out[...]).astype(BF)
    g_gate = jnp.concatenate([tn(normed[...], dg).astype(BF), tn(cross[...], dg).astype(BF)], 0)
    g_gate = g_gate.reshape(D // rows, 2, rows, D)
    g_out = tn(mixed[...], dc).astype(BF).reshape(D // rows, rows, D)
    g_so = g_self[...].reshape(D // rows, rows, D)
    for tt in range(2):
        for cc in range(2):
            lanes = slice(cc * HALF, (cc + 1) * HALF)
            side = g_out if tt == 0 else g_so
            for out, same in ((keep, True), (send, False)):
                @pl.when((c == cc) == same)
                def _():
                    out[t ^ tt, :, :, :HALF] = g_gate[:, tt, :, lanes]
                    out[t ^ tt, :, :, HALF:] = side[:, :, lanes]


def cross_back(owner, valid, q, k, v, dm, logs, dq, dkv, bias):
    @pl.when(pl.program_id(0) == 0)
    def _():
        bias[...] = cross_bias(owner, valid)

    b = bias[...]
    qq, dd = two_heads(q[...]), two_heads(dm[...])
    scores = nt(qq, k[...]) * SCALE + jnp.concatenate([b, b], 0)
    weight = jnp.exp(scores - logs[0])
    dp = nt(dd, v[...])
    ds = (weight * (dp - jnp.sum(weight * dp, -1, keepdims=True))).astype(BF)
    dq[...] = (one_pair(mm(ds, k[...])) * SCALE).astype(BF)
    dkv[0] = (tn(ds, qq) * SCALE).astype(BF)
    dkv[1] = tn(weight.astype(BF), dd).astype(BF)


def cross_weights(at, text_normed, normed, dq, dkv, grad):
    t = at[T]

    @pl.loop(0, 3)
    def _(j):
        lanes = pl.ds(pl.multiple_of(j * 256, 256), 256)
        x = text_normed[:, lanes]
        grad[t, lanes] = tn(x, dkv[0]).astype(BF)
        grad[1 - t, lanes] = tn(x, dkv[1]).astype(BF)
        grad[2, lanes] = tn(normed[:, lanes], dq[...]).astype(BF)


def text_back(at, text, gains, w_kv, own, oth, grad, sums):
    c = at[C]
    d = nt(own[0], w_kv[:, half(c)])
    d = d + nt(oth[0], w_kv[:, half(1 - c)])
    d = d + nt(own[1], w_kv[:, pl.ds(pl.multiple_of(D + c * HALF, 128), HALF)])
    d = d + nt(oth[1], w_kv[:, pl.ds(pl.multiple_of(D + (1 - c) * HALF, 128), HALF)])
    normal, factor = stats(text[...].astype(F32))
    dx, gain, bias = norm_back(d, normal, factor, gain_of(gains, 1))
    grad[...] = dx

    @pl.when(pl.program_id(0) == 0)
    def _():
        sums[...] = jnp.zeros_like(sums)

    sums[0:1] += gain
    sums[1:2] += bias


def visual_back(at, d_normed, dq_own, dq_oth, w_q, visual, d_joined, gains, s1, s2, s3, grad, norms):
    c = at[C]
    depth = norms.shape[0]
    size = 4 * D // (2 * depth)
    d = d_normed[...] + nt(dq_own[...], w_q[:, half(c)]) + nt(dq_oth[...], w_q[:, half(1 - c)])
    normal, factor = stats(visual[...].astype(F32))
    dx, gain, bias = norm_back(d, normal, factor, gain_of(gains, 0))
    grad[...] = d_joined[...] + dx
    g = jnp.concatenate([gain, s1[0:1], s2[0:1], s3[0:1]], 1)
    b = jnp.concatenate([bias, s1[1:2], s2[1:2], s3[1:2]], 1)
    row = lax.broadcasted_iota(jnp.int32, (8, size), 0)
    norms[...] = jnp.zeros_like(norms)
    for s in range(2 * depth):
        lanes = slice(s * size, (s + 1) * size)
        v = jnp.where(row == 0, jnp.broadcast_to(g[:, lanes], (8, size)), jnp.broadcast_to(b[:, lanes], (8, size)))
        norms[s // 2, s % 2, :, :size] = jnp.where(row < 2, v, 0.0).astype(BF)


def finish_ab(at, r, ry, rc, ryc, g_query, g_keyval, gains, biases):
    t, c = at[T], at[C]
    rows, size = g_query.shape[0], gains.shape[0]
    for a, b, cc in ((r, ry, c), (rc, ryc, 1 - c)):
        g_keyval[:, pl.ds(pl.multiple_of(t * D + cc * HALF, 128), HALF)] = a[:rows, :HALF].astype(F32)
        g_keyval[:, pl.ds(pl.multiple_of((1 - t) * D + cc * HALF, 128), HALF)] = b[:rows, :HALF].astype(F32)
        g_query[:, half(cc)] = a[:rows, HALF:].astype(F32) + b[:rows, HALF:].astype(F32)
    norms = [a[rows:, :size].astype(F32) for a in (r, ry, rc, ryc)]
    norms = norms[0] + norms[1] + norms[2] + norms[3]
    gains[...] = norms[0:1].reshape(size)
    biases[...] = norms[1:2].reshape(size)


def in_order(at, groups, lanes):
    c0, t0 = at[C] == 0, at[T] == 0
    own, y, core, both = [r[:, lanes].astype(F32) for r in groups]
    a0, a1 = jnp.where(c0, own, core), jnp.where(c0, core, own)
    b0, b1 = jnp.where(c0, y, both), jnp.where(c0, both, y)
    return jnp.where(t0, a0, b0), jnp.where(t0, a1, b1), jnp.where(t0, b0, a0), jnp.where(t0, b1, a1)


def finish_cd(at, r, ry, rc, ryc, g_qkv, g_up, g_down):
    groups = (r, ry, rc, ryc)
    rows = g_qkv.shape[0]
    p = in_order(at, groups, slice(0, D))
    for i in range(4):
        g_down[i * rows : (i + 1) * rows] = p[i]
    for s in range(D // rows):
        p = in_order(at, groups, slice(D + s * rows, D + (s + 1) * rows))
        g_up[:, s * 4 * rows : (s + 1) * 4 * rows] = jnp.concatenate(p, 1)
    for i in range(3):
        p = in_order(at, groups, slice(2 * D + i * QUART, 2 * D + (i + 1) * QUART))
        g_qkv[:, i * D : (i + 1) * D] = jnp.concatenate(p, 1)


def finish_b(at, r, ry, rc, ryc, g_out, g_gate, g_self):
    groups = (r, ry, rc, ryc)
    rows = g_out.shape[0]
    p = in_order(at, groups, slice(0, HALF))
    for i in range(4):
        g_gate[(i // 2) * rows : (i // 2 + 1) * rows, (i % 2) * HALF : (i % 2 + 1) * HALF] = p[i]
    p = in_order(at, groups, slice(HALF, D))
    g_out[...] = jnp.concatenate(p[:2], 1)
    g_self[...] = jnp.concatenate(p[2:], 1)


def reduce_x(count, extra, lanes, at, *refs):
    out = refs[-1]
    m = extra[0] if extra else 0
    for z in range(out.shape[0]):
        out[z] = reduced(refs, count, m, lanes, z, 1 - at[X]).astype(BF)


def reduced(refs, count, m, lanes, z, side):
    acc = refs[0][z, side, :, lanes].astype(F32)
    for r in refs[1:count]:
        acc = acc + r[z, side, :, lanes].astype(F32)
    if m:
        y = refs[count]
        y = (y[z, side] if len(y.shape) == 4 else y[z]).astype(F32)
        acc = acc + y if y.shape == acc.shape else jnp.concatenate([acc[:, :m] + y, acc[:, m:]], 1)
    return acc


def reduce_z(count, extra, lanes, at, *refs):
    got, keep, send = refs[-3:]
    m = extra[0] if extra else 0
    for i in range(keep.shape[0]):
        for k, out in ((2 * i, keep), (2 * i + 1, send)):
            z = at[Z] ^ k
            out[i] = (reduced(refs, count, m, lanes, z, at[X]) + got[z].astype(F32)).astype(BF)


def reduce_x_proj(at, own, oth, norms, out):
    rows = own.shape[2]
    for z in range(out.shape[0]):
        out[z, :rows] = reduced((own, oth), 1, oth.shape[-1], slice(None), z, 1 - at[X]).astype(BF)
        out[z, rows:] = norms[z, 1 - at[X]]


def reduce_z_proj(at, own, oth, norms, got, keep, send):
    rows = own.shape[2]
    for i in range(keep.shape[0]):
        for k, out in ((2 * i, keep), (2 * i + 1, send)):
            z = at[Z] ^ k
            b = got[z].astype(F32)
            out[i, :rows] = (reduced((own, oth), 1, oth.shape[-1], slice(None), z, at[X]) + b[:rows]).astype(BF)
            out[i, rows:] = (norms[z, at[X]].astype(F32) + b[rows:]).astype(BF)


def reduce_more(at, keep, got, *outs):
    for i in range(keep.shape[0]):
        v = (keep[i].astype(F32) + got[i].astype(F32)).astype(BF)
        if len(outs) == 1:
            outs[0][...] = v
        else:
            outs[i % 2][i // 2] = v


def reduce_last(count, at, *refs):
    out = refs[-1]
    at_lane = 0
    for keep, got in zip(refs[0 : 2 * count : 2], refs[1 : 2 * count : 2]):
        rows, n = keep.shape[1:]
        out[:rows, at_lane : at_lane + n] = (keep[0].astype(F32) + got[0].astype(F32)).astype(BF)
        at_lane += n


def add_core_b(at, keep, came, own, oth_send, oth_keep):
    x = at[X]
    for z in range(own.shape[0]):
        for i in range(2):
            own[z, i] = (keep[0, z, i].astype(F32) + came[0, z, i].astype(F32)).astype(BF)
        oth_send[z] = (keep[1, z, 1 - x].astype(F32) + came[1, z, 1 - x].astype(F32)).astype(BF)
        oth_keep[z] = (keep[1, z, x].astype(F32) + came[1, z, x].astype(F32)).astype(BF)


def add_core_a(at, keep, came, own, oth, q):
    for out, i in ((own, 0), (oth, 1), (q, 2)):
        out[...] = (keep[i].astype(F32) + came[i].astype(F32)).astype(BF)


def add_out(at, carried, y0, came, out):
    out[...] = (carried[...] + y0[...] + came[...].astype(F32)).astype(BF)


def local(reps, shards, visual, text, visual_valid, block_owner, cross_query, cross_keyval, cross_output, gate_weight,
          self_qkv, self_output, ffn_up, ffn_down, norm_gains, norm_biases, cotangent):
    ln = Links(reps, shards)
    at = ln.at
    od = Order()
    run = od.run
    visual, text, cotangent = visual[0], text[0], cotangent[0]
    rows, size = cross_query.shape[0], norm_gains.shape[0]
    vis, txt = visual.shape[0], text.shape[0]
    depth = shards // 2
    w3 = WIDE
    whole = lambda shape: pl.BlockSpec(shape, lambda *_: (0,) * len(shape))
    page = sds((vis, D), F32)
    grid4 = lambda n: (depth, 2, rows, n)

    def far_first(part):
        pieces = {0: part}
        for k in range(depth - 1, 0, -1):
            if k & (k - 1) == 0:
                pieces[k] = od.start(ln.along, part, k)
        return pieces

    def passed_on(pieces):
        for k in sorted(range(1, depth), key=lambda k: (bin(k).count("1"), -k)):
            if k not in pieces:
                od.wait(*[pieces[i] for i in sorted(pieces) if i])
                pieces[k] = od.start(ln.along, pieces[k & (k - 1)], k & -k)
        return [pieces[k] for k in range(depth)]

    (part_a,) = run(pack_a, [sds((rows + 16, D))], at, cross_query, cross_keyval, norm_gains, norm_biases, name="pack_a", far=True)
    pieces_a = far_first(part_a)
    part_b, part_c, part_d, cot = run(
        pack_rest, [sds((rows, D)), sds((rows, w3)), sds((rows, 2 * D)), sds((vis + 8, D))], at,
        cross_output, gate_weight, self_qkv, self_output, ffn_up, ffn_down, cotangent, visual_valid,
        name="pack_rest", far=True)
    d_xo, cot_y = ln.across(part_d), ln.y(cot)
    pieces_a = passed_on(pieces_a)
    od.wait(d_xo, cot_y)
    kv_m, qn_m = run(column_a, [sds((depth, rows, HALF)), sds((depth, rows + 16, HALF))], at, *pieces_a, name="column_a")
    kv_o, qn_o, kv_ym = ln.across(kv_m), ln.across(qn_m), ln.y(kv_m)
    pieces_b = passed_on(far_first(part_b))
    od.wait(kv_o)
    kv_yo = ln.y(kv_o)
    pieces_c = far_first(part_c)
    (b_m,) = run(column, [sds((depth, rows, D))], at, *pieces_b, name="column_b")
    joined_a, gains, biases = run(
        join_a, [sds((3,) + grid4(HALF)), sds((1, 4 * D), F32), sds((1, 4 * D), F32)],
        at, kv_m, kv_o, kv_ym, kv_yo, qn_m, qn_o, name="join_a")
    joined_a = joined_a.reshape(3, D, HALF)
    came_a = ln.core(joined_a)
    b_o, b_ym = od.start(ln.across, b_m), od.start(ln.y, b_m)
    tile = txt // 5
    row_tile = pl.BlockSpec((tile, D), lambda i: (i, 0))
    text_normed, normed = run(
        normed_kernel, [sds((txt, D)), sds((vis, D))], at, text, visual, gains, biases,
        grid=(5,), in_specs=[row_tile, whole((vis, D)), whole((1, 4 * D)), whole((1, 4 * D))],
        out_specs=[row_tile, whole((vis, D))], name="normed", vmem=12)
    pieces_c = passed_on(pieces_c)
    od.wait(came_a)
    pieces_d = far_first(part_d)

    kv, w_kv, w_q, queries = run(
        keyval_kernel, [sds((txt, 2 * D)), sds((D, 2 * D)), sds((D, D)), sds((vis, D))],
        at, text_normed, normed, joined_a, came_a,
        grid=(5,), in_specs=[row_tile, whole((vis, D)), whole((3, D, HALF)), whole((3, D, HALF))],
        out_specs=[pl.BlockSpec((tile, 2 * D), lambda i: (i, 0)), whole((D, 2 * D)), whole((D, D)), whole((vis, D))],
        name="keyval", vmem=30)
    (c_m,) = run(column, [sds((depth, rows, w3))], at, *pieces_c, name="column_c")
    od.wait(b_o, b_ym)
    c_o, b_yo = od.start(ln.across, c_m), od.start(ln.y, b_o)
    pairs = H // 2
    col = lambda n, off=0: pl.BlockSpec((n, 128), lambda p: (0, p + off))
    mixed, logs = run(
        lambda at, *refs: cross_fwd(*refs), [sds((vis, D)), sds((pairs, 2 * vis, 1), F32)],
        at, block_owner, visual_valid, queries, kv, kv,
        grid=(pairs,), in_specs=[whole((1, txt)), whole((1, vis)), col(vis), col(txt), col(txt, pairs)],
        out_specs=[col(vis), pl.BlockSpec((1, 2 * vis, 1), lambda p: (p, 0, 0))],
        scratch=[sds((vis, txt), F32)], name="cross_fwd", vmem=16)
    pieces_d = passed_on(pieces_d)
    (wc_own,) = run(join, [sds(grid4(w3))], at, c_m, c_o, name="join_c")
    wc_oth = ln.core(wc_own)
    (joined_b,) = run(join_b, [sds((2,) + grid4(D))], at, b_m, b_o, b_ym, b_yo, name="join_b")
    joined_b = joined_b.reshape(2, shards, rows, D)
    came_b = ln.core(joined_b)
    w_out, w_self, w_gate = run(
        place_b, [sds((shards, rows, D)), sds((shards, rows, D)), sds((shards, 2, rows, D))], at, joined_b, came_b, name="place_b")
    w_out, w_self, w_gate = w_out.reshape(D, D), w_self.reshape(D, D), w_gate.reshape(2 * D, D)
    od.wait(wc_oth)
    wc_own, wc_oth = wc_own.reshape(D, w3), wc_oth.reshape(D, w3)
    cross, gate, joined, second = run(
        gate_kernel, [sds((vis, D)), page, page, sds((vis, D))],
        at, mixed, normed, visual, gains, biases, w_out, w_gate, name="gate")
    second_y = ln.y(second)
    d_m, d_rest = run(column_rest, [sds((depth, rows, 2 * D)), sds((depth - 1, rows, 2 * D))], at, *pieces_d, name="column_d")
    d_xr, d_cm, d_cxo = ln.across(d_rest), ln.core(d_m), od.start(ln.core, d_xo)
    triple, att_mine, att_send = run(
        self_fwd, [sds((2 * vis, 3 * HALF)), sds((vis, HALF)), sds((vis, HALF))],
        at, second, second_y, cot, cot_y, wc_own, wc_oth, name="self_fwd")
    att_came = ln.y(att_send)
    od.wait(d_cm, d_cxo)
    attended, carried, third = run(
        carry_kernel, [sds((vis, D)), page, sds((vis, D))],
        at, att_mine, att_came, joined, gains, biases, w_self, name="carry")
    third_y = ln.y(third)
    od.wait(third_y)
    d_cxr = od.start(ln.core, d_xr)
    (wd_own,) = run(join_rest, [sds(grid4(2 * D))], at, d_m, d_xo, d_xr, name="join_d")
    (wd_oth,) = run(join_rest, [sds(grid4(2 * D))], at, d_cm, d_cxo, d_cxr, name="join_d")
    wd_own, wd_oth = wd_own.reshape(D, 2 * D), wd_oth.reshape(D, 2 * D)

    y0, y1, d0, d1, gd_oth = run(
        functools.partial(ffn_kernel, False), [page] * 4 + [sds((D, 2 * D))],
        at, third, third_y, cot, cot_y, wd_oth, name="ffn_first")
    gd_came = ln.core(gd_oth).reshape(grid4(2 * D))
    y0, y1, d0, d1, gd_own = run(
        functools.partial(ffn_kernel, True), [page, sds((vis, D))] * 2 + [sds((D, 2 * D))],
        at, third, third_y, cot, cot_y, wd_own, y0, y1, d0, d1, name="ffn_second")
    gd_own = gd_own.reshape(grid4(2 * D))
    d1_came = ln.y(d1)

    class Sum:
        def __init__(self, name, arrays, n, lanes=slice(None), sends=(), keeps=(), norms=None):
            self.name, self.n, self.rows = name, n, arrays[0].shape[2]
            extra = [a.shape[-1] for a in keeps]
            first, self.second = [functools.partial(f, len(arrays), extra, lanes) for f in (reduce_x, reduce_z)]
            self.late = list(arrays) + list(keeps)
            early = list(arrays) + list(sends)
            if norms is not None:
                first, self.second, self.rows = reduce_x_proj, reduce_z_proj, self.rows + norms.shape[2]
                self.late, early = self.late + [norms], early + [norms]
            (self.send,) = run(first, [sds((depth, self.rows, n))], at, *early, name="reduce_x_" + name)
            self.bit = 0

        def go(self):
            self.got = od.start(ln.across, self.send)
            return self

        def step(self):
            if self.bit == 0:
                outs = [sds((depth // 2, self.rows, self.n))] * 2
                self.keep, send = run(self.second, outs, at, *self.late, self.got, name="reduce_z_" + self.name)
                self.bit = 1
            elif self.keep.shape[0] > 1:
                outs = [sds((self.keep.shape[0] // 2, self.rows, self.n))] * 2
                self.keep, send = run(reduce_more, outs, at, self.keep, self.got, name="reduce_m_" + self.name)
                self.bit *= 2
            else:
                return False
            self.got = ln.along(send, self.bit)
            return True

    def finish(*sums):
        ins = [a for one in sums for a in (one.keep, one.got)]
        (total,) = run(functools.partial(reduce_last, len(sums)), [sds((sums[0].rows, sum(one.n for one in sums)))], at,
                       *ins, name="reduce_last")
        for bit in range(2, reps.bit_length() - 1):
            total = (total.astype(F32) + ln.rep_bit(total, 1 << bit).astype(F32)).astype(BF)
        ry = ln.y(total)
        return total, ry, ln.core(total), ln.core(ry)

    def back_half(index):
        def spec(n, off=0):
            return pl.BlockSpec((n, 128), lambda p, at: (0, (at[C] ^ index) * 3 + p + off))

        return run(
            lambda at, *refs: cross_back(*refs), [sds((vis, HALF)), sds((2, txt, HALF))],
            at, block_owner, visual_valid, queries, kv, kv, d_mixed, logs, prefetch=True, grid=(3,),
            in_specs=[whole((1, txt)), whole((1, vis)), spec(vis), spec(txt), spec(txt, pairs), spec(vis),
                      pl.BlockSpec((1, 2 * vis, 1), lambda p, at: ((at[C] ^ index) * 3 + p, 0, 0))],
            out_specs=[pl.BlockSpec((vis, 128), lambda p, at: (0, p)), pl.BlockSpec((2, txt, 128), lambda p, at: (0, 0, p))],
            scratch=[sds((vis, txt), F32)], name="cross_back", vmem=20)

    def weights_half(dq, dkv):
        return run(cross_weights, [sds((3, D, HALF))], at, text_normed, normed, dq, dkv, name="cross_weights")[0]

    down = Sum("down", [gd_own, gd_came], D, slice(D, 2 * D)).go()
    d_carried, da_mine, da_send, g_self, sums3 = run(
        carry_back, [page, sds((vis, HALF)), sds((vis, HALF)), sds((D, D)), sds((2, D), F32)],
        at, d0, d1_came, carried, cotangent, attended, gains, w_self, name="carry_back")
    da_came = ln.y(da_send)
    up = Sum("up", [gd_own, gd_came], D, slice(0, D))
    od.wait(da_came)
    down.step()
    up.go()
    ds0, ds1, gc_own, gc_oth = run(
        self_back, [page, sds((vis, D)), sds(grid4(w3)), sds(grid4(w3))],
        at, triple, da_mine, da_came, cot, cot_y, second, second_y, wc_own, wc_oth,
        scratch=[sds((2 * vis, 3 * HALF))], name="self_back")
    ds1_came = ln.y(ds1)
    gc_came = ln.core(gc_oth)
    down.step()
    up.step()
    d_joined, d_mixed, d_normed, b_keep, b_send, sums2 = run(
        gate_back, [page, sds((vis, D)), page, sds((2, shards, rows, D)), sds((2, shards, rows, D)), sds((2, D), F32)],
        at, d_carried, ds0, ds1_came, joined, normed, cross, gate, mixed, gains, w_gate, w_out, g_self, name="gate_back")
    b_came = ln.core(b_send)
    y1_came = od.start(ln.y, y1)
    dq_oth, dkv_oth = back_half(1)
    qkv = Sum("qkv", [gc_own, gc_came], w3).go()
    od.wait(y1_came)
    own_b, b_ys, b_yk = run(
        add_core_b, [sds(grid4(D)), sds((depth, rows, D)), sds((depth, rows, D))], at,
        b_keep.reshape((2,) + grid4(D)), b_came.reshape((2,) + grid4(D)), name="add_core_b")
    b_ys = ln.y(b_ys)
    a_came = ln.core(weights_half(dq_oth, dkv_oth))
    dq_own, dkv_own = back_half(0)
    up.step()
    gates = Sum("gate", [own_b], D, sends=[b_ys], keeps=[b_yk]).go()
    qkv.step()
    a_keep = weights_half(dq_own, dkv_own)
    od.wait(down.got)
    own_a, a_y, own_q = run(
        add_core_a, [sds(grid4(HALF))] * 3, at,
        a_keep.reshape((3,) + grid4(HALF)), a_came.reshape((3,) + grid4(HALF)), name="add_core_a")
    a_y = ln.y(a_y)
    query = Sum("query", [own_q], HALF).go()
    row3 = pl.BlockSpec((2, tile, HALF), lambda i: (0, i, 0))
    grad_text, sums1 = run(
        text_back, [sds((txt, D), F32), sds((2, D), F32)],
        at, text, gains, w_kv, dkv_own, dkv_oth,
        grid=(5,), in_specs=[row_tile, whole((1, 4 * D)), whole((D, 2 * D)), row3, row3],
        out_specs=[row_tile, whole((2, D))], name="text_back", vmem=24)
    od.wait(up.got, gates.got)
    qkv.step()
    query.step()
    grad_visual, norms = run(
        visual_back, [page, sds((depth, 2, 8, HALF))],
        at, d_normed, dq_own, dq_oth, w_q, visual, d_joined, gains, sums1, sums2, sums3, name="visual_back")
    keyval = Sum("keyval", [own_a], HALF, sends=[a_y], keeps=[a_y], norms=norms).go()
    gates.late[1] = od.start(ln.y, b_yk)
    (layer_out,) = run(add_out, [sds((vis, D))], at, carried, y0, y1_came, name="add_out")
    query.step()
    keyval.step()
    first = finish(down, up, qkv)
    od.wait(query.got)
    keyval.step()
    gates.step()
    out = lambda r, n: sds((r, n), F32)
    last_a = finish(keyval, query)
    gates.step()
    g_qkv, g_up, g_down = run(
        finish_cd, [out(rows, 3 * D), out(rows, 4 * D), out(4 * rows, D)], at, *first, name="finish_cd")
    last_b = finish(gates)
    g_query, g_keyval, g_gains, g_biases = run(
        finish_ab, [out(rows, D), out(rows, 2 * D), sds((size,), F32), sds((size,), F32)], at, *last_a, name="finish_a")
    g_out, g_gate, g_self_out = run(
        finish_b, [out(rows, D), out(2 * rows, D), out(rows, D)], at, *last_b, name="finish_b")
    return (layer_out[None], grad_visual[None], grad_text[None], g_query, g_keyval, g_out, g_gate, g_qkv, g_self_out,
            g_up, g_down, g_gains, g_biases)


def solution(mesh):
    pages = P(("rep", "fsdp"), None, None)
    flags = P(("rep", "fsdp"), None)
    matrix = P("fsdp", None)
    vector = P("fsdp")
    in_specs = (pages, pages, flags, flags) + (matrix,) * 8 + (vector, vector, pages)
    out_specs = (pages, pages, pages) + (matrix,) * 8 + (vector, vector)
    reps, shards = mesh.shape["rep"], mesh.shape["fsdp"]

    def program(*args):
        return local(reps, shards, *args)

    return jax.shard_map(program, mesh=mesh, in_specs=in_specs, out_specs=out_specs, check_vma=False)
```

profile of v0, /device:TPU:1, one launch (start us, length us, event | category | flops | bytes accessed | tf_op | source)
XLA Modules:
  0.0 263.4 jit_solution(13872157338804777827)
XLA Ops:
  8.4 4.1 %pack_rest.1 = (bf16[96,768]{1,0:T(8,128)(2,1)}, bf16[96,640]{1,0:T(8,128)(2,1)}, bf16[96,1536]{1,0:T(8,128)(2,1)}, bf16[136,768]{1,0:T(8,128)(2,1)}, f32[8,128]{1,0:T(8,128)}) custom-call(s32[4]{0:T(128)} %pad_add_fusion.at, bf16[96,768]{1,0:T(8,128)(2,1)} %refs_0_.6, bf16[192,768]{1,0:T(8,128)(2,1)} %refs_1_.6, bf16[96,2304]{1,0:T(8,128)(2,1)} %refs_2_.3, ...), custom_call_target="tpu_custom_call" | custom-call | bytes 1024 | tf_op jit(solution)/shard_map/pack_rest/pallas_call | solution.py:82
  30.4 5.0 %collective-permute-done.11.refs_3_ = bf16[96,768]{1,0:T(8,128)(2,1)S(1)} collective-permute-done((bf16[96,768]{1,0:T(8,128)(2,1)S(1)}, bf16[96,768]{1,0:T(8,128)(2,1)S(1)}, u32[]{:S(2)}, u32[]{:S(2)}) %collective-permute-start.11) | collective-permute-done | bytes 147488 | tf_op jit(solution)/shard_map/ppermute | solution.py:119
  37.6 5.8 %collective-permute-start.12 = (bf16[3,768,384]{2,1,0:T(8,128)(2,1)S(1)}, bf16[3,768,384]{2,1,0:T(8,128)(2,1)S(1)}, u32[]{:S(2)}, u32[]{:S(2)}) collective-permute-start(bf16[3,768,384]{2,1,0:T(8,128)(2,1)S(1)} %bitcast.54), channel_id=1, source_target_pairs={{0,8},{8,0},{16,24},{24,16},{1,9},{9,1},{17,25},{25,17},{2,10},{10... | collective-permute-start | bytes 5308424 | tf_op jit(solution)/shard_map/ppermute | solution.py:107
  50.2 3.4 %collective-permute-start.16 = (bf16[96,640]{1,0:T(8,128)(2,1)S(1)}, bf16[96,640]{1,0:T(8,128)(2,1)S(1)}, u32[]{:S(2)}, u32[]{:S(2)}) collective-permute-start(bf16[96,640]{1,0:T(8,128)(2,1)S(1)} %collective-permute-done.13.refs_6_.refs_2_), channel_id=1, source_target_pairs={{0,2},{1,3},{2,0},{3,1},{4,6},{5,7},{6,4},{7,5},{8,10},{9,11},{10,... | collective-permute-start | bytes 368648 | tf_op jit(solution)/shard_map/ppermute | solution.py:119
  53.7 5.2 %keyval.1 = (bf16[1280,1536]{1,0:T(8,128)(2,1)S(1)}, bf16[768,1536]{1,0:T(8,128)(2,1)S(1)}, bf16[768,768]{1,0:T(8,128)(2,1)S(1)}, bf16[128,768]{1,0:T(8,128)(2,1)S(1)}, f32[8,128]{1,0:T(8,128)S(1)}) custom-call(s32[4]{0:T(128)S(1)} %copy-done.3, bf16[1280,768]{1,0:T(8,128)(2,1)S(1)} %get-tuple-element.298.refs_0_, ...), custom_call_target="tpu_custom_call" | custom-call | bytes 1024 | tf_op jit(solution)/shard_map/keyval/pallas_call | solution.py:82
  62.6 7.5 %cross_fwd.1 = (bf16[128,768]{1,0:T(8,128)(2,1)S(1)}, f32[6,256,1]{2,1,0:T(8,128)S(1)}, f32[8,128]{1,0:T(8,128)S(1)}) custom-call(s32[4]{0:T(128)S(1)} %copy-done.3, s32[1,1280]{1,0:T(1,128)S(1)} %copy-done.9, s32[1,128]{1,0:T(1,128)S(1)} %copy-done.10, bf16[128,768]{1,0:T(8,128)(2,1)S(1)} %get-tuple-element.315.refs_2_, ...), custom_call_target="tpu_custom_call" | custom-call | bytes 1024 | tf_op jit(solution)/shard_map/cross_fwd/pallas_call | solution.py:82
  70.1 4.6 %collective-permute-done.21.refs_3_.refs_1_ = bf16[96,1536]{1,0:T(8,128)(2,1)S(1)} collective-permute-done((bf16[96,1536]{1,0:T(8,128)(2,1)S(1)}, bf16[96,1536]{1,0:T(8,128)(2,1)S(1)}, u32[]{:S(2)}, u32[]{:S(2)}) %collective-permute-start.21) | collective-permute-done | bytes 294944 | tf_op jit(solution)/shard_map/ppermute | solution.py:119
  76.1 3.6 %collective-permute-start.22 = (bf16[2,8,96,768]{3,2,1,0:T(8,128)(2,1)S(1)}, bf16[2,8,96,768]{3,2,1,0:T(8,128)(2,1)S(1)}, u32[]{:S(2)}, u32[]{:S(2)}) collective-permute-start(bf16[2,8,96,768]{3,2,1,0:T(8,128)(2,1)S(1)} %bitcast.48), channel_id=1, source_target_pairs={{0,8},{8,0},{16,24},{24,16},{1,9},{9,1},{17,25},{25,17},{2,10},{10... | collective-permute-start | bytes 7077896 | tf_op jit(solution)/shard_map/ppermute | solution.py:107
  79.9 3.9 %collective-permute-done.22.refs_1_ = bf16[2,8,96,768]{3,2,1,0:T(8,128)(2,1)S(1)} collective-permute-done((bf16[2,8,96,768]{3,2,1,0:T(8,128)(2,1)S(1)}, bf16[2,8,96,768]{3,2,1,0:T(8,128)(2,1)S(1)}, u32[]{:S(2)}, u32[]{:S(2)}) %collective-permute-start.22) | collective-permute-done | bytes 2359328 | tf_op jit(solution)/shard_map/ppermute | solution.py:107
  91.8 5.5 %collective-permute-done.24.refs_1_.refs_6_ = bf16[128,768]{1,0:T(8,128)(2,1)S(1)} collective-permute-done((bf16[128,768]{1,0:T(8,128)(2,1)S(1)}, bf16[128,768]{1,0:T(8,128)(2,1)S(1)}, u32[]{:S(2)}, u32[]{:S(2)}) %collective-permute-start.24) | collective-permute-done | bytes 196640 | tf_op jit(solution)/shard_map/ppermute | solution.py:110
  99.5 3.7 %collective-permute-done.26.refs_1_ = bf16[128,384]{1,0:T(8,128)(2,1)S(1)} collective-permute-done((bf16[128,384]{1,0:T(8,128)(2,1)S(1)}, bf16[128,384]{1,0:T(8,128)(2,1)S(1)}, u32[]{:S(2)}, u32[]{:S(2)}) %collective-permute-start.26) | collective-permute-done | bytes 98336 | tf_op jit(solution)/shard_map/ppermute | solution.py:110
  104.4 6.8 %collective-permute-done.30.refs_2_ = bf16[3,96,1536]{2,1,0:T(8,128)(2,1)S(1)} collective-permute-done((bf16[3,96,1536]{2,1,0:T(8,128)(2,1)S(1)}, bf16[3,96,1536]{2,1,0:T(8,128)(2,1)S(1)}, u32[]{:S(2)}, u32[]{:S(2)}) %collective-permute-start.30) | collective-permute-done | bytes 884768 | tf_op jit(solution)/shard_map/ppermute | solution.py:116
  124.2 5.8 %collective-permute-done.32.refs_1_ = bf16[128,768]{1,0:T(8,128)(2,1)S(1)} collective-permute-done((bf16[128,768]{1,0:T(8,128)(2,1)S(1)}, bf16[128,768]{1,0:T(8,128)(2,1)S(1)}, u32[]{:S(2)}, u32[]{:S(2)}) %collective-permute-start.32) | collective-permute-done | bytes 196640 | tf_op jit(solution)/shard_map/ppermute | solution.py:110
  139.7 5.6 %self_back.1 = (f32[128,768]{1,0:T(8,128)S(1)}, bf16[128,768]{1,0:T(8,128)(2,1)S(1)}, bf16[4,2,96,640]{3,2,1,0:T(8,128)(2,1)S(1)}, bf16[4,2,96,640]{3,2,1,0:T(8,128)(2,1)S(1)}, f32[8,128]{1,0:T(8,128)S(1)}) custom-call(s32[4]{0:T(128)S(1)} %copy-done.3, bf16[256,1152]{1,0:T(8,128)(2,1)S(1)} %get-tuple-element.383.refs_0_, ...), custom_call_target="tpu_custom_call" | custom-call | bytes 1024 | tf_op jit(solution)/shard_map/self_back/pallas_call | solution.py:82
  147.4 4.7 %collective-permute-done.37.refs_2_ = bf16[4,96,768]{2,1,0:T(8,128)(2,1)S(1)} collective-permute-done((bf16[4,96,768]{2,1,0:T(8,128)(2,1)S(1)}, bf16[4,96,768]{2,1,0:T(8,128)(2,1)S(1)}, u32[]{:S(2)}, u32[]{:S(2)}) %collective-permute-start.37) | collective-permute-done | bytes 589856 | tf_op jit(solution)/shard_map/ppermute | solution.py:116
  152.8 3.7 %gate_back.1 = (f32[128,768]{1,0:T(8,128)S(1)}, bf16[128,768]{1,0:T(8,128)(2,1)S(1)}, f32[128,768]{1,0:T(8,128)S(1)}, bf16[2,8,96,768]{3,2,1,0:T(8,128)(2,1)S(1)...) custom-call(s32[4]{0:T(128)S(1)} %copy-done.3, ...), custom_call_target="tpu_custom_call" | custom-call | bytes 1024 | tf_op jit(solution)/shard_map/gate_back/pallas_call | solution.py:82
  158.8 5.8 %cross_back.2 = (bf16[128,384]{1,0:T(8,128)(2,1)S(1)}, bf16[2,1280,384]{2,1,0:T(8,128)(2,1)S(1)}, f32[8,128]{1,0:T(8,128)S(1)}) custom-call(s32[4]{0:T(128)S(1)} %copy-done.3, s32[1,1280]{1,0:T(1,128)S(1)} %copy-done.9, s32[1,128]{1,0:T(1,128)S(1)} %copy-done.10, bf16[128,768]{1,0:T(8,128)(2,1)S(1)} %get-tuple-element.315.refs_2_, ...), custom_call_target="tpu_custom_call" | custom-call | bytes 1024 | tf_op jit(solution)/shard_map/cross_back/pallas_call | solution.py:82
  166.4 3.4 %cross_weights.2 = (bf16[3,768,384]{2,1,0:T(8,128)(2,1)S(1)}, f32[8,128]{1,0:T(8,128)S(1)}) custom-call(s32[4]{0:T(128)S(1)} %copy-done.3, bf16[1280,768]{1,0:T(8,128)(2,1)S(1)} %get-tuple-element.298.refs_0_, bf16[128,768]{1,0:T(8,128)(2,1)S(1)} %get-tuple-element.299.refs_1_.refs_4_, bf16[128,384]{1,0:T(8,128)(2,1)S(1)} %get-tuple-element.415.refs_2_, ...), custom_call_target="tpu_custom_call" | custom-call | bytes 1024 | tf_op jit(solution)/shard_map/cross_weights/pallas_call | solution.py:82
  175.6 5.8 %cross_back.3 = (bf16[128,384]{1,0:T(8,128)(2,1)S(1)}, bf16[2,1280,384]{2,1,0:T(8,128)(2,1)S(1)}, f32[8,128]{1,0:T(8,128)S(1)}) custom-call(s32[4]{0:T(128)S(1)} %copy-done.3, s32[1,1280]{1,0:T(1,128)S(1)} %copy-done.9, s32[1,128]{1,0:T(1,128)S(1)} %copy-done.10, bf16[128,768]{1,0:T(8,128)(2,1)S(1)} %get-tuple-element.315.refs_2_, ...), custom_call_target="tpu_custom_call" | custom-call | bytes 1024 | tf_op jit(solution)/shard_map/cross_back/pallas_call | solution.py:82
  188.2 3.4 %cross_weights.3 = (bf16[3,768,384]{2,1,0:T(8,128)(2,1)S(1)}, f32[8,128]{1,0:T(8,128)S(1)}) custom-call(s32[4]{0:T(128)S(1)} %copy-done.3, bf16[1280,768]{1,0:T(8,128)(2,1)S(1)} %get-tuple-element.298.refs_0_, bf16[128,768]{1,0:T(8,128)(2,1)S(1)} %get-tuple-element.299.refs_1_.refs_4_, bf16[128,384]{1,0:T(8,128)(2,1)S(1)} %get-tuple-element.419.refs_2_.refs_1_, ...), custom_call_target="tpu_custom_call" | custom-call | bytes 1024 | tf_op jit(solution)/shard_map/cross_weights/pallas_call | solution.py:82
  197.4 8.1 %text_back.1 = (f32[1280,768]{1,0:T(8,128)}, f32[2,768]{1,0:T(2,128)S(1)}, f32[8,128]{1,0:T(8,128)S(1)}) custom-call(s32[4]{0:T(128)S(1)} %copy-done.3, bf16[1280,768]{1,0:T(8,128)(2,1)S(1)} %bitcast.38, f32[1,3072]{1,0:T(1,128)S(1)} %get-tuple-element.292.refs_2_.refs_3_.refs_5_.refs_8_.refs_1_.refs_6_, bf16[768,1536]{1,0:T(8,128)(2,1)S(1)} %get-tuple-element.439.refs_2_, ...), custom_call_target="tpu_custom_call" | custom-call | bytes 1024 | tf_op jit(solution)/shard_map/text_back/pallas_call | solution.py:82
  228.9 4.6 %collective-permute-start.65 = (bf16[96,2176]{1,0:T(8,128)(2,1)S(1)}, bf16[96,2176]{1,0:T(8,128)(2,1)S(1)}, u32[]{:S(2)}, u32[]{:S(2)}) collective-permute-start(bf16[96,2176]{1,0:T(8,128)(2,1)S(1)} %get-tuple-element.487.refs_0_), channel_id=1, source_target_pairs={{0,8},{8,0},{16,24},{24,16},{1,9},{9,1},{17,25},{25,17},{2,10},{10... | collective-permute-start | bytes 1253384 | tf_op jit(solution)/shard_map/ppermute | solution.py:107
  238.0 4.4 %collective-permute-done.57.refs_1_ = bf16[1,104,384]{2,1,0:T(8,128)(2,1)S(1)} collective-permute-done((bf16[1,104,384]{2,1,0:T(8,128)(2,1)S(1)}, bf16[1,104,384]{2,1,0:T(8,128)(2,1)S(1)}, u32[]{:S(2)}, u32[]{:S(2)}) %collective-permute-start.57) | collective-permute-done | bytes 79904 | tf_op jit(solution)/shard_map/ppermute | solution.py:119
  248.2 4.2 %collective-permute-done.63.refs_1_ = bf16[1,96,768]{2,1,0:T(8,128)(2,1)S(1)} collective-permute-done((bf16[1,96,768]{2,1,0:T(8,128)(2,1)S(1)}, bf16[1,96,768]{2,1,0:T(8,128)(2,1)S(1)}, u32[]{:S(2)}, u32[]{:S(2)}) %collective-permute-start.63) | collective-permute-done | bytes 147488 | tf_op jit(solution)/shard_map/ppermute | solution.py:119
  (197 shorter events, 143.7 us)
Async XLA Ops:
  22.6 14.3 %collective-permute-start.8 = (bf16[4,112,384]{2,1,0:T(8,128)(2,1)S(1)}, bf16[4,112,384]{2,1,0:T(8,128)(2,1)S(1)}, u32[]{:S(2)}, u32[]{:S(2)}) collective-permute-start(bf16[4,112,384]{2,1,0:T(8,128)(2,1)S(1)} %get-tuple-element.271.refs_4_), channel_id=1, source_target_pairs={{0,1},{1,0},{2,3},{3,2},{4,5},{5,4},{6,7},{7,6},{8,9},{9,8},{10,11... | collective-permute-start | bytes 1032200 | tf_op jit(solution)/shard_map/ppermute | solution.py:116
  24.5 12.4 %collective-permute-start.6 = (bf16[4,96,384]{2,1,0:T(8,128)(2,1)S(1)}, bf16[4,96,384]{2,1,0:T(8,128)(2,1)S(1)}, u32[]{:S(2)}, u32[]{:S(2)}) collective-permute-start(bf16[4,96,384]{2,1,0:T(8,128)(2,1)S(1)} %get-tuple-element.270.refs_0_), channel_id=1, source_target_pairs={{0,16},{8,24},{16,0},{24,8},{1,17},{9,25},{17,1},{25,9},{2,18},{10... | collective-permute-start | bytes 884744 | tf_op jit(solution)/shard_map/ppermute | solution.py:110
  37.6 16.0 %collective-permute-start.12 = (bf16[3,768,384]{2,1,0:T(8,128)(2,1)S(1)}, bf16[3,768,384]{2,1,0:T(8,128)(2,1)S(1)}, u32[]{:S(2)}, u32[]{:S(2)}) collective-permute-start(bf16[3,768,384]{2,1,0:T(8,128)(2,1)S(1)} %bitcast.54), channel_id=1, source_target_pairs={{0,8},{8,0},{16,24},{24,16},{1,9},{9,1},{17,25},{25,17},{2,10},{10... | collective-permute-start | bytes 5308424 | tf_op jit(solution)/shard_map/ppermute | solution.py:107
  43.4 16.0 %collective-permute-start.17 = (bf16[4,96,768]{2,1,0:T(8,128)(2,1)S(1)}, bf16[4,96,768]{2,1,0:T(8,128)(2,1)S(1)}, u32[]{:S(2)}, u32[]{:S(2)}) collective-permute-start(bf16[4,96,768]{2,1,0:T(8,128)(2,1)S(1)} %get-tuple-element.322.refs_0_), channel_id=1, source_target_pairs={{0,16},{8,24},{16,0},{24,8},{1,17},{9,25},{17,1},{25,9},{2,18},{10... | collective-permute-start | bytes 1769480 | tf_op jit(solution)/shard_map/ppermute | solution.py:110
  43.7 15.8 %collective-permute-start.15 = (bf16[4,96,768]{2,1,0:T(8,128)(2,1)S(1)}, bf16[4,96,768]{2,1,0:T(8,128)(2,1)S(1)}, u32[]{:S(2)}, u32[]{:S(2)}) collective-permute-start(bf16[4,96,768]{2,1,0:T(8,128)(2,1)S(1)} %get-tuple-element.322.refs_0_), channel_id=1, source_target_pairs={{0,1},{1,0},{2,3},{3,2},{4,5},{5,4},{6,7},{7,6},{8,9},{9,8},{10,11... | collective-permute-start | bytes 1769480 | tf_op jit(solution)/shard_map/ppermute | solution.py:116
  59.5 15.9 %collective-permute-start.18 = (bf16[4,96,768]{2,1,0:T(8,128)(2,1)S(1)}, bf16[4,96,768]{2,1,0:T(8,128)(2,1)S(1)}, u32[]{:S(2)}, u32[]{:S(2)}) collective-permute-start(bf16[4,96,768]{2,1,0:T(8,128)(2,1)S(1)} %collective-permute-done.15.refs_6_.refs_1_), channel_id=1, source_target_pairs={{0,16},{8,24},{16,0},{24,8},{1,17},{9,25},{17,1},{25,9},{2,18},{10... | collective-permute-start | bytes 1769480 | tf_op jit(solution)/shard_map/ppermute | solution.py:110
  59.8 15.0 %collective-permute-start.19 = (bf16[4,96,640]{2,1,0:T(8,128)(2,1)S(1)}, bf16[4,96,640]{2,1,0:T(8,128)(2,1)S(1)}, u32[]{:S(2)}, u32[]{:S(2)}) collective-permute-start(bf16[4,96,640]{2,1,0:T(8,128)(2,1)S(1)} %get-tuple-element.331.refs_0_), channel_id=1, source_target_pairs={{0,1},{1,0},{2,3},{3,2},{4,5},{5,4},{6,7},{7,6},{8,9},{9,8},{10,11... | collective-permute-start | bytes 1474568 | tf_op jit(solution)/shard_map/ppermute | solution.py:116
  60.7 14.0 %collective-permute-start.21 = (bf16[96,1536]{1,0:T(8,128)(2,1)S(1)}, bf16[96,1536]{1,0:T(8,128)(2,1)S(1)}, u32[]{:S(2)}, u32[]{:S(2)}) collective-permute-start(bf16[96,1536]{1,0:T(8,128)(2,1)S(1)} %copy-done.5), channel_id=1, source_target_pairs={{0,2},{1,3},{2,0},{3,1},{4,6},{5,7},{6,4},{7,5},{8,10},{9,11},{10,... | collective-permute-start | bytes 884744 | tf_op jit(solution)/shard_map/ppermute | solution.py:119
  60.9 13.9 %collective-permute-start.20 = (bf16[96,1536]{1,0:T(8,128)(2,1)S(1)}, bf16[96,1536]{1,0:T(8,128)(2,1)S(1)}, u32[]{:S(2)}, u32[]{:S(2)}) collective-permute-start(bf16[96,1536]{1,0:T(8,128)(2,1)S(1)} %copy-done.5), channel_id=1, source_target_pairs={{0,4},{1,5},{2,6},{3,7},{4,0},{5,1},{6,2},{7,3},{8,12},{9,13},{10,... | collective-permute-start | bytes 884744 | tf_op jit(solution)/shard_map/ppermute | solution.py:119
  88.6 14.6 %collective-permute-start.27 = (bf16[4,96,1536]{2,1,0:T(8,128)(2,1)S(1)}, bf16[4,96,1536]{2,1,0:T(8,128)(2,1)S(1)}, u32[]{:S(2)}, u32[]{:S(2)}) collective-permute-start(bf16[4,96,1536]{2,1,0:T(8,128)(2,1)S(1)} %get-tuple-element.355.refs_0_), channel_id=1, source_target_pairs={{0,8},{8,0},{16,24},{24,16},{1,9},{9,1},{17,25},{25,17},{2,10},{10... | collective-permute-start | bytes 3538952 | tf_op jit(solution)/shard_map/ppermute | solution.py:107
  89.9 21.2 %collective-permute-start.30 = (bf16[3,96,1536]{2,1,0:T(8,128)(2,1)S(1)}, bf16[3,96,1536]{2,1,0:T(8,128)(2,1)S(1)}, u32[]{:S(2)}, u32[]{:S(2)}) collective-permute-start(bf16[3,96,1536]{2,1,0:T(8,128)(2,1)S(1)} %get-tuple-element.359), channel_id=1, source_target_pairs={{0,1},{1,0},{2,3},{3,2},{4,5},{5,4},{6,7},{7,6},{8,9},{9,8},{10,11... | collective-permute-start | bytes 2654216 | tf_op jit(solution)/shard_map/ppermute | solution.py:116
  123.0 14.6 %collective-permute-start.35 = (bf16[4,96,768]{2,1,0:T(8,128)(2,1)S(1)}, bf16[4,96,768]{2,1,0:T(8,128)(2,1)S(1)}, u32[]{:S(2)}, u32[]{:S(2)}) collective-permute-start(bf16[4,96,768]{2,1,0:T(8,128)(2,1)S(1)} %get-tuple-element.388), channel_id=1, source_target_pairs={{0,1},{1,0},{2,3},{3,2},{4,5},{5,4},{6,7},{7,6},{8,9},{9,8},{10,11... | collective-permute-start | bytes 1769480 | tf_op jit(solution)/shard_map/ppermute | solution.py:116
  138.4 13.7 %collective-permute-start.37 = (bf16[4,96,768]{2,1,0:T(8,128)(2,1)S(1)}, bf16[4,96,768]{2,1,0:T(8,128)(2,1)S(1)}, u32[]{:S(2)}, u32[]{:S(2)}) collective-permute-start(bf16[4,96,768]{2,1,0:T(8,128)(2,1)S(1)} %get-tuple-element.397), channel_id=1, source_target_pairs={{0,1},{1,0},{2,3},{3,2},{4,5},{5,4},{6,7},{7,6},{8,9},{9,8},{10,11... | collective-permute-start | bytes 1769480 | tf_op jit(solution)/shard_map/ppermute | solution.py:116
  169.8 21.8 %collective-permute-start.45 = (bf16[3,768,384]{2,1,0:T(8,128)(2,1)S(1)}, bf16[3,768,384]{2,1,0:T(8,128)(2,1)S(1)}, u32[]{:S(2)}, u32[]{:S(2)}) collective-permute-start(bf16[3,768,384]{2,1,0:T(8,128)(2,1)S(1)} %get-tuple-element.431), channel_id=1, source_target_pairs={{0,8},{8,0},{16,24},{24,16},{1,9},{9,1},{17,25},{25,17},{2,10},{10... | collective-permute-start | bytes 5308424 | tf_op jit(solution)/shard_map/ppermute | solution.py:107
  170.7 14.9 %collective-permute-start.43 = (bf16[4,96,768]{2,1,0:T(8,128)(2,1)S(1)}, bf16[4,96,768]{2,1,0:T(8,128)(2,1)S(1)}, u32[]{:S(2)}, u32[]{:S(2)}) collective-permute-start(bf16[4,96,768]{2,1,0:T(8,128)(2,1)S(1)} %get-tuple-element.423), channel_id=1, source_target_pairs={{0,16},{8,24},{16,0},{24,8},{1,17},{9,25},{17,1},{25,9},{2,18},{10... | collective-permute-start | bytes 1769480 | tf_op jit(solution)/shard_map/ppermute | solution.py:110
  172.0 15.5 %collective-permute-start.42 = (bf16[4,96,640]{2,1,0:T(8,128)(2,1)S(1)}, bf16[4,96,640]{2,1,0:T(8,128)(2,1)S(1)}, u32[]{:S(2)}, u32[]{:S(2)}) collective-permute-start(bf16[4,96,640]{2,1,0:T(8,128)(2,1)S(1)} %get-tuple-element.421), channel_id=1, source_target_pairs={{0,1},{1,0},{2,3},{3,2},{4,5},{5,4},{6,7},{7,6},{8,9},{9,8},{10,11... | collective-permute-start | bytes 1474568 | tf_op jit(solution)/shard_map/ppermute | solution.py:116
  173.3 18.3 %collective-permute-start.46 = (bf16[1,96,768]{2,1,0:T(8,128)(2,1)S(1)}, bf16[1,96,768]{2,1,0:T(8,128)(2,1)S(1)}, u32[]{:S(2)}, u32[]{:S(2)}) collective-permute-start(bf16[1,96,768]{2,1,0:T(8,128)(2,1)S(1)} %get-tuple-element.433), channel_id=1, source_target_pairs={{0,4},{1,5},{2,6},{3,7},{4,0},{5,1},{6,2},{7,3},{8,12},{9,13},{10,... | collective-permute-start | bytes 442376 | tf_op jit(solution)/shard_map/ppermute | solution.py:119
  186.3 19.3 %collective-permute-start.51 = (bf16[4,96,768]{2,1,0:T(8,128)(2,1)S(1)}, bf16[4,96,768]{2,1,0:T(8,128)(2,1)S(1)}, u32[]{:S(2)}, u32[]{:S(2)}) collective-permute-start(bf16[4,96,768]{2,1,0:T(8,128)(2,1)S(1)} %get-tuple-element.451), channel_id=1, source_target_pairs={{0,1},{1,0},{2,3},{3,2},{4,5},{5,4},{6,7},{7,6},{8,9},{9,8},{10,11... | collective-permute-start | bytes 1769480 | tf_op jit(solution)/shard_map/ppermute | solution.py:116
  192.6 16.7 %collective-permute-start.47 = (bf16[4,2,96,384]{3,2,1,0:T(8,128)(2,1)S(1)}, bf16[4,2,96,384]{3,2,1,0:T(8,128)(2,1)S(1)}, u32[]{:S(2)}, u32[]{:S(2)}) collective-permute-start(bf16[4,2,96,384]{3,2,1,0:T(8,128)(2,1)S(1)} %get-tuple-element.435), channel_id=1, source_target_pairs={{0,16},{8,24},{16,0},{24,8},{1,17},{9,25},{17,1},{25,9},{2,18},{10... | collective-permute-start | bytes 1769480 | tf_op jit(solution)/shard_map/ppermute | solution.py:110
  194.6 12.1 %collective-permute-start.48 = (bf16[4,96,384]{2,1,0:T(8,128)(2,1)S(1)}, bf16[4,96,384]{2,1,0:T(8,128)(2,1)S(1)}, u32[]{:S(2)}, u32[]{:S(2)}) collective-permute-start(bf16[4,96,384]{2,1,0:T(8,128)(2,1)S(1)} %get-tuple-element.446), channel_id=1, source_target_pairs={{0,1},{1,0},{2,3},{3,2},{4,5},{5,4},{6,7},{7,6},{8,9},{9,8},{10,11... | collective-permute-start | bytes 884744 | tf_op jit(solution)/shard_map/ppermute | solution.py:116
  211.1 15.2 %collective-permute-start.58 = (bf16[4,96,768]{2,1,0:T(8,128)(2,1)S(1)}, bf16[4,96,768]{2,1,0:T(8,128)(2,1)S(1)}, u32[]{:S(2)}, u32[]{:S(2)}) collective-permute-start(bf16[4,96,768]{2,1,0:T(8,128)(2,1)S(1)} %get-tuple-element.478), channel_id=1, source_target_pairs={{0,16},{8,24},{16,0},{24,8},{1,17},{9,25},{17,1},{25,9},{2,18},{10... | collective-permute-start | bytes 1769480 | tf_op jit(solution)/shard_map/ppermute | solution.py:110
  220.0 13.5 %collective-permute-start.64 = (bf16[96,2176]{1,0:T(8,128)(2,1)S(1)}, bf16[96,2176]{1,0:T(8,128)(2,1)S(1)}, u32[]{:S(2)}, u32[]{:S(2)}) collective-permute-start(bf16[96,2176]{1,0:T(8,128)(2,1)S(1)} %get-tuple-element.487.refs_0_), channel_id=1, source_target_pairs={{0,16},{8,24},{16,0},{24,8},{1,17},{9,25},{17,1},{25,9},{2,18},{10... | collective-permute-start | bytes 1253384 | tf_op jit(solution)/shard_map/ppermute | solution.py:110
  227.0 16.0 %collective-permute-start.62 = (bf16[2,96,768]{2,1,0:T(8,128)(2,1)S(1)}, bf16[2,96,768]{2,1,0:T(8,128)(2,1)S(1)}, u32[]{:S(2)}, u32[]{:S(2)}) collective-permute-start(bf16[2,96,768]{2,1,0:T(8,128)(2,1)S(1)} %get-tuple-element.483), channel_id=1, source_target_pairs={{0,2},{1,3},{2,0},{3,1},{4,6},{5,7},{6,4},{7,5},{8,10},{9,11},{10,... | collective-permute-start | bytes 884744 | tf_op jit(solution)/shard_map/ppermute | solution.py:119
  228.9 16.4 %collective-permute-start.65 = (bf16[96,2176]{1,0:T(8,128)(2,1)S(1)}, bf16[96,2176]{1,0:T(8,128)(2,1)S(1)}, u32[]{:S(2)}, u32[]{:S(2)}) collective-permute-start(bf16[96,2176]{1,0:T(8,128)(2,1)S(1)} %get-tuple-element.487.refs_0_), channel_id=1, source_target_pairs={{0,8},{8,0},{16,24},{24,16},{1,9},{9,1},{17,25},{25,17},{2,10},{10... | collective-permute-start | bytes 1253384 | tf_op jit(solution)/shard_map/ppermute | solution.py:107
  (58 other events, 467.4 us)
where the time goes:
time: 264 us; the launch traced here: 263 us
  Pallas kernels  102 us (39%)
  starting transfers between devices  82.8 us (31%)
  waiting for transfers between devices  75.3 us (29%)
    pallas_call x56, Pallas kernels, run(): pl.pallas_call(marked, out_shape=list(outs) + [sds((8, 128), F32)], compi...  102 us
    ppermute x24, starting transfers between devices, along(): return lax.ppermute(a, 'fsdp', [(s, s ^ 2 * k) for s in range(self.shards)])  30.9 us
    ppermute x24, waiting for transfers between devices, along(): return lax.ppermute(a, 'fsdp', [(s, s ^ 2 * k) for s in range(self.shards)])  28.5 us
    ppermute x16, starting transfers between devices, core(): return lax.ppermute(a, 'rep', [(r, r ^ 1) for r in range(self.reps)])  25.6 us
    ppermute x18, waiting for transfers between devices, y(): return lax.ppermute(a, 'rep', [(r, r ^ 2) for r in range(self.reps)])  23.5 us
    ppermute x12, waiting for transfers between devices, across(): return lax.ppermute(a, 'fsdp', [(s, s ^ 1) for s in range(self.shards)])  16.2 us
    ppermute x18, starting transfers between devices, y(): return lax.ppermute(a, 'rep', [(r, r ^ 2) for r in range(self.reps)])  13.7 us
    ppermute x12, starting transfers between devices, across(): return lax.ppermute(a, 'fsdp', [(s, s ^ 1) for s in range(self.shards)])  12.6 us
  transfers between devices with their start and end apart: 70, of which 27 were waited for; matrix products, arithmetic and copies ran while one was open for 0% of the time, Pallas kernels for 31%

commit v1 on v0

--- a/solution.py
+++ b/solution.py
@@ -23,6 +23,7 @@
 VM = pl.BlockSpec()
 SM = pl.BlockSpec(memory_space=pltpu.SMEM)
 ANY = pl.BlockSpec(memory_space=pl.ANY)
+PIN = pl.BlockSpec(memory_space=pltpu.VMEM)
 
 
 def sds(shape, dtype=BF):
@@ -47,7 +48,7 @@
     def wait(self, *arrays):
         self.tokens = self.tokens + list(arrays)
 
-    def run(self, body, outs, where, *ins, name=None, scratch=(), grid=None, in_specs=None, out_specs=None, vmem=None, prefetch=False, far=False):
+    def run(self, body, outs, where, *ins, name=None, scratch=(), grid=None, in_specs=None, out_specs=None, vmem=None, prefetch=False, far=False, cost=0):
         moved = sum(size_of(a) for a in ins) + sum(size_of(o) for o in outs)
         held = moved + sum(size_of(s) for s in scratch)
         limit = 66_000_000 if far else vmem << 20 if vmem else min(60 << 20, int(1.25 * held) + (10 << 20))
@@ -83,7 +84,7 @@
             marked,
             out_shape=list(outs) + [sds((8, 128), F32)],
             compiler_params=pltpu.CompilerParams(vmem_limit_bytes=limit),
-            cost_estimate=pl.CostEstimate(flops=0, bytes_accessed=1024, transcendentals=0),
+            cost_estimate=pl.CostEstimate(flops=cost * 1_150_000_000, bytes_accessed=1024, transcendentals=0),
             name=name,
             **spec,
         )(where, *ins, *self.tokens)
@@ -172,7 +173,7 @@
     peak = jnp.max(scores, -1, keepdims=True)
     expo = jnp.exp(scores - peak)
     total = jnp.sum(expo, -1, keepdims=True)
-    return expo / total, peak + jnp.log(total)
+    return expo * (1.0 / total), peak + jnp.log(total)
 
 
 def pack_a(at, query, keyval, gains, biases, part):
@@ -228,20 +229,20 @@
         qn[at[Z] ^ k] = piece[:, HALF:]
 
 
-def column_rest(at, *refs):
-    whole, rest = refs[-2:]
+def column_halves(at, *refs):
+    up, down = refs[-2:]
     for k, piece in enumerate(refs[:-2]):
-        whole[at[Z] ^ k] = piece[...]
-        if k:
-            rest[k - 1] = piece[...]
-
-
-def join_rest(at, mine, other_own, other_rest, out):
-    depth = mine.shape[0]
-    for z in range(depth):
-        out[z, at[X]] = mine[z]
-    for k in range(depth):
-        out[at[Z] ^ k, 1 - at[X]] = other_own[...] if k == 0 else other_rest[k - 1]
+        up[at[Z] ^ k] = piece[:, :D]
+        down[at[Z] ^ k] = piece[:, D:]
+
+
+def join_pieces(at, up, down, *refs):
+    out = refs[-1]
+    for z in range(up.shape[0]):
+        out[z, at[X], :, :D] = up[z]
+        out[z, at[X], :, D:] = down[z]
+    for k, piece in enumerate(refs[:-1]):
+        out[at[Z] ^ k, 1 - at[X]] = piece[...]
 
 
 def join(at, mine, other, out):
@@ -312,16 +313,22 @@
     return jnp.where(parent, shared_sheet_reward, 0.0) + jnp.where(present, 0.0, filtered_logits)
 
 
-def cross_fwd(owner, valid, q, k, v, out, logs, bias):
-    @pl.when(pl.program_id(0) == 0)
-    def _():
-        bias[...] = cross_bias(owner, valid)
-
-    b = bias[...]
-    scores = nt(two_heads(q[...]), k[...]) * SCALE + jnp.concatenate([b, b], 0)
-    weight, log = softmax(scores)
-    logs[0] = log
-    out[...] = one_pair(mm(weight.astype(BF), v[...])).astype(BF)
+def lanes_at(i):
+    return pl.ds(pl.multiple_of(i * 128, 128), 128)
+
+
+def cross_fwd(at, owner, valid, q, kv, out, logs, bias):
+    bias[...] = cross_bias(owner, valid)
+    pairs = q.shape[1] // 128
+
+    @pl.loop(0, pairs)
+    def _(p):
+        b = bias[...]
+        k, v = kv[:, lanes_at(p)], kv[:, lanes_at(pairs + p)]
+        scores = nt(two_heads(q[:, lanes_at(p)] * SCALE), k) + jnp.concatenate([b, b], 0)
+        weight, log = softmax(scores)
+        logs[p] = log
+        out[:, lanes_at(p)] = one_pair(mm(weight.astype(BF), v)).astype(BF)
 
 
 def gate_kernel(at, mixed, normed, visual, gains, biases, w_out, w_gate, cross, gate, joined, second):
@@ -374,9 +381,9 @@
 def ffn_kernel(last, at, third0, third1, cot0, cot1, w, *refs):
     n = third0.shape[0]
     if last:
-        y0i, y1i, d0i, d1i, y0, y1, d0, d1, grad = refs
+        y0i, y1i, d0i, d1i, y0, y1, d0, d1, g_up, g_down = refs
     else:
-        y0, y1, d0, d1, grad = refs
+        y0, y1, d0, d1, g_up, g_down = refs
     rows = jnp.concatenate([third0[...], third1[...]], 0)
     cot = jnp.concatenate([cot0[:n], cot1[:n]], 0)
     up, down = w[:, :D], w[:, D:]
@@ -386,10 +393,10 @@
     act = (0.5 * v * (1.0 + th)).astype(BF)
     slope = 0.5 * (1.0 + th) + 0.5 * v * (1.0 - th * th) * (k * (1.0 + 3.0 * 0.044715 * (v * v)))
     y = mm(act, down)
-    grad[:, D:] = tn(act, cot).astype(BF)
+    g_down[...] = tn(act, cot).astype(BF)
     dl = (nt(cot, down) * slope).astype(BF)
     d = nt(dl, up)
-    grad[:, :D] = tn(rows, dl).astype(BF)
+    g_up[...] = tn(rows, dl).astype(BF)
     if last:
         y0[...] = y[:n] + y0i[...]
         y1[...] = (y[n:] + y1i[...]).astype(BF)
@@ -472,32 +479,37 @@
                     out[t ^ tt, :, :, HALF:] = side[:, :, lanes]
 
 
-def cross_back(owner, valid, q, k, v, dm, logs, dq, dkv, bias):
-    @pl.when(pl.program_id(0) == 0)
-    def _():
-        bias[...] = cross_bias(owner, valid)
-
-    b = bias[...]
-    qq, dd = two_heads(q[...]), two_heads(dm[...])
-    scores = nt(qq, k[...]) * SCALE + jnp.concatenate([b, b], 0)
-    weight = jnp.exp(scores - logs[0])
-    dp = nt(dd, v[...])
-    ds = (weight * (dp - jnp.sum(weight * dp, -1, keepdims=True))).astype(BF)
-    dq[...] = (one_pair(mm(ds, k[...])) * SCALE).astype(BF)
-    dkv[0] = (tn(ds, qq) * SCALE).astype(BF)
-    dkv[1] = tn(weight.astype(BF), dd).astype(BF)
-
-
-def cross_weights(at, text_normed, normed, dq, dkv, grad):
-    t = at[T]
+def cross_back(index, at, owner, valid, q, kv, dm, logs, dq, dkv, bias):
+    bias[...] = cross_bias(owner, valid)
+    pairs = q.shape[1] // 128
+    first = (at[C] ^ index) * (pairs // 2)
+
+    @pl.loop(0, pairs // 2)
+    def _(i):
+        p = first + i
+        b = bias[...]
+        k, v = kv[:, lanes_at(p)], kv[:, lanes_at(pairs + p)]
+        qq, dd = two_heads(q[:, lanes_at(p)]), two_heads(dm[:, lanes_at(p)])
+        scores = nt(qq * SCALE, k) + jnp.concatenate([b, b], 0)
+        weight = jnp.exp(scores - logs[p])
+        dp = nt(dd, v)
+        ds = (weight * (dp - jnp.sum(weight * dp, -1, keepdims=True))).astype(BF)
+        dq[:, lanes_at(i)] = (one_pair(mm(ds, k)) * SCALE).astype(BF)
+        dkv[0, :, lanes_at(i)] = (tn(ds, qq) * SCALE).astype(BF)
+        dkv[1, :, lanes_at(i)] = tn(weight.astype(BF), dd).astype(BF)
+
+
+def cross_weights(at, text_normed, normed, dq, dkv, own, oth, q):
+    t0 = at[T] == 0
 
     @pl.loop(0, 3)
     def _(j):
         lanes = pl.ds(pl.multiple_of(j * 256, 256), 256)
         x = text_normed[:, lanes]
-        grad[t, lanes] = tn(x, dkv[0]).astype(BF)
-        grad[1 - t, lanes] = tn(x, dkv[1]).astype(BF)
-        grad[2, lanes] = tn(normed[:, lanes], dq[...]).astype(BF)
+        k, v = tn(x, dkv[0]).astype(BF), tn(x, dkv[1]).astype(BF)
+        own[lanes] = jnp.where(t0, k, v)
+        oth[lanes] = jnp.where(t0, v, k)
+        q[lanes] = tn(normed[:, lanes], dq[...]).astype(BF)
 
 
 def text_back(at, text, gains, w_kv, own, oth, grad, sums):
@@ -653,9 +665,9 @@
         oth_keep[z] = (keep[1, z, x].astype(F32) + came[1, z, x].astype(F32)).astype(BF)
 
 
-def add_core_a(at, keep, came, own, oth, q):
-    for out, i in ((own, 0), (oth, 1), (q, 2)):
-        out[...] = (keep[i].astype(F32) + came[i].astype(F32)).astype(BF)
+def add_core_a(at, *refs):
+    for keep, came, out in zip(refs[:3], refs[3:6], refs[6:]):
+        out[...] = (keep[...].astype(F32) + came[...].astype(F32)).astype(BF)
 
 
 def add_out(at, carried, y0, came, out):
@@ -733,13 +745,15 @@
     od.wait(b_o, b_ym)
     c_o, b_yo = od.start(ln.across, c_m), od.start(ln.y, b_o)
     pairs = H // 2
-    col = lambda n, off=0: pl.BlockSpec((n, 128), lambda p: (0, p + off))
     mixed, logs = run(
-        lambda at, *refs: cross_fwd(*refs), [sds((vis, D)), sds((pairs, 2 * vis, 1), F32)],
-        at, block_owner, visual_valid, queries, kv, kv,
-        grid=(pairs,), in_specs=[whole((1, txt)), whole((1, vis)), col(vis), col(txt), col(txt, pairs)],
-        out_specs=[col(vis), pl.BlockSpec((1, 2 * vis, 1), lambda p: (p, 0, 0))],
-        scratch=[sds((vis, txt), F32)], name="cross_fwd", vmem=16)
+        cross_fwd, [sds((vis, D)), sds((pairs, 2 * vis, 1), F32)],
+        at, block_owner, visual_valid, queries, kv,
+        in_specs=[VM, VM, VM, PIN], scratch=[sds((vis, txt), F32)], name="cross_fwd", vmem=16)
+    od.wait(*[pieces_d[k] for k in sorted(pieces_d) if k])
+    d_x = {0: d_xo}
+    for k in sorted(pieces_d):
+        if k:
+            d_x[k] = od.start(ln.across, pieces_d[k])
     pieces_d = passed_on(pieces_d)
     (wc_own,) = run(join, [sds(grid4(w3))], at, c_m, c_o, name="join_c")
     wc_oth = ln.core(wc_own)
@@ -755,31 +769,38 @@
         gate_kernel, [sds((vis, D)), page, page, sds((vis, D))],
         at, mixed, normed, visual, gains, biases, w_out, w_gate, name="gate")
     second_y = ln.y(second)
-    d_m, d_rest = run(column_rest, [sds((depth, rows, 2 * D)), sds((depth - 1, rows, 2 * D))], at, *pieces_d, name="column_d")
-    d_xr, d_cm, d_cxo = ln.across(d_rest), ln.core(d_m), od.start(ln.core, d_xo)
+    d_u, d_d = run(column_halves, [sds((depth, rows, D))] * 2, at, *pieces_d, name="column_d")
+    d_cu, d_cd = ln.core(d_u), ln.core(d_d)
+    od.wait(*[d_x[k] for k in d_x])
     triple, att_mine, att_send = run(
         self_fwd, [sds((2 * vis, 3 * HALF)), sds((vis, HALF)), sds((vis, HALF))],
-        at, second, second_y, cot, cot_y, wc_own, wc_oth, name="self_fwd")
+        at, second, second_y, cot, cot_y, wc_own, wc_oth, name="self_fwd", cost=3)
     att_came = ln.y(att_send)
-    od.wait(d_cm, d_cxo)
+    d_cx = {k: od.start(ln.core, d_x[k]) for k in d_x}
+    for k in range(depth):
+        if k not in d_x:
+            d_x[k] = od.start(ln.across, pieces_d[k])
+    od.wait(d_cu, d_cd)
     attended, carried, third = run(
         carry_kernel, [sds((vis, D)), page, sds((vis, D))],
-        at, att_mine, att_came, joined, gains, biases, w_self, name="carry")
+        at, att_mine, att_came, joined, gains, biases, w_self, name="carry", cost=3)
     third_y = ln.y(third)
+    (wd_own,) = run(join_pieces, [sds(grid4(2 * D))], at, d_u, d_d, *[d_x[k] for k in range(depth)], name="join_d")
     od.wait(third_y)
-    d_cxr = od.start(ln.core, d_xr)
-    (wd_own,) = run(join_rest, [sds(grid4(2 * D))], at, d_m, d_xo, d_xr, name="join_d")
-    (wd_oth,) = run(join_rest, [sds(grid4(2 * D))], at, d_cm, d_cxo, d_cxr, name="join_d")
+    for k in range(depth):
+        if k not in d_cx:
+            d_cx[k] = od.start(ln.core, d_x[k])
+    (wd_oth,) = run(join_pieces, [sds(grid4(2 * D))], at, d_cu, d_cd, *[d_cx[k] for k in range(depth)], name="join_d")
     wd_own, wd_oth = wd_own.reshape(D, 2 * D), wd_oth.reshape(D, 2 * D)
 
-    y0, y1, d0, d1, gd_oth = run(
-        functools.partial(ffn_kernel, False), [page] * 4 + [sds((D, 2 * D))],
+    y0, y1, d0, d1, gu_oth, gd_oth = run(
+        functools.partial(ffn_kernel, False), [page] * 4 + [sds((D, D))] * 2,
         at, third, third_y, cot, cot_y, wd_oth, name="ffn_first")
-    gd_came = ln.core(gd_oth).reshape(grid4(2 * D))
-    y0, y1, d0, d1, gd_own = run(
-        functools.partial(ffn_kernel, True), [page, sds((vis, D))] * 2 + [sds((D, 2 * D))],
+    gd_came, gu_came = [ln.core(g).reshape(grid4(D)) for g in (gd_oth, gu_oth)]
+    y0, y1, d0, d1, gu_own, gd_own = run(
+        functools.partial(ffn_kernel, True), [page, sds((vis, D))] * 2 + [sds((D, D))] * 2,
         at, third, third_y, cot, cot_y, wd_own, y0, y1, d0, d1, name="ffn_second")
-    gd_own = gd_own.reshape(grid4(2 * D))
+    gd_own, gu_own = gd_own.reshape(grid4(D)), gu_own.reshape(grid4(D))
     d1_came = ln.y(d1)
 
     class Sum:
@@ -814,6 +835,9 @@
             return True
 
     def finish(*sums):
+        for one in sums:
+            while one.keep.shape[0] > 1:
+                one.step()
         ins = [a for one in sums for a in (one.keep, one.got)]
         (total,) = run(functools.partial(reduce_last, len(sums)), [sds((sums[0].rows, sum(one.n for one in sums)))], at,
                        *ins, name="reduce_last")
@@ -823,26 +847,20 @@
         return total, ry, ln.core(total), ln.core(ry)
 
     def back_half(index):
-        def spec(n, off=0):
-            return pl.BlockSpec((n, 128), lambda p, at: (0, (at[C] ^ index) * 3 + p + off))
-
         return run(
-            lambda at, *refs: cross_back(*refs), [sds((vis, HALF)), sds((2, txt, HALF))],
-            at, block_owner, visual_valid, queries, kv, kv, d_mixed, logs, prefetch=True, grid=(3,),
-            in_specs=[whole((1, txt)), whole((1, vis)), spec(vis), spec(txt), spec(txt, pairs), spec(vis),
-                      pl.BlockSpec((1, 2 * vis, 1), lambda p, at: ((at[C] ^ index) * 3 + p, 0, 0))],
-            out_specs=[pl.BlockSpec((vis, 128), lambda p, at: (0, p)), pl.BlockSpec((2, txt, 128), lambda p, at: (0, 0, p))],
-            scratch=[sds((vis, txt), F32)], name="cross_back", vmem=20)
+            functools.partial(cross_back, index), [sds((vis, HALF)), sds((2, txt, HALF))],
+            at, block_owner, visual_valid, queries, kv, d_mixed, logs,
+            in_specs=[VM, VM, VM, PIN, VM, VM], scratch=[sds((vis, txt), F32)], name="cross_back", vmem=20)
 
     def weights_half(dq, dkv):
-        return run(cross_weights, [sds((3, D, HALF))], at, text_normed, normed, dq, dkv, name="cross_weights")[0]
-
-    down = Sum("down", [gd_own, gd_came], D, slice(D, 2 * D)).go()
+        return run(cross_weights, [sds((D, HALF))] * 3, at, text_normed, normed, dq, dkv, name="cross_weights")
+
+    down = Sum("down", [gd_own, gd_came], D).go()
     d_carried, da_mine, da_send, g_self, sums3 = run(
         carry_back, [page, sds((vis, HALF)), sds((vis, HALF)), sds((D, D)), sds((2, D), F32)],
         at, d0, d1_came, carried, cotangent, attended, gains, w_self, name="carry_back")
     da_came = ln.y(da_send)
-    up = Sum("up", [gd_own, gd_came], D, slice(0, D))
+    up = Sum("up", [gu_own, gu_came], D)
     od.wait(da_came)
     down.step()
     up.go()
@@ -861,21 +879,20 @@
     y1_came = od.start(ln.y, y1)
     dq_oth, dkv_oth = back_half(1)
     qkv = Sum("qkv", [gc_own, gc_came], w3).go()
-    od.wait(y1_came)
+    od.wait(y1_came, down.got)
     own_b, b_ys, b_yk = run(
         add_core_b, [sds(grid4(D)), sds((depth, rows, D)), sds((depth, rows, D))], at,
         b_keep.reshape((2,) + grid4(D)), b_came.reshape((2,) + grid4(D)), name="add_core_b")
     b_ys = ln.y(b_ys)
-    a_came = ln.core(weights_half(dq_oth, dkv_oth))
+    a_came = [ln.core(a) for a in weights_half(dq_oth, dkv_oth)]
     dq_own, dkv_own = back_half(0)
     up.step()
     gates = Sum("gate", [own_b], D, sends=[b_ys], keeps=[b_yk]).go()
     qkv.step()
     a_keep = weights_half(dq_own, dkv_own)
-    od.wait(down.got)
     own_a, a_y, own_q = run(
         add_core_a, [sds(grid4(HALF))] * 3, at,
-        a_keep.reshape((3,) + grid4(HALF)), a_came.reshape((3,) + grid4(HALF)), name="add_core_a")
+        *[a.reshape(grid4(HALF)) for a in (*a_keep, *a_came)], name="add_core_a")
     a_y = ln.y(a_y)
     query = Sum("query", [own_q], HALF).go()
     row3 = pl.BlockSpec((2, tile, HALF), lambda i: (0, i, 0))

time: 264 us -> 260 us (0.985)
  waiting for transfers between devices: 75.3 us -> 63.8 us
  starting transfers between devices: 82.8 us -> 93.3 us
  Pallas kernels: 102 us -> 99.3 us
    ppermute x18, waiting for transfers between devices: 23.5 us -> 12.1 us  [y(): return lax.ppermute(a, 'rep', [(r, r ^ 2) for r in range(self.reps)])]
    ppermute x16 -> x22, starting transfers between devices: 25.6 us -> 33.1 us  [core(): return lax.ppermute(a, 'rep', [(r, r ^ 1) for r in range(self.reps)])]
    ppermute x16 -> x22, waiting for transfers between devices: 7.03 us -> 4.15 us  [core(): return lax.ppermute(a, 'rep', [(r, r ^ 1) for r in range(self.reps)])]
    ppermute x12 -> x14, waiting for transfers between devices: 16.2 us -> 17.9 us  [across(): return lax.ppermute(a, 'fsdp', [(s, s ^ 1) for s in range(self.shards)])]
    ppermute x12 -> x14, starting transfers between devices: 12.6 us -> 13.5 us  [across(): return lax.ppermute(a, 'fsdp', [(s, s ^ 1) for s in range(self.shards)])]
  transfers between devices with their start and end apart: 70 -> 78, of which waited for: 27 -> 25; matrix products, arithmetic and copies ran while one was open for 0% -> 0% of each run, Pallas kernels for 31% -> 32%
where the time goes in v1:
time: 260 us
  Pallas kernels  99.3 us (38%)
  starting transfers between devices  93.3 us (36%)
  waiting for transfers between devices  63.8 us (25%)
    pallas_call x56, Pallas kernels, run(): pl.pallas_call(marked, out_shape=list(outs) + [sds((8, 128), F32)], compi...  99.3 us
    ppermute x22, starting transfers between devices, core(): return lax.ppermute(a, 'rep', [(r, r ^ 1) for r in range(self.reps)])  33.1 us
    ppermute x24, starting transfers between devices, along(): return lax.ppermute(a, 'fsdp', [(s, s ^ 2 * k) for s in range(self.shards)])  32.8 us
    ppermute x24, waiting for transfers between devices, along(): return lax.ppermute(a, 'fsdp', [(s, s ^ 2 * k) for s in range(self.shards)])  29.6 us
    ppermute x14, waiting for transfers between devices, across(): return lax.ppermute(a, 'fsdp', [(s, s ^ 1) for s in range(self.shards)])  17.9 us
    ppermute x18, starting transfers between devices, y(): return lax.ppermute(a, 'rep', [(r, r ^ 2) for r in range(self.reps)])  13.9 us
    ppermute x14, starting transfers between devices, across(): return lax.ppermute(a, 'fsdp', [(s, s ^ 1) for s in range(self.shards)])  13.5 us
    ppermute x18, waiting for transfers between devices, y(): return lax.ppermute(a, 'rep', [(r, r ^ 2) for r in range(self.reps)])  12.1 us
  transfers between devices with their start and end apart: 78, of which 25 were waited for; matrix products, arithmetic and copies ran while one was open for 0% of the time, Pallas kernels for 32%

profile of v1, /device:TPU:1, one launch (start us, length us, event | category | flops | bytes accessed | tf_op | source)
XLA Modules:
  0.0 260.0 jit_solution(11397761568873593549)
XLA Ops:
  8.4 4.1 %pack_rest.1 = (bf16[96,768]{1,0:T(8,128)(2,1)}, bf16[96,640]{1,0:T(8,128)(2,1)}, bf16[96,1536]{1,0:T(8,128)(2,1)}, bf16[136,768]{1,0:T(8,128)(2,1)}, f32[8,128]{1,0:T(8,128)}) custom-call(s32[4]{0:T(128)} %pad_add_fusion.at, bf16[96,768]{1,0:T(8,128)(2,1)} %refs_0_.6, bf16[192,768]{1,0:T(8,128)(2,1)} %refs_1_.6, bf16[96,2304]{1,0:T(8,128)(2,1)} %refs_2_.3, ...), custom_call_target="tpu_custom_call" | custom-call | bytes 1024 | tf_op jit(solution)/shard_map/pack_rest/pallas_call | solution.py:83
  30.4 5.0 %collective-permute-done.11.refs_3_ = bf16[96,768]{1,0:T(8,128)(2,1)S(1)} collective-permute-done((bf16[96,768]{1,0:T(8,128)(2,1)S(1)}, bf16[96,768]{1,0:T(8,128)(2,1)S(1)}, u32[]{:S(2)}, u32[]{:S(2)}) %collective-permute-start.11) | collective-permute-done | bytes 147488 | tf_op jit(solution)/shard_map/ppermute | solution.py:120
  37.6 5.8 %collective-permute-start.12 = (bf16[3,768,384]{2,1,0:T(8,128)(2,1)S(1)}, bf16[3,768,384]{2,1,0:T(8,128)(2,1)S(1)}, u32[]{:S(2)}, u32[]{:S(2)}) collective-permute-start(bf16[3,768,384]{2,1,0:T(8,128)(2,1)S(1)} %bitcast.56), channel_id=1, source_target_pairs={{0,8},{8,0},{16,24},{24,16},{1,9},{9,1},{17,25},{25,17},{2,10},{10... | collective-permute-start | bytes 5308424 | tf_op jit(solution)/shard_map/ppermute | solution.py:108
  50.2 3.4 %collective-permute-start.16 = (bf16[96,640]{1,0:T(8,128)(2,1)S(1)}, bf16[96,640]{1,0:T(8,128)(2,1)S(1)}, u32[]{:S(2)}, u32[]{:S(2)}) collective-permute-start(bf16[96,640]{1,0:T(8,128)(2,1)S(1)} %collective-permute-done.13.refs_6_.refs_2_), channel_id=1, source_target_pairs={{0,2},{1,3},{2,0},{3,1},{4,6},{5,7},{6,4},{7,5},{8,10},{9,11},{10,... | collective-permute-start | bytes 368648 | tf_op jit(solution)/shard_map/ppermute | solution.py:120
  53.7 5.2 %keyval.1 = (bf16[1280,1536]{1,0:T(8,128)(2,1)S(1)}, bf16[768,1536]{1,0:T(8,128)(2,1)S(1)}, bf16[768,768]{1,0:T(8,128)(2,1)S(1)}, bf16[128,768]{1,0:T(8,128)(2,1)S(1)}, f32[8,128]{1,0:T(8,128)S(1)}) custom-call(s32[4]{0:T(128)S(1)} %copy-done.3, bf16[1280,768]{1,0:T(8,128)(2,1)S(1)} %get-tuple-element.320.refs_0_, ...), custom_call_target="tpu_custom_call" | custom-call | bytes 1024 | tf_op jit(solution)/shard_map/keyval/pallas_call | solution.py:83
  62.6 6.8 %cross_fwd.1 = (bf16[128,768]{1,0:T(8,128)(2,1)S(1)}, f32[6,256,1]{2,1,0:T(8,128)S(1)}, f32[8,128]{1,0:T(8,128)S(1)}) custom-call(s32[4]{0:T(128)S(1)} %copy-done.3, s32[1,1280]{1,0:T(1,128)S(1)} %copy-done.9, s32[1,128]{1,0:T(1,128)S(1)} %copy-done.10, bf16[128,768]{1,0:T(8,128)(2,1)S(1)} %get-tuple-element.337.refs_2_, ...), custom_call_target="tpu_custom_call" | custom-call | bytes 1024 | tf_op jit(solution)/shard_map/cross_fwd/pallas_call | solution.py:83
  69.4 5.3 %collective-permute-done.21.refs_3_.refs_5_.refs_1_ = bf16[96,1536]{1,0:T(8,128)(2,1)S(1)} collective-permute-done((bf16[96,1536]{1,0:T(8,128)(2,1)S(1)}, bf16[96,1536]{1,0:T(8,128)(2,1)S(1)}, u32[]{:S(2)}, u32[]{:S(2)}) %collective-permute-start.21) | collective-permute-done | bytes 294944 | tf_op jit(solution)/shard_map/ppermute | solution.py:120
  76.1 3.6 %collective-permute-start.22 = (bf16[2,8,96,768]{3,2,1,0:T(8,128)(2,1)S(1)}, bf16[2,8,96,768]{3,2,1,0:T(8,128)(2,1)S(1)}, u32[]{:S(2)}, u32[]{:S(2)}) collective-permute-start(bf16[2,8,96,768]{3,2,1,0:T(8,128)(2,1)S(1)} %bitcast.50), channel_id=1, source_target_pairs={{0,8},{8,0},{16,24},{24,16},{1,9},{9,1},{17,25},{25,17},{2,10},{10... | collective-permute-start | bytes 7077896 | tf_op jit(solution)/shard_map/ppermute | solution.py:108
  90.0 4.1 %collective-permute-done.26.refs_8_.refs_3_ = bf16[96,1536]{1,0:T(8,128)(2,1)S(1)} collective-permute-done((bf16[96,1536]{1,0:T(8,128)(2,1)S(1)}, bf16[96,1536]{1,0:T(8,128)(2,1)S(1)}, u32[]{:S(2)}, u32[]{:S(2)}) %collective-permute-start.26) | collective-permute-done | bytes 294944 | tf_op jit(solution)/shard_map/ppermute | solution.py:117
  120.8 4.5 %collective-permute-done.37.refs_1_ = bf16[128,768]{1,0:T(8,128)(2,1)S(1)} collective-permute-done((bf16[128,768]{1,0:T(8,128)(2,1)S(1)}, bf16[128,768]{1,0:T(8,128)(2,1)S(1)}, u32[]{:S(2)}, u32[]{:S(2)}) %collective-permute-start.37) | collective-permute-done | bytes 196640 | tf_op jit(solution)/shard_map/ppermute | solution.py:111
  136.2 5.6 %self_back.1 = (f32[128,768]{1,0:T(8,128)S(1)}, bf16[128,768]{1,0:T(8,128)(2,1)S(1)}, bf16[4,2,96,640]{3,2,1,0:T(8,128)(2,1)S(1)}, bf16[4,2,96,640]{3,2,1,0:T(8,128)(2,1)S(1)}, f32[8,128]{1,0:T(8,128)S(1)}) custom-call(s32[4]{0:T(128)S(1)} %copy-done.3, bf16[256,1152]{1,0:T(8,128)(2,1)S(1)} %get-tuple-element.421.refs_0_, ...), custom_call_target="tpu_custom_call" | custom-call | bytes 1024 | tf_op jit(solution)/shard_map/self_back/pallas_call | solution.py:83
  142.5 4.7 %collective-permute-done.43.refs_2_ = bf16[4,96,768]{2,1,0:T(8,128)(2,1)S(1)} collective-permute-done((bf16[4,96,768]{2,1,0:T(8,128)(2,1)S(1)}, bf16[4,96,768]{2,1,0:T(8,128)(2,1)S(1)}, u32[]{:S(2)}, u32[]{:S(2)}) %collective-permute-start.43) | collective-permute-done | bytes 589856 | tf_op jit(solution)/shard_map/ppermute | solution.py:117
  148.0 3.7 %gate_back.1 = (f32[128,768]{1,0:T(8,128)S(1)}, bf16[128,768]{1,0:T(8,128)(2,1)S(1)}, f32[128,768]{1,0:T(8,128)S(1)}, bf16[2,8,96,768]{3,2,1,0:T(8,128)(2,1)S(1)...) custom-call(s32[4]{0:T(128)S(1)} %copy-done.3, ...), custom_call_target="tpu_custom_call" | custom-call | bytes 1024 | tf_op jit(solution)/shard_map/gate_back/pallas_call | solution.py:83
  157.7 4.9 %cross_back.2 = (bf16[128,384]{1,0:T(8,128)(2,1)S(1)}, bf16[2,1280,384]{2,1,0:T(8,128)(2,1)S(1)}, f32[8,128]{1,0:T(8,128)S(1)}) custom-call(s32[4]{0:T(128)S(1)} %copy-done.3, s32[1,1280]{1,0:T(1,128)S(1)} %copy-done.9, s32[1,128]{1,0:T(1,128)S(1)} %copy-done.10, bf16[128,768]{1,0:T(8,128)(2,1)S(1)} %get-tuple-element.337.refs_2_, ...), custom_call_target="tpu_custom_call" | custom-call | bytes 1024 | tf_op jit(solution)/shard_map/cross_back/pallas_call | solution.py:83
  166.7 3.4 %cross_weights.2 = (bf16[768,384]{1,0:T(8,128)(2,1)S(1)}, bf16[768,384]{1,0:T(8,128)(2,1)S(1)}, bf16[768,384]{1,0:T(8,128)(2,1)S(1)}, f32[8,128]{1,0:T(8,128)S(1)}) custom-call(s32[4]{0:T(128)S(1)} %copy-done.3, bf16[1280,768]{1,0:T(8,128)(2,1)S(1)} %get-tuple-element.320.refs_0_, bf16[128,768]{1,0:T(8,128)(2,1)S(1)} %get-tuple-element.321.refs_1_.refs_4_, ...), custom_call_target="tpu_custom_call" | custom-call | bytes 1024 | tf_op jit(solution)/shard_map/cross_weights/pallas_call | solution.py:83
  173.8 4.9 %cross_back.3 = (bf16[128,384]{1,0:T(8,128)(2,1)S(1)}, bf16[2,1280,384]{2,1,0:T(8,128)(2,1)S(1)}, f32[8,128]{1,0:T(8,128)S(1)}) custom-call(s32[4]{0:T(128)S(1)} %copy-done.3, s32[1,1280]{1,0:T(1,128)S(1)} %copy-done.9, s32[1,128]{1,0:T(1,128)S(1)} %copy-done.10, bf16[128,768]{1,0:T(8,128)(2,1)S(1)} %get-tuple-element.337.refs_2_, ...), custom_call_target="tpu_custom_call" | custom-call | bytes 1024 | tf_op jit(solution)/shard_map/cross_back/pallas_call | solution.py:83
  180.5 4.9 %collective-permute-done.49.refs_2_ = bf16[4,96,640]{2,1,0:T(8,128)(2,1)S(1)} collective-permute-done((bf16[4,96,640]{2,1,0:T(8,128)(2,1)S(1)}, bf16[4,96,640]{2,1,0:T(8,128)(2,1)S(1)}, u32[]{:S(2)}, u32[]{:S(2)}) %collective-permute-start.49) | collective-permute-done | bytes 491552 | tf_op jit(solution)/shard_map/ppermute | solution.py:117
  186.1 3.4 %cross_weights.3 = (bf16[768,384]{1,0:T(8,128)(2,1)S(1)}, bf16[768,384]{1,0:T(8,128)(2,1)S(1)}, bf16[768,384]{1,0:T(8,128)(2,1)S(1)}, f32[8,128]{1,0:T(8,128)S(1)}) custom-call(s32[4]{0:T(128)S(1)} %copy-done.3, bf16[1280,768]{1,0:T(8,128)(2,1)S(1)} %get-tuple-element.320.refs_0_, bf16[128,768]{1,0:T(8,128)(2,1)S(1)} %get-tuple-element.321.refs_1_.refs_4_, ...), custom_call_target="tpu_custom_call" | custom-call | bytes 1024 | tf_op jit(solution)/shard_map/cross_weights/pallas_call | solution.py:83
  192.4 4.5 %collective-permute-start.57 = (bf16[2,96,640]{2,1,0:T(8,128)(2,1)S(1)}, bf16[2,96,640]{2,1,0:T(8,128)(2,1)S(1)}, u32[]{:S(2)}, u32[]{:S(2)}) collective-permute-start(bf16[2,96,640]{2,1,0:T(8,128)(2,1)S(1)} %get-tuple-element.492), channel_id=1, source_target_pairs={{0,2},{1,3},{2,0},{3,1},{4,6},{5,7},{6,4},{7,5},{8,10},{9,11},{10,... | collective-permute-start | bytes 737288 | tf_op jit(solution)/shard_map/ppermute | solution.py:120
  197.0 8.1 %text_back.1 = (f32[1280,768]{1,0:T(8,128)}, f32[2,768]{1,0:T(2,128)S(1)}, f32[8,128]{1,0:T(8,128)S(1)}) custom-call(s32[4]{0:T(128)S(1)} %copy-done.3, bf16[1280,768]{1,0:T(8,128)(2,1)S(1)} %bitcast.34, f32[1,3072]{1,0:T(1,128)S(1)} %get-tuple-element.314.refs_2_.refs_3_.refs_5_.refs_8_.refs_1_.refs_6_, bf16[768,1536]{1,0:T(8,128)(2,1)S(1)} %get-tuple-element.483.refs_2_, ...), custom_call_target="tpu_custom_call" | custom-call | bytes 1024 | tf_op jit(solution)/shard_map/text_back/pallas_call | solution.py:83
  209.4 4.0 %collective-permute-start.61 = (bf16[2,96,384]{2,1,0:T(8,128)(2,1)S(1)}, bf16[2,96,384]{2,1,0:T(8,128)(2,1)S(1)}, u32[]{:S(2)}, u32[]{:S(2)}) collective-permute-start(bf16[2,96,384]{2,1,0:T(8,128)(2,1)S(1)} %get-tuple-element.507), channel_id=1, source_target_pairs={{0,2},{1,3},{2,0},{3,1},{4,6},{5,7},{6,4},{7,5},{8,10},{9,11},{10,... | collective-permute-start | bytes 442376 | tf_op jit(solution)/shard_map/ppermute | solution.py:120
  221.8 4.9 %collective-permute-done.64.refs_3_ = bf16[1,96,384]{2,1,0:T(8,128)(2,1)S(1)} collective-permute-done((bf16[1,96,384]{2,1,0:T(8,128)(2,1)S(1)}, bf16[1,96,384]{2,1,0:T(8,128)(2,1)S(1)}, u32[]{:S(2)}, u32[]{:S(2)}) %collective-permute-start.64) | collective-permute-done | bytes 73760 | tf_op jit(solution)/shard_map/ppermute | solution.py:120
  228.1 4.4 %collective-permute-start.73 = (bf16[96,2176]{1,0:T(8,128)(2,1)S(1)}, bf16[96,2176]{1,0:T(8,128)(2,1)S(1)}, u32[]{:S(2)}, u32[]{:S(2)}) collective-permute-start(bf16[96,2176]{1,0:T(8,128)(2,1)S(1)} %get-tuple-element.531.refs_0_), channel_id=1, source_target_pairs={{0,8},{8,0},{16,24},{24,16},{1,9},{9,1},{17,25},{25,17},{2,10},{10... | collective-permute-start | bytes 1253384 | tf_op jit(solution)/shard_map/ppermute | solution.py:108
  246.2 3.4 %collective-permute-done.71.refs_1_ = bf16[1,96,768]{2,1,0:T(8,128)(2,1)S(1)} collective-permute-done((bf16[1,96,768]{2,1,0:T(8,128)(2,1)S(1)}, bf16[1,96,768]{2,1,0:T(8,128)(2,1)S(1)}, u32[]{:S(2)}, u32[]{:S(2)}) %collective-permute-start.71) | collective-permute-done | bytes 147488 | tf_op jit(solution)/shard_map/ppermute | solution.py:120
  (213 shorter events, 146.1 us)
Async XLA Ops:
  22.6 14.3 %collective-permute-start.8 = (bf16[4,112,384]{2,1,0:T(8,128)(2,1)S(1)}, bf16[4,112,384]{2,1,0:T(8,128)(2,1)S(1)}, u32[]{:S(2)}, u32[]{:S(2)}) collective-permute-start(bf16[4,112,384]{2,1,0:T(8,128)(2,1)S(1)} %get-tuple-element.293.refs_4_), channel_id=1, source_target_pairs={{0,1},{1,0},{2,3},{3,2},{4,5},{5,4},{6,7},{7,6},{8,9},{9,8},{10,11... | collective-permute-start | bytes 1032200 | tf_op jit(solution)/shard_map/ppermute | solution.py:117
  37.6 16.0 %collective-permute-start.12 = (bf16[3,768,384]{2,1,0:T(8,128)(2,1)S(1)}, bf16[3,768,384]{2,1,0:T(8,128)(2,1)S(1)}, u32[]{:S(2)}, u32[]{:S(2)}) collective-permute-start(bf16[3,768,384]{2,1,0:T(8,128)(2,1)S(1)} %bitcast.56), channel_id=1, source_target_pairs={{0,8},{8,0},{16,24},{24,16},{1,9},{9,1},{17,25},{25,17},{2,10},{10... | collective-permute-start | bytes 5308424 | tf_op jit(solution)/shard_map/ppermute | solution.py:108
  43.4 16.0 %collective-permute-start.17 = (bf16[4,96,768]{2,1,0:T(8,128)(2,1)S(1)}, bf16[4,96,768]{2,1,0:T(8,128)(2,1)S(1)}, u32[]{:S(2)}, u32[]{:S(2)}) collective-permute-start(bf16[4,96,768]{2,1,0:T(8,128)(2,1)S(1)} %get-tuple-element.344.refs_0_), channel_id=1, source_target_pairs={{0,16},{8,24},{16,0},{24,8},{1,17},{9,25},{17,1},{25,9},{2,18},{10... | collective-permute-start | bytes 1769480 | tf_op jit(solution)/shard_map/ppermute | solution.py:111
  43.7 15.8 %collective-permute-start.15 = (bf16[4,96,768]{2,1,0:T(8,128)(2,1)S(1)}, bf16[4,96,768]{2,1,0:T(8,128)(2,1)S(1)}, u32[]{:S(2)}, u32[]{:S(2)}) collective-permute-start(bf16[4,96,768]{2,1,0:T(8,128)(2,1)S(1)} %get-tuple-element.344.refs_0_), channel_id=1, source_target_pairs={{0,1},{1,0},{2,3},{3,2},{4,5},{5,4},{6,7},{7,6},{8,9},{9,8},{10,11... | collective-permute-start | bytes 1769480 | tf_op jit(solution)/shard_map/ppermute | solution.py:117
  59.5 15.9 %collective-permute-start.18 = (bf16[4,96,768]{2,1,0:T(8,128)(2,1)S(1)}, bf16[4,96,768]{2,1,0:T(8,128)(2,1)S(1)}, u32[]{:S(2)}, u32[]{:S(2)}) collective-permute-start(bf16[4,96,768]{2,1,0:T(8,128)(2,1)S(1)} %collective-permute-done.15.refs_5_.refs_1_), channel_id=1, source_target_pairs={{0,16},{8,24},{16,0},{24,8},{1,17},{9,25},{17,1},{25,9},{2,18},{10... | collective-permute-start | bytes 1769480 | tf_op jit(solution)/shard_map/ppermute | solution.py:111
  59.8 15.0 %collective-permute-start.19 = (bf16[4,96,640]{2,1,0:T(8,128)(2,1)S(1)}, bf16[4,96,640]{2,1,0:T(8,128)(2,1)S(1)}, u32[]{:S(2)}, u32[]{:S(2)}) collective-permute-start(bf16[4,96,640]{2,1,0:T(8,128)(2,1)S(1)} %get-tuple-element.353.refs_0_), channel_id=1, source_target_pairs={{0,1},{1,0},{2,3},{3,2},{4,5},{5,4},{6,7},{7,6},{8,9},{9,8},{10,11... | collective-permute-start | bytes 1474568 | tf_op jit(solution)/shard_map/ppermute | solution.py:117
  60.7 14.0 %collective-permute-start.21 = (bf16[96,1536]{1,0:T(8,128)(2,1)S(1)}, bf16[96,1536]{1,0:T(8,128)(2,1)S(1)}, u32[]{:S(2)}, u32[]{:S(2)}) collective-permute-start(bf16[96,1536]{1,0:T(8,128)(2,1)S(1)} %copy-done.5), channel_id=1, source_target_pairs={{0,2},{1,3},{2,0},{3,1},{4,6},{5,7},{6,4},{7,5},{8,10},{9,11},{10,... | collective-permute-start | bytes 884744 | tf_op jit(solution)/shard_map/ppermute | solution.py:120
  60.9 13.9 %collective-permute-start.20 = (bf16[96,1536]{1,0:T(8,128)(2,1)S(1)}, bf16[96,1536]{1,0:T(8,128)(2,1)S(1)}, u32[]{:S(2)}, u32[]{:S(2)}) collective-permute-start(bf16[96,1536]{1,0:T(8,128)(2,1)S(1)} %copy-done.5), channel_id=1, source_target_pairs={{0,4},{1,5},{2,6},{3,7},{4,0},{5,1},{6,2},{7,3},{8,12},{9,13},{10,... | collective-permute-start | bytes 884744 | tf_op jit(solution)/shard_map/ppermute | solution.py:120
  81.1 12.9 %collective-permute-start.26 = (bf16[96,1536]{1,0:T(8,128)(2,1)S(1)}, bf16[96,1536]{1,0:T(8,128)(2,1)S(1)}, u32[]{:S(2)}, u32[]{:S(2)}) collective-permute-start(bf16[96,1536]{1,0:T(8,128)(2,1)S(1)} %collective-permute-done.21.refs_3_.refs_5_.refs_1_), channel_id=1, source_target_pairs={{0,1},{1,0},{2,3},{3,2},{4,5},{5,4},{6,7},{7,6},{8,9},{9,8},{10,11... | collective-permute-start | bytes 884744 | tf_op jit(solution)/shard_map/ppermute | solution.py:117
  114.5 13.8 %collective-permute-start.40 = (bf16[768,768]{1,0:T(8,128)(2,1)S(1)}, bf16[768,768]{1,0:T(8,128)(2,1)S(1)}, u32[]{:S(2)}, u32[]{:S(2)}) collective-permute-start(bf16[768,768]{1,0:T(8,128)(2,1)S(1)} %get-tuple-element.425), channel_id=1, source_target_pairs={{0,8},{8,0},{16,24},{24,16},{1,9},{9,1},{17,25},{25,17},{2,10},{10... | collective-permute-start | bytes 3538952 | tf_op jit(solution)/shard_map/ppermute | solution.py:108
  118.2 14.6 %collective-permute-start.41 = (bf16[4,96,768]{2,1,0:T(8,128)(2,1)S(1)}, bf16[4,96,768]{2,1,0:T(8,128)(2,1)S(1)}, u32[]{:S(2)}, u32[]{:S(2)}) collective-permute-start(bf16[4,96,768]{2,1,0:T(8,128)(2,1)S(1)} %get-tuple-element.428), channel_id=1, source_target_pairs={{0,1},{1,0},{2,3},{3,2},{4,5},{5,4},{6,7},{7,6},{8,9},{9,8},{10,11... | collective-permute-start | bytes 1769480 | tf_op jit(solution)/shard_map/ppermute | solution.py:117
  133.6 13.7 %collective-permute-start.43 = (bf16[4,96,768]{2,1,0:T(8,128)(2,1)S(1)}, bf16[4,96,768]{2,1,0:T(8,128)(2,1)S(1)}, u32[]{:S(2)}, u32[]{:S(2)}) collective-permute-start(bf16[4,96,768]{2,1,0:T(8,128)(2,1)S(1)} %get-tuple-element.437), channel_id=1, source_target_pairs={{0,1},{1,0},{2,3},{3,2},{4,5},{5,4},{6,7},{7,6},{8,9},{9,8},{10,11... | collective-permute-start | bytes 1769480 | tf_op jit(solution)/shard_map/ppermute | solution.py:117
  155.3 17.3 %collective-permute-start.51 = (bf16[2,96,768]{2,1,0:T(8,128)(2,1)S(1)}, bf16[2,96,768]{2,1,0:T(8,128)(2,1)S(1)}, u32[]{:S(2)}, u32[]{:S(2)}) collective-permute-start(bf16[2,96,768]{2,1,0:T(8,128)(2,1)S(1)} %get-tuple-element.466), channel_id=1, source_target_pairs={{0,2},{1,3},{2,0},{3,1},{4,6},{5,7},{6,4},{7,5},{8,10},{9,11},{10,... | collective-permute-start | bytes 884744 | tf_op jit(solution)/shard_map/ppermute | solution.py:120
  165.2 14.1 %collective-permute-start.50 = (bf16[4,96,768]{2,1,0:T(8,128)(2,1)S(1)}, bf16[4,96,768]{2,1,0:T(8,128)(2,1)S(1)}, u32[]{:S(2)}, u32[]{:S(2)}) collective-permute-start(bf16[4,96,768]{2,1,0:T(8,128)(2,1)S(1)} %get-tuple-element.464), channel_id=1, source_target_pairs={{0,16},{8,24},{16,0},{24,8},{1,17},{9,25},{17,1},{25,9},{2,18},{10... | collective-permute-start | bytes 1769480 | tf_op jit(solution)/shard_map/ppermute | solution.py:111
  170.1 19.4 %collective-permute-start.52 = (bf16[768,384]{1,0:T(8,128)(2,1)S(1)}, bf16[768,384]{1,0:T(8,128)(2,1)S(1)}, u32[]{:S(2)}, u32[]{:S(2)}) collective-permute-start(bf16[768,384]{1,0:T(8,128)(2,1)S(1)} %get-tuple-element.474), channel_id=1, source_target_pairs={{0,8},{8,0},{16,24},{24,16},{1,9},{9,1},{17,25},{25,17},{2,10},{10... | collective-permute-start | bytes 1769480 | tf_op jit(solution)/shard_map/ppermute | solution.py:108
  172.0 17.4 %collective-permute-start.53 = (bf16[768,384]{1,0:T(8,128)(2,1)S(1)}, bf16[768,384]{1,0:T(8,128)(2,1)S(1)}, u32[]{:S(2)}, u32[]{:S(2)}) collective-permute-start(bf16[768,384]{1,0:T(8,128)(2,1)S(1)} %get-tuple-element.475), channel_id=1, source_target_pairs={{0,8},{8,0},{16,24},{24,16},{1,9},{9,1},{17,25},{25,17},{2,10},{10... | collective-permute-start | bytes 1769480 | tf_op jit(solution)/shard_map/ppermute | solution.py:108
  172.1 17.4 %collective-permute-start.54 = (bf16[768,384]{1,0:T(8,128)(2,1)S(1)}, bf16[768,384]{1,0:T(8,128)(2,1)S(1)}, u32[]{:S(2)}, u32[]{:S(2)}) collective-permute-start(bf16[768,384]{1,0:T(8,128)(2,1)S(1)} %get-tuple-element.476), channel_id=1, source_target_pairs={{0,8},{8,0},{16,24},{24,16},{1,9},{9,1},{17,25},{25,17},{2,10},{10... | collective-permute-start | bytes 1769480 | tf_op jit(solution)/shard_map/ppermute | solution.py:108
  172.6 12.8 %collective-permute-start.49 = (bf16[4,96,640]{2,1,0:T(8,128)(2,1)S(1)}, bf16[4,96,640]{2,1,0:T(8,128)(2,1)S(1)}, u32[]{:S(2)}, u32[]{:S(2)}) collective-permute-start(bf16[4,96,640]{2,1,0:T(8,128)(2,1)S(1)} %get-tuple-element.462), channel_id=1, source_target_pairs={{0,1},{1,0},{2,3},{3,2},{4,5},{5,4},{6,7},{7,6},{8,9},{9,8},{10,11... | collective-permute-start | bytes 1474568 | tf_op jit(solution)/shard_map/ppermute | solution.py:117
  180.0 25.1 %collective-permute-start.59 = (bf16[4,96,768]{2,1,0:T(8,128)(2,1)S(1)}, bf16[4,96,768]{2,1,0:T(8,128)(2,1)S(1)}, u32[]{:S(2)}, u32[]{:S(2)}) collective-permute-start(bf16[4,96,768]{2,1,0:T(8,128)(2,1)S(1)} %get-tuple-element.495), channel_id=1, source_target_pairs={{0,1},{1,0},{2,3},{3,2},{4,5},{5,4},{6,7},{7,6},{8,9},{9,8},{10,11... | collective-permute-start | bytes 1769480 | tf_op jit(solution)/shard_map/ppermute | solution.py:117
  190.5 17.8 %collective-permute-start.55 = (bf16[4,2,96,384]{3,2,1,0:T(8,128)(2,1)S(1)}, bf16[4,2,96,384]{3,2,1,0:T(8,128)(2,1)S(1)}, u32[]{:S(2)}, u32[]{:S(2)}) collective-permute-start(bf16[4,2,96,384]{3,2,1,0:T(8,128)(2,1)S(1)} %get-tuple-element.479), channel_id=1, source_target_pairs={{0,16},{8,24},{16,0},{24,8},{1,17},{9,25},{17,1},{25,9},{2,18},{10... | collective-permute-start | bytes 1769480 | tf_op jit(solution)/shard_map/ppermute | solution.py:111
  191.2 14.6 %collective-permute-start.56 = (bf16[4,96,384]{2,1,0:T(8,128)(2,1)S(1)}, bf16[4,96,384]{2,1,0:T(8,128)(2,1)S(1)}, u32[]{:S(2)}, u32[]{:S(2)}) collective-permute-start(bf16[4,96,384]{2,1,0:T(8,128)(2,1)S(1)} %get-tuple-element.490), channel_id=1, source_target_pairs={{0,1},{1,0},{2,3},{3,2},{4,5},{5,4},{6,7},{7,6},{8,9},{9,8},{10,11... | collective-permute-start | bytes 884744 | tf_op jit(solution)/shard_map/ppermute | solution.py:117
  192.4 12.7 %collective-permute-start.57 = (bf16[2,96,640]{2,1,0:T(8,128)(2,1)S(1)}, bf16[2,96,640]{2,1,0:T(8,128)(2,1)S(1)}, u32[]{:S(2)}, u32[]{:S(2)}) collective-permute-start(bf16[2,96,640]{2,1,0:T(8,128)(2,1)S(1)} %get-tuple-element.492), channel_id=1, source_target_pairs={{0,2},{1,3},{2,0},{3,1},{4,6},{5,7},{6,4},{7,5},{8,10},{9,11},{10,... | collective-permute-start | bytes 737288 | tf_op jit(solution)/shard_map/ppermute | solution.py:120
  209.3 18.0 %collective-permute-start.66 = (bf16[4,96,768]{2,1,0:T(8,128)(2,1)S(1)}, bf16[4,96,768]{2,1,0:T(8,128)(2,1)S(1)}, u32[]{:S(2)}, u32[]{:S(2)}) collective-permute-start(bf16[4,96,768]{2,1,0:T(8,128)(2,1)S(1)} %get-tuple-element.522), channel_id=1, source_target_pairs={{0,16},{8,24},{16,0},{24,8},{1,17},{9,25},{17,1},{25,9},{2,18},{10... | collective-permute-start | bytes 1769480 | tf_op jit(solution)/shard_map/ppermute | solution.py:111
  228.1 15.2 %collective-permute-start.73 = (bf16[96,2176]{1,0:T(8,128)(2,1)S(1)}, bf16[96,2176]{1,0:T(8,128)(2,1)S(1)}, u32[]{:S(2)}, u32[]{:S(2)}) collective-permute-start(bf16[96,2176]{1,0:T(8,128)(2,1)S(1)} %get-tuple-element.531.refs_0_), channel_id=1, source_target_pairs={{0,8},{8,0},{16,24},{24,16},{1,9},{9,1},{17,25},{25,17},{2,10},{10... | collective-permute-start | bytes 1253384 | tf_op jit(solution)/shard_map/ppermute | solution.py:108
  (66 other events, 538.2 us)

commit v2 on v1

--- a/solution.py
+++ b/solution.py
@@ -879,17 +879,18 @@
     y1_came = od.start(ln.y, y1)
     dq_oth, dkv_oth = back_half(1)
     qkv = Sum("qkv", [gc_own, gc_came], w3).go()
-    od.wait(y1_came, down.got)
+    od.wait(y1_came)
     own_b, b_ys, b_yk = run(
         add_core_b, [sds(grid4(D)), sds((depth, rows, D)), sds((depth, rows, D))], at,
         b_keep.reshape((2,) + grid4(D)), b_came.reshape((2,) + grid4(D)), name="add_core_b")
     b_ys = ln.y(b_ys)
+    od.wait(down.got)
     a_came = [ln.core(a) for a in weights_half(dq_oth, dkv_oth)]
     dq_own, dkv_own = back_half(0)
     up.step()
     gates = Sum("gate", [own_b], D, sends=[b_ys], keeps=[b_yk]).go()
+    a_keep = weights_half(dq_own, dkv_own)
     qkv.step()
-    a_keep = weights_half(dq_own, dkv_own)
     own_a, a_y, own_q = run(
         add_core_a, [sds(grid4(HALF))] * 3, at,
         *[a.reshape(grid4(HALF)) for a in (*a_keep, *a_came)], name="add_core_a")

time: 260 us -> 258 us (level)
  waiting for transfers between devices: 63.8 us -> 56.8 us
  starting transfers between devices: 93.3 us -> 97.8 us
    ppermute x18, starting transfers between devices: 13.9 us -> 21.2 us  [y(): return lax.ppermute(a, 'rep', [(r, r ^ 2) for r in range(self.reps)])]
    ppermute x24, waiting for transfers between devices: 29.6 us -> 26.1 us  [along(): return lax.ppermute(a, 'fsdp', [(s, s ^ 2 * k) for s in range(self.shards)])]
    ppermute x14, waiting for transfers between devices: 17.9 us -> 15 us  [across(): return lax.ppermute(a, 'fsdp', [(s, s ^ 1) for s in range(self.shards)])]
  transfers between devices with their start and end apart: 78 -> 78, of which waited for: 25 -> 25; matrix products, arithmetic and copies ran while one was open for 0% -> 0% of each run, Pallas kernels for 32% -> 33%
where the time goes in v2:
time: 258 us; the launch traced here: 257 us
  Pallas kernels  99.3 us (38%)
  starting transfers between devices  97.8 us (38%)
  waiting for transfers between devices  56.8 us (22%)
    pallas_call x56, Pallas kernels, run(): pl.pallas_call(marked, out_shape=list(outs) + [sds((8, 128), F32)], compi...  99.3 us
    ppermute x22, starting transfers between devices, core(): return lax.ppermute(a, 'rep', [(r, r ^ 1) for r in range(self.reps)])  31 us
    ppermute x24, starting transfers between devices, along(): return lax.ppermute(a, 'fsdp', [(s, s ^ 2 * k) for s in range(self.shards)])  30.3 us
    ppermute x24, waiting for transfers between devices, along(): return lax.ppermute(a, 'fsdp', [(s, s ^ 2 * k) for s in range(self.shards)])  26.1 us
    ppermute x18, starting transfers between devices, y(): return lax.ppermute(a, 'rep', [(r, r ^ 2) for r in range(self.reps)])  21.2 us
    ppermute x14, starting transfers between devices, across(): return lax.ppermute(a, 'fsdp', [(s, s ^ 1) for s in range(self.shards)])  15.2 us
    ppermute x14, waiting for transfers between devices, across(): return lax.ppermute(a, 'fsdp', [(s, s ^ 1) for s in range(self.shards)])  15 us
    ppermute x18, waiting for transfers between devices, y(): return lax.ppermute(a, 'rep', [(r, r ^ 2) for r in range(self.reps)])  11.5 us
  transfers between devices with their start and end apart: 78, of which 25 were waited for; matrix products, arithmetic and copies ran while one was open for 0% of the time, Pallas kernels for 33%

profile of v2, /device:TPU:1, one launch (start us, length us, event | category | flops | bytes accessed | tf_op | source)
XLA Modules:
  0.0 257.4 jit_solution(630919627047895667)
XLA Ops:
  8.4 4.1 %pack_rest.1 = (bf16[96,768]{1,0:T(8,128)(2,1)}, bf16[96,640]{1,0:T(8,128)(2,1)}, bf16[96,1536]{1,0:T(8,128)(2,1)}, bf16[136,768]{1,0:T(8,128)(2,1)}, f32[8,128]{1,0:T(8,128)}) custom-call(s32[4]{0:T(128)} %pad_add_fusion.at, bf16[96,768]{1,0:T(8,128)(2,1)} %refs_0_.6, bf16[192,768]{1,0:T(8,128)(2,1)} %refs_1_.6, bf16[96,2304]{1,0:T(8,128)(2,1)} %refs_2_.3, ...), custom_call_target="tpu_custom_call" | custom-call | bytes 1024 | tf_op jit(solution)/shard_map/pack_rest/pallas_call | solution.py:83
  30.4 5.0 %collective-permute-done.11.refs_3_ = bf16[96,768]{1,0:T(8,128)(2,1)S(1)} collective-permute-done((bf16[96,768]{1,0:T(8,128)(2,1)S(1)}, bf16[96,768]{1,0:T(8,128)(2,1)S(1)}, u32[]{:S(2)}, u32[]{:S(2)}) %collective-permute-start.11) | collective-permute-done | bytes 147488 | tf_op jit(solution)/shard_map/ppermute | solution.py:120
  37.6 5.8 %collective-permute-start.12 = (bf16[3,768,384]{2,1,0:T(8,128)(2,1)S(1)}, bf16[3,768,384]{2,1,0:T(8,128)(2,1)S(1)}, u32[]{:S(2)}, u32[]{:S(2)}) collective-permute-start(bf16[3,768,384]{2,1,0:T(8,128)(2,1)S(1)} %bitcast.56), channel_id=1, source_target_pairs={{0,8},{8,0},{16,24},{24,16},{1,9},{9,1},{17,25},{25,17},{2,10},{10... | collective-permute-start | bytes 5308424 | tf_op jit(solution)/shard_map/ppermute | solution.py:108
  50.2 3.4 %collective-permute-start.16 = (bf16[96,640]{1,0:T(8,128)(2,1)S(1)}, bf16[96,640]{1,0:T(8,128)(2,1)S(1)}, u32[]{:S(2)}, u32[]{:S(2)}) collective-permute-start(bf16[96,640]{1,0:T(8,128)(2,1)S(1)} %collective-permute-done.13.refs_6_.refs_2_), channel_id=1, source_target_pairs={{0,2},{1,3},{2,0},{3,1},{4,6},{5,7},{6,4},{7,5},{8,10},{9,11},{10,... | collective-permute-start | bytes 368648 | tf_op jit(solution)/shard_map/ppermute | solution.py:120
  53.7 5.2 %keyval.1 = (bf16[1280,1536]{1,0:T(8,128)(2,1)S(1)}, bf16[768,1536]{1,0:T(8,128)(2,1)S(1)}, bf16[768,768]{1,0:T(8,128)(2,1)S(1)}, bf16[128,768]{1,0:T(8,128)(2,1)S(1)}, f32[8,128]{1,0:T(8,128)S(1)}) custom-call(s32[4]{0:T(128)S(1)} %copy-done.3, bf16[1280,768]{1,0:T(8,128)(2,1)S(1)} %get-tuple-element.320.refs_0_, ...), custom_call_target="tpu_custom_call" | custom-call | bytes 1024 | tf_op jit(solution)/shard_map/keyval/pallas_call | solution.py:83
  62.6 6.8 %cross_fwd.1 = (bf16[128,768]{1,0:T(8,128)(2,1)S(1)}, f32[6,256,1]{2,1,0:T(8,128)S(1)}, f32[8,128]{1,0:T(8,128)S(1)}) custom-call(s32[4]{0:T(128)S(1)} %copy-done.3, s32[1,1280]{1,0:T(1,128)S(1)} %copy-done.9, s32[1,128]{1,0:T(1,128)S(1)} %copy-done.10, bf16[128,768]{1,0:T(8,128)(2,1)S(1)} %get-tuple-element.337.refs_2_, ...), custom_call_target="tpu_custom_call" | custom-call | bytes 1024 | tf_op jit(solution)/shard_map/cross_fwd/pallas_call | solution.py:83
  69.4 5.3 %collective-permute-done.21.refs_3_.refs_5_.refs_1_ = bf16[96,1536]{1,0:T(8,128)(2,1)S(1)} collective-permute-done((bf16[96,1536]{1,0:T(8,128)(2,1)S(1)}, bf16[96,1536]{1,0:T(8,128)(2,1)S(1)}, u32[]{:S(2)}, u32[]{:S(2)}) %collective-permute-start.21) | collective-permute-done | bytes 294944 | tf_op jit(solution)/shard_map/ppermute | solution.py:120
  76.1 3.6 %collective-permute-start.22 = (bf16[2,8,96,768]{3,2,1,0:T(8,128)(2,1)S(1)}, bf16[2,8,96,768]{3,2,1,0:T(8,128)(2,1)S(1)}, u32[]{:S(2)}, u32[]{:S(2)}) collective-permute-start(bf16[2,8,96,768]{3,2,1,0:T(8,128)(2,1)S(1)} %bitcast.50), channel_id=1, source_target_pairs={{0,8},{8,0},{16,24},{24,16},{1,9},{9,1},{17,25},{25,17},{2,10},{10... | collective-permute-start | bytes 7077896 | tf_op jit(solution)/shard_map/ppermute | solution.py:108
  90.0 4.1 %collective-permute-done.26.refs_8_.refs_3_ = bf16[96,1536]{1,0:T(8,128)(2,1)S(1)} collective-permute-done((bf16[96,1536]{1,0:T(8,128)(2,1)S(1)}, bf16[96,1536]{1,0:T(8,128)(2,1)S(1)}, u32[]{:S(2)}, u32[]{:S(2)}) %collective-permute-start.26) | collective-permute-done | bytes 294944 | tf_op jit(solution)/shard_map/ppermute | solution.py:117
  102.1 3.0 %collective-permute-start.35 = (bf16[96,1536]{1,0:T(8,128)(2,1)S(1)}, bf16[96,1536]{1,0:T(8,128)(2,1)S(1)}, u32[]{:S(2)}, u32[]{:S(2)}) collective-permute-start(bf16[96,1536]{1,0:T(8,128)(2,1)S(1)} %collective-permute-done.27.refs_9_.refs_4_), channel_id=1, source_target_pairs={{0,8},{8,0},{16,24},{24,16},{1,9},{9,1},{17,25},{25,17},{2,10},{10... | collective-permute-start | bytes 884744 | tf_op jit(solution)/shard_map/ppermute | solution.py:108
  120.8 4.5 %collective-permute-done.37.refs_1_ = bf16[128,768]{1,0:T(8,128)(2,1)S(1)} collective-permute-done((bf16[128,768]{1,0:T(8,128)(2,1)S(1)}, bf16[128,768]{1,0:T(8,128)(2,1)S(1)}, u32[]{:S(2)}, u32[]{:S(2)}) %collective-permute-start.37) | collective-permute-done | bytes 196640 | tf_op jit(solution)/shard_map/ppermute | solution.py:111
  136.2 5.6 %self_back.1 = (f32[128,768]{1,0:T(8,128)S(1)}, bf16[128,768]{1,0:T(8,128)(2,1)S(1)}, bf16[4,2,96,640]{3,2,1,0:T(8,128)(2,1)S(1)}, bf16[4,2,96,640]{3,2,1,0:T(8,128)(2,1)S(1)}, f32[8,128]{1,0:T(8,128)S(1)}) custom-call(s32[4]{0:T(128)S(1)} %copy-done.3, bf16[256,1152]{1,0:T(8,128)(2,1)S(1)} %get-tuple-element.421.refs_0_, ...), custom_call_target="tpu_custom_call" | custom-call | bytes 1024 | tf_op jit(solution)/shard_map/self_back/pallas_call | solution.py:83
  142.5 4.7 %collective-permute-done.43.refs_2_ = bf16[4,96,768]{2,1,0:T(8,128)(2,1)S(1)} collective-permute-done((bf16[4,96,768]{2,1,0:T(8,128)(2,1)S(1)}, bf16[4,96,768]{2,1,0:T(8,128)(2,1)S(1)}, u32[]{:S(2)}, u32[]{:S(2)}) %collective-permute-start.43) | collective-permute-done | bytes 589856 | tf_op jit(solution)/shard_map/ppermute | solution.py:117
  148.0 3.7 %gate_back.1 = (f32[128,768]{1,0:T(8,128)S(1)}, bf16[128,768]{1,0:T(8,128)(2,1)S(1)}, f32[128,768]{1,0:T(8,128)S(1)}, bf16[2,8,96,768]{3,2,1,0:T(8,128)(2,1)S(1)...) custom-call(s32[4]{0:T(128)S(1)} %copy-done.3, ...), custom_call_target="tpu_custom_call" | custom-call | bytes 1024 | tf_op jit(solution)/shard_map/gate_back/pallas_call | solution.py:83
  157.7 4.9 %cross_back.2 = (bf16[128,384]{1,0:T(8,128)(2,1)S(1)}, bf16[2,1280,384]{2,1,0:T(8,128)(2,1)S(1)}, f32[8,128]{1,0:T(8,128)S(1)}) custom-call(s32[4]{0:T(128)S(1)} %copy-done.3, s32[1,1280]{1,0:T(1,128)S(1)} %copy-done.9, s32[1,128]{1,0:T(1,128)S(1)} %copy-done.10, bf16[128,768]{1,0:T(8,128)(2,1)S(1)} %get-tuple-element.337.refs_2_, ...), custom_call_target="tpu_custom_call" | custom-call | bytes 1024 | tf_op jit(solution)/shard_map/cross_back/pallas_call | solution.py:83
  164.6 3.4 %cross_weights.2 = (bf16[768,384]{1,0:T(8,128)(2,1)S(1)}, bf16[768,384]{1,0:T(8,128)(2,1)S(1)}, bf16[768,384]{1,0:T(8,128)(2,1)S(1)}, f32[8,128]{1,0:T(8,128)S(1)}) custom-call(s32[4]{0:T(128)S(1)} %copy-done.3, bf16[1280,768]{1,0:T(8,128)(2,1)S(1)} %get-tuple-element.320.refs_0_, bf16[128,768]{1,0:T(8,128)(2,1)S(1)} %get-tuple-element.321.refs_1_.refs_4_, ...), custom_call_target="tpu_custom_call" | custom-call | bytes 1024 | tf_op jit(solution)/shard_map/cross_weights/pallas_call | solution.py:83
  171.3 4.9 %cross_back.3 = (bf16[128,384]{1,0:T(8,128)(2,1)S(1)}, bf16[2,1280,384]{2,1,0:T(8,128)(2,1)S(1)}, f32[8,128]{1,0:T(8,128)S(1)}) custom-call(s32[4]{0:T(128)S(1)} %copy-done.3, s32[1,1280]{1,0:T(1,128)S(1)} %copy-done.9, s32[1,128]{1,0:T(1,128)S(1)} %copy-done.10, bf16[128,768]{1,0:T(8,128)(2,1)S(1)} %get-tuple-element.337.refs_2_, ...), custom_call_target="tpu_custom_call" | custom-call | bytes 1024 | tf_op jit(solution)/shard_map/cross_back/pallas_call | solution.py:83
  179.9 3.4 %cross_weights.3 = (bf16[768,384]{1,0:T(8,128)(2,1)S(1)}, bf16[768,384]{1,0:T(8,128)(2,1)S(1)}, bf16[768,384]{1,0:T(8,128)(2,1)S(1)}, f32[8,128]{1,0:T(8,128)S(1)}) custom-call(s32[4]{0:T(128)S(1)} %copy-done.3, bf16[1280,768]{1,0:T(8,128)(2,1)S(1)} %get-tuple-element.320.refs_0_, bf16[128,768]{1,0:T(8,128)(2,1)S(1)} %get-tuple-element.321.refs_1_.refs_4_, ...), custom_call_target="tpu_custom_call" | custom-call | bytes 1024 | tf_op jit(solution)/shard_map/cross_weights/pallas_call | solution.py:83
  187.9 2.9 %collective-permute-start.57 = (bf16[2,96,640]{2,1,0:T(8,128)(2,1)S(1)}, bf16[2,96,640]{2,1,0:T(8,128)(2,1)S(1)}, u32[]{:S(2)}, u32[]{:S(2)}) collective-permute-start(bf16[2,96,640]{2,1,0:T(8,128)(2,1)S(1)} %get-tuple-element.492), channel_id=1, source_target_pairs={{0,2},{1,3},{2,0},{3,1},{4,6},{5,7},{6,4},{7,5},{8,10},{9,11},{10,... | collective-permute-start | bytes 737288 | tf_op jit(solution)/shard_map/ppermute | solution.py:120
  190.8 8.1 %text_back.1 = (f32[1280,768]{1,0:T(8,128)}, f32[2,768]{1,0:T(2,128)S(1)}, f32[8,128]{1,0:T(8,128)S(1)}) custom-call(s32[4]{0:T(128)S(1)} %copy-done.3, bf16[1280,768]{1,0:T(8,128)(2,1)S(1)} %bitcast.34, f32[1,3072]{1,0:T(1,128)S(1)} %get-tuple-element.314.refs_2_.refs_3_.refs_5_.refs_8_.refs_1_.refs_6_, bf16[768,1536]{1,0:T(8,128)(2,1)S(1)} %get-tuple-element.483.refs_2_, ...), custom_call_target="tpu_custom_call" | custom-call | bytes 1024 | tf_op jit(solution)/shard_map/text_back/pallas_call | solution.py:83
  207.7 2.9 %collective-permute-start.61 = (bf16[2,96,384]{2,1,0:T(8,128)(2,1)S(1)}, bf16[2,96,384]{2,1,0:T(8,128)(2,1)S(1)}, u32[]{:S(2)}, u32[]{:S(2)}) collective-permute-start(bf16[2,96,384]{2,1,0:T(8,128)(2,1)S(1)} %get-tuple-element.507), channel_id=1, source_target_pairs={{0,2},{1,3},{2,0},{3,1},{4,6},{5,7},{6,4},{7,5},{8,10},{9,11},{10,... | collective-permute-start | bytes 442376 | tf_op jit(solution)/shard_map/ppermute | solution.py:120
  220.2 4.2 %collective-permute-done.64.refs_3_ = bf16[1,96,384]{2,1,0:T(8,128)(2,1)S(1)} collective-permute-done((bf16[1,96,384]{2,1,0:T(8,128)(2,1)S(1)}, bf16[1,96,384]{2,1,0:T(8,128)(2,1)S(1)}, u32[]{:S(2)}, u32[]{:S(2)}) %collective-permute-start.64) | collective-permute-done | bytes 73760 | tf_op jit(solution)/shard_map/ppermute | solution.py:120
  227.3 3.4 %collective-permute-start.73 = (bf16[96,2176]{1,0:T(8,128)(2,1)S(1)}, bf16[96,2176]{1,0:T(8,128)(2,1)S(1)}, u32[]{:S(2)}, u32[]{:S(2)}) collective-permute-start(bf16[96,2176]{1,0:T(8,128)(2,1)S(1)} %get-tuple-element.531.refs_0_), channel_id=1, source_target_pairs={{0,8},{8,0},{16,24},{24,16},{1,9},{9,1},{17,25},{25,17},{2,10},{10... | collective-permute-start | bytes 1253384 | tf_op jit(solution)/shard_map/ppermute | solution.py:108
  244.9 3.9 %collective-permute-start.75 = (bf16[96,768]{1,0:T(8,128)(2,1)S(1)}, bf16[96,768]{1,0:T(8,128)(2,1)S(1)}, u32[]{:S(2)}, u32[]{:S(2)}) collective-permute-start(bf16[96,768]{1,0:T(8,128)(2,1)S(1)} %get-tuple-element.537.refs_0_), channel_id=1, source_target_pairs={{0,16},{8,24},{16,0},{24,8},{1,17},{9,25},{17,1},{25,9},{2,18},{10... | collective-permute-start | bytes 442376 | tf_op jit(solution)/shard_map/ppermute | solution.py:111
  (213 shorter events, 149.2 us)
Async XLA Ops:
  22.6 14.3 %collective-permute-start.8 = (bf16[4,112,384]{2,1,0:T(8,128)(2,1)S(1)}, bf16[4,112,384]{2,1,0:T(8,128)(2,1)S(1)}, u32[]{:S(2)}, u32[]{:S(2)}) collective-permute-start(bf16[4,112,384]{2,1,0:T(8,128)(2,1)S(1)} %get-tuple-element.293.refs_4_), channel_id=1, source_target_pairs={{0,1},{1,0},{2,3},{3,2},{4,5},{5,4},{6,7},{7,6},{8,9},{9,8},{10,11... | collective-permute-start | bytes 1032200 | tf_op jit(solution)/shard_map/ppermute | solution.py:117
  37.6 16.0 %collective-permute-start.12 = (bf16[3,768,384]{2,1,0:T(8,128)(2,1)S(1)}, bf16[3,768,384]{2,1,0:T(8,128)(2,1)S(1)}, u32[]{:S(2)}, u32[]{:S(2)}) collective-permute-start(bf16[3,768,384]{2,1,0:T(8,128)(2,1)S(1)} %bitcast.56), channel_id=1, source_target_pairs={{0,8},{8,0},{16,24},{24,16},{1,9},{9,1},{17,25},{25,17},{2,10},{10... | collective-permute-start | bytes 5308424 | tf_op jit(solution)/shard_map/ppermute | solution.py:108
  43.4 16.0 %collective-permute-start.17 = (bf16[4,96,768]{2,1,0:T(8,128)(2,1)S(1)}, bf16[4,96,768]{2,1,0:T(8,128)(2,1)S(1)}, u32[]{:S(2)}, u32[]{:S(2)}) collective-permute-start(bf16[4,96,768]{2,1,0:T(8,128)(2,1)S(1)} %get-tuple-element.344.refs_0_), channel_id=1, source_target_pairs={{0,16},{8,24},{16,0},{24,8},{1,17},{9,25},{17,1},{25,9},{2,18},{10... | collective-permute-start | bytes 1769480 | tf_op jit(solution)/shard_map/ppermute | solution.py:111
  43.7 15.8 %collective-permute-start.15 = (bf16[4,96,768]{2,1,0:T(8,128)(2,1)S(1)}, bf16[4,96,768]{2,1,0:T(8,128)(2,1)S(1)}, u32[]{:S(2)}, u32[]{:S(2)}) collective-permute-start(bf16[4,96,768]{2,1,0:T(8,128)(2,1)S(1)} %get-tuple-element.344.refs_0_), channel_id=1, source_target_pairs={{0,1},{1,0},{2,3},{3,2},{4,5},{5,4},{6,7},{7,6},{8,9},{9,8},{10,11... | collective-permute-start | bytes 1769480 | tf_op jit(solution)/shard_map/ppermute | solution.py:117
  59.5 15.9 %collective-permute-start.18 = (bf16[4,96,768]{2,1,0:T(8,128)(2,1)S(1)}, bf16[4,96,768]{2,1,0:T(8,128)(2,1)S(1)}, u32[]{:S(2)}, u32[]{:S(2)}) collective-permute-start(bf16[4,96,768]{2,1,0:T(8,128)(2,1)S(1)} %collective-permute-done.15.refs_5_.refs_1_), channel_id=1, source_target_pairs={{0,16},{8,24},{16,0},{24,8},{1,17},{9,25},{17,1},{25,9},{2,18},{10... | collective-permute-start | bytes 1769480 | tf_op jit(solution)/shard_map/ppermute | solution.py:111
  59.8 15.0 %collective-permute-start.19 = (bf16[4,96,640]{2,1,0:T(8,128)(2,1)S(1)}, bf16[4,96,640]{2,1,0:T(8,128)(2,1)S(1)}, u32[]{:S(2)}, u32[]{:S(2)}) collective-permute-start(bf16[4,96,640]{2,1,0:T(8,128)(2,1)S(1)} %get-tuple-element.353.refs_0_), channel_id=1, source_target_pairs={{0,1},{1,0},{2,3},{3,2},{4,5},{5,4},{6,7},{7,6},{8,9},{9,8},{10,11... | collective-permute-start | bytes 1474568 | tf_op jit(solution)/shard_map/ppermute | solution.py:117
  60.7 14.0 %collective-permute-start.21 = (bf16[96,1536]{1,0:T(8,128)(2,1)S(1)}, bf16[96,1536]{1,0:T(8,128)(2,1)S(1)}, u32[]{:S(2)}, u32[]{:S(2)}) collective-permute-start(bf16[96,1536]{1,0:T(8,128)(2,1)S(1)} %copy-done.5), channel_id=1, source_target_pairs={{0,2},{1,3},{2,0},{3,1},{4,6},{5,7},{6,4},{7,5},{8,10},{9,11},{10,... | collective-permute-start | bytes 884744 | tf_op jit(solution)/shard_map/ppermute | solution.py:120
  60.9 13.9 %collective-permute-start.20 = (bf16[96,1536]{1,0:T(8,128)(2,1)S(1)}, bf16[96,1536]{1,0:T(8,128)(2,1)S(1)}, u32[]{:S(2)}, u32[]{:S(2)}) collective-permute-start(bf16[96,1536]{1,0:T(8,128)(2,1)S(1)} %copy-done.5), channel_id=1, source_target_pairs={{0,4},{1,5},{2,6},{3,7},{4,0},{5,1},{6,2},{7,3},{8,12},{9,13},{10,... | collective-permute-start | bytes 884744 | tf_op jit(solution)/shard_map/ppermute | solution.py:120
  81.1 12.9 %collective-permute-start.26 = (bf16[96,1536]{1,0:T(8,128)(2,1)S(1)}, bf16[96,1536]{1,0:T(8,128)(2,1)S(1)}, u32[]{:S(2)}, u32[]{:S(2)}) collective-permute-start(bf16[96,1536]{1,0:T(8,128)(2,1)S(1)} %collective-permute-done.21.refs_3_.refs_5_.refs_1_), channel_id=1, source_target_pairs={{0,1},{1,0},{2,3},{3,2},{4,5},{5,4},{6,7},{7,6},{8,9},{9,8},{10,11... | collective-permute-start | bytes 884744 | tf_op jit(solution)/shard_map/ppermute | solution.py:117
  114.5 13.8 %collective-permute-start.40 = (bf16[768,768]{1,0:T(8,128)(2,1)S(1)}, bf16[768,768]{1,0:T(8,128)(2,1)S(1)}, u32[]{:S(2)}, u32[]{:S(2)}) collective-permute-start(bf16[768,768]{1,0:T(8,128)(2,1)S(1)} %get-tuple-element.425), channel_id=1, source_target_pairs={{0,8},{8,0},{16,24},{24,16},{1,9},{9,1},{17,25},{25,17},{2,10},{10... | collective-permute-start | bytes 3538952 | tf_op jit(solution)/shard_map/ppermute | solution.py:108
  118.2 14.6 %collective-permute-start.41 = (bf16[4,96,768]{2,1,0:T(8,128)(2,1)S(1)}, bf16[4,96,768]{2,1,0:T(8,128)(2,1)S(1)}, u32[]{:S(2)}, u32[]{:S(2)}) collective-permute-start(bf16[4,96,768]{2,1,0:T(8,128)(2,1)S(1)} %get-tuple-element.428), channel_id=1, source_target_pairs={{0,1},{1,0},{2,3},{3,2},{4,5},{5,4},{6,7},{7,6},{8,9},{9,8},{10,11... | collective-permute-start | bytes 1769480 | tf_op jit(solution)/shard_map/ppermute | solution.py:117
  133.6 13.7 %collective-permute-start.43 = (bf16[4,96,768]{2,1,0:T(8,128)(2,1)S(1)}, bf16[4,96,768]{2,1,0:T(8,128)(2,1)S(1)}, u32[]{:S(2)}, u32[]{:S(2)}) collective-permute-start(bf16[4,96,768]{2,1,0:T(8,128)(2,1)S(1)} %get-tuple-element.437), channel_id=1, source_target_pairs={{0,1},{1,0},{2,3},{3,2},{4,5},{5,4},{6,7},{7,6},{8,9},{9,8},{10,11... | collective-permute-start | bytes 1769480 | tf_op jit(solution)/shard_map/ppermute | solution.py:117
  155.3 14.8 %collective-permute-start.50 = (bf16[2,96,768]{2,1,0:T(8,128)(2,1)S(1)}, bf16[2,96,768]{2,1,0:T(8,128)(2,1)S(1)}, u32[]{:S(2)}, u32[]{:S(2)}) collective-permute-start(bf16[2,96,768]{2,1,0:T(8,128)(2,1)S(1)} %get-tuple-element.465), channel_id=1, source_target_pairs={{0,2},{1,3},{2,0},{3,1},{4,6},{5,7},{6,4},{7,5},{8,10},{9,11},{10,... | collective-permute-start | bytes 884744 | tf_op jit(solution)/shard_map/ppermute | solution.py:120
  164.4 13.6 %collective-permute-start.49 = (bf16[4,96,768]{2,1,0:T(8,128)(2,1)S(1)}, bf16[4,96,768]{2,1,0:T(8,128)(2,1)S(1)}, u32[]{:S(2)}, u32[]{:S(2)}) collective-permute-start(bf16[4,96,768]{2,1,0:T(8,128)(2,1)S(1)} %get-tuple-element.463), channel_id=1, source_target_pairs={{0,16},{8,24},{16,0},{24,8},{1,17},{9,25},{17,1},{25,9},{2,18},{10... | collective-permute-start | bytes 1769480 | tf_op jit(solution)/shard_map/ppermute | solution.py:111
  168.0 16.1 %collective-permute-start.51 = (bf16[768,384]{1,0:T(8,128)(2,1)S(1)}, bf16[768,384]{1,0:T(8,128)(2,1)S(1)}, u32[]{:S(2)}, u32[]{:S(2)}) collective-permute-start(bf16[768,384]{1,0:T(8,128)(2,1)S(1)} %get-tuple-element.472), channel_id=1, source_target_pairs={{0,8},{8,0},{16,24},{24,16},{1,9},{9,1},{17,25},{25,17},{2,10},{10... | collective-permute-start | bytes 1769480 | tf_op jit(solution)/shard_map/ppermute | solution.py:108
  169.6 14.5 %collective-permute-start.52 = (bf16[768,384]{1,0:T(8,128)(2,1)S(1)}, bf16[768,384]{1,0:T(8,128)(2,1)S(1)}, u32[]{:S(2)}, u32[]{:S(2)}) collective-permute-start(bf16[768,384]{1,0:T(8,128)(2,1)S(1)} %get-tuple-element.473), channel_id=1, source_target_pairs={{0,8},{8,0},{16,24},{24,16},{1,9},{9,1},{17,25},{25,17},{2,10},{10... | collective-permute-start | bytes 1769480 | tf_op jit(solution)/shard_map/ppermute | solution.py:108
  169.7 14.4 %collective-permute-start.53 = (bf16[768,384]{1,0:T(8,128)(2,1)S(1)}, bf16[768,384]{1,0:T(8,128)(2,1)S(1)}, u32[]{:S(2)}, u32[]{:S(2)}) collective-permute-start(bf16[768,384]{1,0:T(8,128)(2,1)S(1)} %get-tuple-element.474), channel_id=1, source_target_pairs={{0,8},{8,0},{16,24},{24,16},{1,9},{9,1},{17,25},{25,17},{2,10},{10... | collective-permute-start | bytes 1769480 | tf_op jit(solution)/shard_map/ppermute | solution.py:108
  170.1 13.2 %collective-permute-start.54 = (bf16[4,96,640]{2,1,0:T(8,128)(2,1)S(1)}, bf16[4,96,640]{2,1,0:T(8,128)(2,1)S(1)}, u32[]{:S(2)}, u32[]{:S(2)}) collective-permute-start(bf16[4,96,640]{2,1,0:T(8,128)(2,1)S(1)} %get-tuple-element.475), channel_id=1, source_target_pairs={{0,1},{1,0},{2,3},{3,2},{4,5},{5,4},{6,7},{7,6},{8,9},{9,8},{10,11... | collective-permute-start | bytes 1474568 | tf_op jit(solution)/shard_map/ppermute | solution.py:117
  178.7 20.3 %collective-permute-start.59 = (bf16[4,96,768]{2,1,0:T(8,128)(2,1)S(1)}, bf16[4,96,768]{2,1,0:T(8,128)(2,1)S(1)}, u32[]{:S(2)}, u32[]{:S(2)}) collective-permute-start(bf16[4,96,768]{2,1,0:T(8,128)(2,1)S(1)} %get-tuple-element.495), channel_id=1, source_target_pairs={{0,1},{1,0},{2,3},{3,2},{4,5},{5,4},{6,7},{7,6},{8,9},{9,8},{10,11... | collective-permute-start | bytes 1769480 | tf_op jit(solution)/shard_map/ppermute | solution.py:117
  185.1 19.0 %collective-permute-start.55 = (bf16[4,2,96,384]{3,2,1,0:T(8,128)(2,1)S(1)}, bf16[4,2,96,384]{3,2,1,0:T(8,128)(2,1)S(1)}, u32[]{:S(2)}, u32[]{:S(2)}) collective-permute-start(bf16[4,2,96,384]{3,2,1,0:T(8,128)(2,1)S(1)} %get-tuple-element.479), channel_id=1, source_target_pairs={{0,16},{8,24},{16,0},{24,8},{1,17},{9,25},{17,1},{25,9},{2,18},{10... | collective-permute-start | bytes 1769480 | tf_op jit(solution)/shard_map/ppermute | solution.py:111
  186.6 14.9 %collective-permute-start.56 = (bf16[4,96,384]{2,1,0:T(8,128)(2,1)S(1)}, bf16[4,96,384]{2,1,0:T(8,128)(2,1)S(1)}, u32[]{:S(2)}, u32[]{:S(2)}) collective-permute-start(bf16[4,96,384]{2,1,0:T(8,128)(2,1)S(1)} %get-tuple-element.490), channel_id=1, source_target_pairs={{0,1},{1,0},{2,3},{3,2},{4,5},{5,4},{6,7},{7,6},{8,9},{9,8},{10,11... | collective-permute-start | bytes 884744 | tf_op jit(solution)/shard_map/ppermute | solution.py:117
  206.0 20.1 %collective-permute-start.66 = (bf16[4,96,768]{2,1,0:T(8,128)(2,1)S(1)}, bf16[4,96,768]{2,1,0:T(8,128)(2,1)S(1)}, u32[]{:S(2)}, u32[]{:S(2)}) collective-permute-start(bf16[4,96,768]{2,1,0:T(8,128)(2,1)S(1)} %get-tuple-element.522), channel_id=1, source_target_pairs={{0,16},{8,24},{16,0},{24,8},{1,17},{9,25},{17,1},{25,9},{2,18},{10... | collective-permute-start | bytes 1769480 | tf_op jit(solution)/shard_map/ppermute | solution.py:111
  217.7 13.0 %collective-permute-start.72 = (bf16[96,2176]{1,0:T(8,128)(2,1)S(1)}, bf16[96,2176]{1,0:T(8,128)(2,1)S(1)}, u32[]{:S(2)}, u32[]{:S(2)}) collective-permute-start(bf16[96,2176]{1,0:T(8,128)(2,1)S(1)} %get-tuple-element.531.refs_0_), channel_id=1, source_target_pairs={{0,16},{8,24},{16,0},{24,8},{1,17},{9,25},{17,1},{25,9},{2,18},{10... | collective-permute-start | bytes 1253384 | tf_op jit(solution)/shard_map/ppermute | solution.py:111
  227.3 14.1 %collective-permute-start.73 = (bf16[96,2176]{1,0:T(8,128)(2,1)S(1)}, bf16[96,2176]{1,0:T(8,128)(2,1)S(1)}, u32[]{:S(2)}, u32[]{:S(2)}) collective-permute-start(bf16[96,2176]{1,0:T(8,128)(2,1)S(1)} %get-tuple-element.531.refs_0_), channel_id=1, source_target_pairs={{0,8},{8,0},{16,24},{24,16},{1,9},{9,1},{17,25},{25,17},{2,10},{10... | collective-permute-start | bytes 1253384 | tf_op jit(solution)/shard_map/ppermute | solution.py:108
  (66 other events, 531.1 us)

commit v3 on v2

--- a/solution.py
+++ b/solution.py
@@ -748,7 +748,7 @@
     mixed, logs = run(
         cross_fwd, [sds((vis, D)), sds((pairs, 2 * vis, 1), F32)],
         at, block_owner, visual_valid, queries, kv,
-        in_specs=[VM, VM, VM, PIN], scratch=[sds((vis, txt), F32)], name="cross_fwd", vmem=16)
+        in_specs=[VM, VM, VM, PIN], scratch=[sds((vis, txt), F32)], name="cross_fwd", vmem=16, cost=6)
     od.wait(*[pieces_d[k] for k in sorted(pieces_d) if k])
     d_x = {0: d_xo}
     for k in sorted(pieces_d):

time: 258 us -> 257 us (level)
  starting transfers between devices: 97.8 us -> 92.1 us
  waiting for transfers between devices: 56.8 us -> 61.5 us
    ppermute x18, starting transfers between devices: 21.2 us -> 11.1 us  [y(): return lax.ppermute(a, 'rep', [(r, r ^ 2) for r in range(self.reps)])]
    ppermute x22, starting transfers between devices: 31 us -> 35.7 us  [core(): return lax.ppermute(a, 'rep', [(r, r ^ 1) for r in range(self.reps)])]
    ppermute x18, waiting for transfers between devices: 11.5 us -> 15.9 us  [y(): return lax.ppermute(a, 'rep', [(r, r ^ 2) for r in range(self.reps)])]
    ppermute x14, waiting for transfers between devices: 15 us -> 18.8 us  [across(): return lax.ppermute(a, 'fsdp', [(s, s ^ 1) for s in range(self.shards)])]
  transfers between devices with their start and end apart: 78 -> 78, of which waited for: 25 -> 28; matrix products, arithmetic and copies ran while one was open for 0% -> 0% of each run, Pallas kernels for 33% -> 33%
where the time goes in v3:
time: 257 us; the launch traced here: 256 us
  Pallas kernels  99.2 us (39%)
  starting transfers between devices  92.1 us (36%)
  waiting for transfers between devices  61.5 us (24%)
    pallas_call x56, Pallas kernels, run(): pl.pallas_call(marked, out_shape=list(outs) + [sds((8, 128), F32)], compi...  99.2 us
    ppermute x22, starting transfers between devices, core(): return lax.ppermute(a, 'rep', [(r, r ^ 1) for r in range(self.reps)])  35.7 us
    ppermute x24, starting transfers between devices, along(): return lax.ppermute(a, 'fsdp', [(s, s ^ 2 * k) for s in range(self.shards)])  30.6 us
    ppermute x24, waiting for transfers between devices, along(): return lax.ppermute(a, 'fsdp', [(s, s ^ 2 * k) for s in range(self.shards)])  23.9 us
    ppermute x14, waiting for transfers between devices, across(): return lax.ppermute(a, 'fsdp', [(s, s ^ 1) for s in range(self.shards)])  18.8 us
    ppermute x18, waiting for transfers between devices, y(): return lax.ppermute(a, 'rep', [(r, r ^ 2) for r in range(self.reps)])  15.9 us
    ppermute x14, starting transfers between devices, across(): return lax.ppermute(a, 'fsdp', [(s, s ^ 1) for s in range(self.shards)])  14.6 us
    ppermute x18, starting transfers between devices, y(): return lax.ppermute(a, 'rep', [(r, r ^ 2) for r in range(self.reps)])  11.1 us
  transfers between devices with their start and end apart: 78, of which 28 were waited for; matrix products, arithmetic and copies ran while one was open for 0% of the time, Pallas kernels for 33%

profile of v3, /device:TPU:1, one launch (start us, length us, event | category | flops | bytes accessed | tf_op | source)
XLA Modules:
  0.0 256.3 jit_solution(10472035322549879869)
XLA Ops:
  8.4 4.1 %pack_rest.1 = (bf16[96,768]{1,0:T(8,128)(2,1)}, bf16[96,640]{1,0:T(8,128)(2,1)}, bf16[96,1536]{1,0:T(8,128)(2,1)}, bf16[136,768]{1,0:T(8,128)(2,1)}, f32[8,128]{1,0:T(8,128)}) custom-call(s32[4]{0:T(128)} %pad_add_fusion.at, bf16[96,768]{1,0:T(8,128)(2,1)} %refs_0_.6, bf16[192,768]{1,0:T(8,128)(2,1)} %refs_1_.6, bf16[96,2304]{1,0:T(8,128)(2,1)} %refs_2_.3, ...), custom_call_target="tpu_custom_call" | custom-call | bytes 1024 | tf_op jit(solution)/shard_map/pack_rest/pallas_call | solution.py:83
  30.4 5.0 %collective-permute-done.11.refs_3_ = bf16[96,768]{1,0:T(8,128)(2,1)S(1)} collective-permute-done((bf16[96,768]{1,0:T(8,128)(2,1)S(1)}, bf16[96,768]{1,0:T(8,128)(2,1)S(1)}, u32[]{:S(2)}, u32[]{:S(2)}) %collective-permute-start.11) | collective-permute-done | bytes 147488 | tf_op jit(solution)/shard_map/ppermute | solution.py:120
  37.6 5.8 %collective-permute-start.12 = (bf16[3,768,384]{2,1,0:T(8,128)(2,1)S(1)}, bf16[3,768,384]{2,1,0:T(8,128)(2,1)S(1)}, u32[]{:S(2)}, u32[]{:S(2)}) collective-permute-start(bf16[3,768,384]{2,1,0:T(8,128)(2,1)S(1)} %bitcast.56), channel_id=1, source_target_pairs={{0,8},{8,0},{16,24},{24,16},{1,9},{9,1},{17,25},{25,17},{2,10},{10... | collective-permute-start | bytes 5308424 | tf_op jit(solution)/shard_map/ppermute | solution.py:108
  50.2 3.4 %collective-permute-start.16 = (bf16[96,640]{1,0:T(8,128)(2,1)S(1)}, bf16[96,640]{1,0:T(8,128)(2,1)S(1)}, u32[]{:S(2)}, u32[]{:S(2)}) collective-permute-start(bf16[96,640]{1,0:T(8,128)(2,1)S(1)} %collective-permute-done.13.refs_6_.refs_2_), channel_id=1, source_target_pairs={{0,2},{1,3},{2,0},{3,1},{4,6},{5,7},{6,4},{7,5},{8,10},{9,11},{10,... | collective-permute-start | bytes 368648 | tf_op jit(solution)/shard_map/ppermute | solution.py:120
  56.5 5.1 %keyval.1 = (bf16[1280,1536]{1,0:T(8,128)(2,1)S(1)}, bf16[768,1536]{1,0:T(8,128)(2,1)S(1)}, bf16[768,768]{1,0:T(8,128)(2,1)S(1)}, bf16[128,768]{1,0:T(8,128)(2,1)S(1)}, f32[8,128]{1,0:T(8,128)S(1)}) custom-call(s32[4]{0:T(128)S(1)} %copy-done.3, bf16[1280,768]{1,0:T(8,128)(2,1)S(1)} %get-tuple-element.320.refs_0_, ...), custom_call_target="tpu_custom_call" | custom-call | bytes 1024 | tf_op jit(solution)/shard_map/keyval/pallas_call | solution.py:83
  62.6 6.8 %cross_fwd.1 = (bf16[128,768]{1,0:T(8,128)(2,1)S(1)}, f32[6,256,1]{2,1,0:T(8,128)S(1)}, f32[8,128]{1,0:T(8,128)S(1)}) custom-call(s32[4]{0:T(128)S(1)} %copy-done.3, s32[1,1280]{1,0:T(1,128)S(1)} %copy-done.9, s32[1,128]{1,0:T(1,128)S(1)} %copy-done.10, bf16[128,768]{1,0:T(8,128)(2,1)S(1)} %get-tuple-element.337.refs_2_, ...), custom_call_target="tpu_custom_call" | custom-call | flops 6899999744 | bytes 1024 | tf_op jit(solution)/shard_map/cross_fwd/pallas_call | solution.py:83
  73.5 5.6 %collective-permute-start.22 = (bf16[2,8,96,768]{3,2,1,0:T(8,128)(2,1)S(1)}, bf16[2,8,96,768]{3,2,1,0:T(8,128)(2,1)S(1)}, u32[]{:S(2)}, u32[]{:S(2)}) collective-permute-start(bf16[2,8,96,768]{3,2,1,0:T(8,128)(2,1)S(1)} %bitcast.50), channel_id=1, source_target_pairs={{0,8},{8,0},{16,24},{24,16},{1,9},{9,1},{17,25},{25,17},{2,10},{10... | collective-permute-start | bytes 7077896 | tf_op jit(solution)/shard_map/ppermute | solution.py:108
  89.3 5.4 %collective-permute-done.26.refs_8_.refs_3_ = bf16[96,1536]{1,0:T(8,128)(2,1)S(1)} collective-permute-done((bf16[96,1536]{1,0:T(8,128)(2,1)S(1)}, bf16[96,1536]{1,0:T(8,128)(2,1)S(1)}, u32[]{:S(2)}, u32[]{:S(2)}) %collective-permute-start.26) | collective-permute-done | bytes 294944 | tf_op jit(solution)/shard_map/ppermute | solution.py:117
  101.5 3.0 %collective-permute-start.35 = (bf16[96,1536]{1,0:T(8,128)(2,1)S(1)}, bf16[96,1536]{1,0:T(8,128)(2,1)S(1)}, u32[]{:S(2)}, u32[]{:S(2)}) collective-permute-start(bf16[96,1536]{1,0:T(8,128)(2,1)S(1)} %collective-permute-done.27.refs_9_.refs_4_), channel_id=1, source_target_pairs={{0,8},{8,0},{16,24},{24,16},{1,9},{9,1},{17,25},{25,17},{2,10},{10... | collective-permute-start | bytes 884744 | tf_op jit(solution)/shard_map/ppermute | solution.py:108
  106.0 3.9 %collective-permute-start.36 = (bf16[96,1536]{1,0:T(8,128)(2,1)S(1)}, bf16[96,1536]{1,0:T(8,128)(2,1)S(1)}, u32[]{:S(2)}, u32[]{:S(2)}) collective-permute-start(bf16[96,1536]{1,0:T(8,128)(2,1)S(1)} %collective-permute-done.32.refs_5_), channel_id=1, source_target_pairs={{0,8},{8,0},{16,24},{24,16},{1,9},{9,1},{17,25},{25,17},{2,10},{10... | collective-permute-start | bytes 884744 | tf_op jit(solution)/shard_map/ppermute | solution.py:108
  120.0 5.8 %collective-permute-done.37.refs_1_ = bf16[128,768]{1,0:T(8,128)(2,1)S(1)} collective-permute-done((bf16[128,768]{1,0:T(8,128)(2,1)S(1)}, bf16[128,768]{1,0:T(8,128)(2,1)S(1)}, u32[]{:S(2)}, u32[]{:S(2)}) %collective-permute-start.37) | collective-permute-done | bytes 196640 | tf_op jit(solution)/shard_map/ppermute | solution.py:111
  128.2 3.0 %collective-permute-done.39.refs_4_.refs_2_ = bf16[128,384]{1,0:T(8,128)(2,1)S(1)} collective-permute-done((bf16[128,384]{1,0:T(8,128)(2,1)S(1)}, bf16[128,384]{1,0:T(8,128)(2,1)S(1)}, u32[]{:S(2)}, u32[]{:S(2)}) %collective-permute-start.39) | collective-permute-done | bytes 98336 | tf_op jit(solution)/shard_map/ppermute | solution.py:111
  135.4 5.6 %self_back.1 = (f32[128,768]{1,0:T(8,128)S(1)}, bf16[128,768]{1,0:T(8,128)(2,1)S(1)}, bf16[4,2,96,640]{3,2,1,0:T(8,128)(2,1)S(1)}, bf16[4,2,96,640]{3,2,1,0:T(8,128)(2,1)S(1)}, f32[8,128]{1,0:T(8,128)S(1)}) custom-call(s32[4]{0:T(128)S(1)} %copy-done.3, bf16[256,1152]{1,0:T(8,128)(2,1)S(1)} %get-tuple-element.421.refs_0_, ...), custom_call_target="tpu_custom_call" | custom-call | bytes 1024 | tf_op jit(solution)/shard_map/self_back/pallas_call | solution.py:83
  143.0 4.8 %collective-permute-done.43.refs_2_ = bf16[4,96,768]{2,1,0:T(8,128)(2,1)S(1)} collective-permute-done((bf16[4,96,768]{2,1,0:T(8,128)(2,1)S(1)}, bf16[4,96,768]{2,1,0:T(8,128)(2,1)S(1)}, u32[]{:S(2)}, u32[]{:S(2)}) %collective-permute-start.43) | collective-permute-done | bytes 589856 | tf_op jit(solution)/shard_map/ppermute | solution.py:117
  148.5 3.7 %gate_back.1 = (f32[128,768]{1,0:T(8,128)S(1)}, bf16[128,768]{1,0:T(8,128)(2,1)S(1)}, f32[128,768]{1,0:T(8,128)S(1)}, bf16[2,8,96,768]{3,2,1,0:T(8,128)(2,1)S(1)...) custom-call(s32[4]{0:T(128)S(1)} %copy-done.3, ...), custom_call_target="tpu_custom_call" | custom-call | bytes 1024 | tf_op jit(solution)/shard_map/gate_back/pallas_call | solution.py:83
  155.4 4.9 %cross_back.2 = (bf16[128,384]{1,0:T(8,128)(2,1)S(1)}, bf16[2,1280,384]{2,1,0:T(8,128)(2,1)S(1)}, f32[8,128]{1,0:T(8,128)S(1)}) custom-call(s32[4]{0:T(128)S(1)} %copy-done.3, s32[1,1280]{1,0:T(1,128)S(1)} %copy-done.9, s32[1,128]{1,0:T(1,128)S(1)} %copy-done.10, bf16[128,768]{1,0:T(8,128)(2,1)S(1)} %get-tuple-element.337.refs_2_, ...), custom_call_target="tpu_custom_call" | custom-call | bytes 1024 | tf_op jit(solution)/shard_map/cross_back/pallas_call | solution.py:83
  163.8 3.4 %cross_weights.2 = (bf16[768,384]{1,0:T(8,128)(2,1)S(1)}, bf16[768,384]{1,0:T(8,128)(2,1)S(1)}, bf16[768,384]{1,0:T(8,128)(2,1)S(1)}, f32[8,128]{1,0:T(8,128)S(1)}) custom-call(s32[4]{0:T(128)S(1)} %copy-done.3, bf16[1280,768]{1,0:T(8,128)(2,1)S(1)} %get-tuple-element.320.refs_0_, bf16[128,768]{1,0:T(8,128)(2,1)S(1)} %get-tuple-element.321.refs_1_.refs_4_, ...), custom_call_target="tpu_custom_call" | custom-call | bytes 1024 | tf_op jit(solution)/shard_map/cross_weights/pallas_call | solution.py:83
  170.5 4.9 %cross_back.3 = (bf16[128,384]{1,0:T(8,128)(2,1)S(1)}, bf16[2,1280,384]{2,1,0:T(8,128)(2,1)S(1)}, f32[8,128]{1,0:T(8,128)S(1)}) custom-call(s32[4]{0:T(128)S(1)} %copy-done.3, s32[1,1280]{1,0:T(1,128)S(1)} %copy-done.9, s32[1,128]{1,0:T(1,128)S(1)} %copy-done.10, bf16[128,768]{1,0:T(8,128)(2,1)S(1)} %get-tuple-element.337.refs_2_, ...), custom_call_target="tpu_custom_call" | custom-call | bytes 1024 | tf_op jit(solution)/shard_map/cross_back/pallas_call | solution.py:83
  178.0 3.4 %cross_weights.3 = (bf16[768,384]{1,0:T(8,128)(2,1)S(1)}, bf16[768,384]{1,0:T(8,128)(2,1)S(1)}, bf16[768,384]{1,0:T(8,128)(2,1)S(1)}, f32[8,128]{1,0:T(8,128)S(1)}) custom-call(s32[4]{0:T(128)S(1)} %copy-done.3, bf16[1280,768]{1,0:T(8,128)(2,1)S(1)} %get-tuple-element.320.refs_0_, bf16[128,768]{1,0:T(8,128)(2,1)S(1)} %get-tuple-element.321.refs_1_.refs_4_, ...), custom_call_target="tpu_custom_call" | custom-call | bytes 1024 | tf_op jit(solution)/shard_map/cross_weights/pallas_call | solution.py:83
  186.9 3.1 %collective-permute-start.57 = (bf16[2,96,640]{2,1,0:T(8,128)(2,1)S(1)}, bf16[2,96,640]{2,1,0:T(8,128)(2,1)S(1)}, u32[]{:S(2)}, u32[]{:S(2)}) collective-permute-start(bf16[2,96,640]{2,1,0:T(8,128)(2,1)S(1)} %get-tuple-element.492), channel_id=1, source_target_pairs={{0,2},{1,3},{2,0},{3,1},{4,6},{5,7},{6,4},{7,5},{8,10},{9,11},{10,... | collective-permute-start | bytes 737288 | tf_op jit(solution)/shard_map/ppermute | solution.py:120
  190.0 8.1 %text_back.1 = (f32[1280,768]{1,0:T(8,128)}, f32[2,768]{1,0:T(2,128)S(1)}, f32[8,128]{1,0:T(8,128)S(1)}) custom-call(s32[4]{0:T(128)S(1)} %copy-done.3, bf16[1280,768]{1,0:T(8,128)(2,1)S(1)} %bitcast.34, f32[1,3072]{1,0:T(1,128)S(1)} %get-tuple-element.314.refs_2_.refs_3_.refs_5_.refs_8_.refs_1_.refs_6_, bf16[768,1536]{1,0:T(8,128)(2,1)S(1)} %get-tuple-element.483.refs_2_, ...), custom_call_target="tpu_custom_call" | custom-call | bytes 1024 | tf_op jit(solution)/shard_map/text_back/pallas_call | solution.py:83
  206.6 3.1 %collective-permute-start.61 = (bf16[2,96,384]{2,1,0:T(8,128)(2,1)S(1)}, bf16[2,96,384]{2,1,0:T(8,128)(2,1)S(1)}, u32[]{:S(2)}, u32[]{:S(2)}) collective-permute-start(bf16[2,96,384]{2,1,0:T(8,128)(2,1)S(1)} %get-tuple-element.507), channel_id=1, source_target_pairs={{0,2},{1,3},{2,0},{3,1},{4,6},{5,7},{6,4},{7,5},{8,10},{9,11},{10,... | collective-permute-start | bytes 442376 | tf_op jit(solution)/shard_map/ppermute | solution.py:120
  218.2 5.0 %collective-permute-done.64.refs_3_ = bf16[1,96,384]{2,1,0:T(8,128)(2,1)S(1)} collective-permute-done((bf16[1,96,384]{2,1,0:T(8,128)(2,1)S(1)}, bf16[1,96,384]{2,1,0:T(8,128)(2,1)S(1)}, u32[]{:S(2)}, u32[]{:S(2)}) %collective-permute-start.64) | collective-permute-done | bytes 73760 | tf_op jit(solution)/shard_map/ppermute | solution.py:120
  224.6 4.1 %collective-permute-start.73 = (bf16[96,2176]{1,0:T(8,128)(2,1)S(1)}, bf16[96,2176]{1,0:T(8,128)(2,1)S(1)}, u32[]{:S(2)}, u32[]{:S(2)}) collective-permute-start(bf16[96,2176]{1,0:T(8,128)(2,1)S(1)} %get-tuple-element.531.refs_0_), channel_id=1, source_target_pairs={{0,8},{8,0},{16,24},{24,16},{1,9},{9,1},{17,25},{25,17},{2,10},{10... | collective-permute-start | bytes 1253384 | tf_op jit(solution)/shard_map/ppermute | solution.py:108
  (213 shorter events, 144.2 us)
Async XLA Ops:
  22.6 14.3 %collective-permute-start.8 = (bf16[4,112,384]{2,1,0:T(8,128)(2,1)S(1)}, bf16[4,112,384]{2,1,0:T(8,128)(2,1)S(1)}, u32[]{:S(2)}, u32[]{:S(2)}) collective-permute-start(bf16[4,112,384]{2,1,0:T(8,128)(2,1)S(1)} %get-tuple-element.293.refs_4_), channel_id=1, source_target_pairs={{0,1},{1,0},{2,3},{3,2},{4,5},{5,4},{6,7},{7,6},{8,9},{9,8},{10,11... | collective-permute-start | bytes 1032200 | tf_op jit(solution)/shard_map/ppermute | solution.py:117
  24.5 12.4 %collective-permute-start.6 = (bf16[4,96,384]{2,1,0:T(8,128)(2,1)S(1)}, bf16[4,96,384]{2,1,0:T(8,128)(2,1)S(1)}, u32[]{:S(2)}, u32[]{:S(2)}) collective-permute-start(bf16[4,96,384]{2,1,0:T(8,128)(2,1)S(1)} %get-tuple-element.292.refs_0_), channel_id=1, source_target_pairs={{0,16},{8,24},{16,0},{24,8},{1,17},{9,25},{17,1},{25,9},{2,18},{10... | collective-permute-start | bytes 884744 | tf_op jit(solution)/shard_map/ppermute | solution.py:111
  37.6 16.0 %collective-permute-start.12 = (bf16[3,768,384]{2,1,0:T(8,128)(2,1)S(1)}, bf16[3,768,384]{2,1,0:T(8,128)(2,1)S(1)}, u32[]{:S(2)}, u32[]{:S(2)}) collective-permute-start(bf16[3,768,384]{2,1,0:T(8,128)(2,1)S(1)} %bitcast.56), channel_id=1, source_target_pairs={{0,8},{8,0},{16,24},{24,16},{1,9},{9,1},{17,25},{25,17},{2,10},{10... | collective-permute-start | bytes 5308424 | tf_op jit(solution)/shard_map/ppermute | solution.py:108
  43.5 18.8 %collective-permute-start.17 = (bf16[4,96,768]{2,1,0:T(8,128)(2,1)S(1)}, bf16[4,96,768]{2,1,0:T(8,128)(2,1)S(1)}, u32[]{:S(2)}, u32[]{:S(2)}) collective-permute-start(bf16[4,96,768]{2,1,0:T(8,128)(2,1)S(1)} %get-tuple-element.344.refs_0_), channel_id=1, source_target_pairs={{0,16},{8,24},{16,0},{24,8},{1,17},{9,25},{17,1},{25,9},{2,18},{10... | collective-permute-start | bytes 1769480 | tf_op jit(solution)/shard_map/ppermute | solution.py:111
  43.7 18.5 %collective-permute-start.15 = (bf16[4,96,768]{2,1,0:T(8,128)(2,1)S(1)}, bf16[4,96,768]{2,1,0:T(8,128)(2,1)S(1)}, u32[]{:S(2)}, u32[]{:S(2)}) collective-permute-start(bf16[4,96,768]{2,1,0:T(8,128)(2,1)S(1)} %get-tuple-element.344.refs_0_), channel_id=1, source_target_pairs={{0,1},{1,0},{2,3},{3,2},{4,5},{5,4},{6,7},{7,6},{8,9},{9,8},{10,11... | collective-permute-start | bytes 1769480 | tf_op jit(solution)/shard_map/ppermute | solution.py:117
  53.7 15.7 %collective-permute-start.21 = (bf16[96,1536]{1,0:T(8,128)(2,1)S(1)}, bf16[96,1536]{1,0:T(8,128)(2,1)S(1)}, u32[]{:S(2)}, u32[]{:S(2)}) collective-permute-start(bf16[96,1536]{1,0:T(8,128)(2,1)S(1)} %copy-done.5), channel_id=1, source_target_pairs={{0,2},{1,3},{2,0},{3,1},{4,6},{5,7},{6,4},{7,5},{8,10},{9,11},{10,... | collective-permute-start | bytes 884744 | tf_op jit(solution)/shard_map/ppermute | solution.py:120
  53.7 15.6 %collective-permute-start.20 = (bf16[96,1536]{1,0:T(8,128)(2,1)S(1)}, bf16[96,1536]{1,0:T(8,128)(2,1)S(1)}, u32[]{:S(2)}, u32[]{:S(2)}) collective-permute-start(bf16[96,1536]{1,0:T(8,128)(2,1)S(1)} %copy-done.5), channel_id=1, source_target_pairs={{0,4},{1,5},{2,6},{3,7},{4,0},{5,1},{6,2},{7,3},{8,12},{9,13},{10,... | collective-permute-start | bytes 884744 | tf_op jit(solution)/shard_map/ppermute | solution.py:120
  81.8 12.9 %collective-permute-start.26 = (bf16[96,1536]{1,0:T(8,128)(2,1)S(1)}, bf16[96,1536]{1,0:T(8,128)(2,1)S(1)}, u32[]{:S(2)}, u32[]{:S(2)}) collective-permute-start(bf16[96,1536]{1,0:T(8,128)(2,1)S(1)} %collective-permute-done.21.refs_3_.refs_5_.refs_1_), channel_id=1, source_target_pairs={{0,1},{1,0},{2,3},{3,2},{4,5},{5,4},{6,7},{7,6},{8,9},{9,8},{10,11... | collective-permute-start | bytes 884744 | tf_op jit(solution)/shard_map/ppermute | solution.py:117
  87.9 12.4 %collective-permute-start.29 = (bf16[4,96,768]{2,1,0:T(8,128)(2,1)S(1)}, bf16[4,96,768]{2,1,0:T(8,128)(2,1)S(1)}, u32[]{:S(2)}, u32[]{:S(2)}) collective-permute-start(bf16[4,96,768]{2,1,0:T(8,128)(2,1)S(1)} %get-tuple-element.390.refs_0_), channel_id=1, source_target_pairs={{0,8},{8,0},{16,24},{24,16},{1,9},{9,1},{17,25},{25,17},{2,10},{10... | collective-permute-start | bytes 1769480 | tf_op jit(solution)/shard_map/ppermute | solution.py:108
  115.1 12.4 %collective-permute-start.40 = (bf16[768,768]{1,0:T(8,128)(2,1)S(1)}, bf16[768,768]{1,0:T(8,128)(2,1)S(1)}, u32[]{:S(2)}, u32[]{:S(2)}) collective-permute-start(bf16[768,768]{1,0:T(8,128)(2,1)S(1)} %get-tuple-element.425), channel_id=1, source_target_pairs={{0,8},{8,0},{16,24},{24,16},{1,9},{9,1},{17,25},{25,17},{2,10},{10... | collective-permute-start | bytes 3538952 | tf_op jit(solution)/shard_map/ppermute | solution.py:108
  118.7 14.6 %collective-permute-start.41 = (bf16[4,96,768]{2,1,0:T(8,128)(2,1)S(1)}, bf16[4,96,768]{2,1,0:T(8,128)(2,1)S(1)}, u32[]{:S(2)}, u32[]{:S(2)}) collective-permute-start(bf16[4,96,768]{2,1,0:T(8,128)(2,1)S(1)} %get-tuple-element.428), channel_id=1, source_target_pairs={{0,1},{1,0},{2,3},{3,2},{4,5},{5,4},{6,7},{7,6},{8,9},{9,8},{10,11... | collective-permute-start | bytes 1769480 | tf_op jit(solution)/shard_map/ppermute | solution.py:117
  134.1 13.7 %collective-permute-start.43 = (bf16[4,96,768]{2,1,0:T(8,128)(2,1)S(1)}, bf16[4,96,768]{2,1,0:T(8,128)(2,1)S(1)}, u32[]{:S(2)}, u32[]{:S(2)}) collective-permute-start(bf16[4,96,768]{2,1,0:T(8,128)(2,1)S(1)} %get-tuple-element.437), channel_id=1, source_target_pairs={{0,1},{1,0},{2,3},{3,2},{4,5},{5,4},{6,7},{7,6},{8,9},{9,8},{10,11... | collective-permute-start | bytes 1769480 | tf_op jit(solution)/shard_map/ppermute | solution.py:117
  154.5 14.8 %collective-permute-start.50 = (bf16[2,96,768]{2,1,0:T(8,128)(2,1)S(1)}, bf16[2,96,768]{2,1,0:T(8,128)(2,1)S(1)}, u32[]{:S(2)}, u32[]{:S(2)}) collective-permute-start(bf16[2,96,768]{2,1,0:T(8,128)(2,1)S(1)} %get-tuple-element.465), channel_id=1, source_target_pairs={{0,2},{1,3},{2,0},{3,1},{4,6},{5,7},{6,4},{7,5},{8,10},{9,11},{10,... | collective-permute-start | bytes 884744 | tf_op jit(solution)/shard_map/ppermute | solution.py:120
  162.3 13.8 %collective-permute-start.49 = (bf16[4,96,768]{2,1,0:T(8,128)(2,1)S(1)}, bf16[4,96,768]{2,1,0:T(8,128)(2,1)S(1)}, u32[]{:S(2)}, u32[]{:S(2)}) collective-permute-start(bf16[4,96,768]{2,1,0:T(8,128)(2,1)S(1)} %get-tuple-element.463), channel_id=1, source_target_pairs={{0,16},{8,24},{16,0},{24,8},{1,17},{9,25},{17,1},{25,9},{2,18},{10... | collective-permute-start | bytes 1769480 | tf_op jit(solution)/shard_map/ppermute | solution.py:111
  167.1 15.7 %collective-permute-start.51 = (bf16[768,384]{1,0:T(8,128)(2,1)S(1)}, bf16[768,384]{1,0:T(8,128)(2,1)S(1)}, u32[]{:S(2)}, u32[]{:S(2)}) collective-permute-start(bf16[768,384]{1,0:T(8,128)(2,1)S(1)} %get-tuple-element.472), channel_id=1, source_target_pairs={{0,8},{8,0},{16,24},{24,16},{1,9},{9,1},{17,25},{25,17},{2,10},{10... | collective-permute-start | bytes 1769480 | tf_op jit(solution)/shard_map/ppermute | solution.py:108
  168.8 14.1 %collective-permute-start.52 = (bf16[768,384]{1,0:T(8,128)(2,1)S(1)}, bf16[768,384]{1,0:T(8,128)(2,1)S(1)}, u32[]{:S(2)}, u32[]{:S(2)}) collective-permute-start(bf16[768,384]{1,0:T(8,128)(2,1)S(1)} %get-tuple-element.473), channel_id=1, source_target_pairs={{0,8},{8,0},{16,24},{24,16},{1,9},{9,1},{17,25},{25,17},{2,10},{10... | collective-permute-start | bytes 1769480 | tf_op jit(solution)/shard_map/ppermute | solution.py:108
  168.9 14.0 %collective-permute-start.53 = (bf16[768,384]{1,0:T(8,128)(2,1)S(1)}, bf16[768,384]{1,0:T(8,128)(2,1)S(1)}, u32[]{:S(2)}, u32[]{:S(2)}) collective-permute-start(bf16[768,384]{1,0:T(8,128)(2,1)S(1)} %get-tuple-element.474), channel_id=1, source_target_pairs={{0,8},{8,0},{16,24},{24,16},{1,9},{9,1},{17,25},{25,17},{2,10},{10... | collective-permute-start | bytes 1769480 | tf_op jit(solution)/shard_map/ppermute | solution.py:108
  169.3 12.8 %collective-permute-start.54 = (bf16[4,96,640]{2,1,0:T(8,128)(2,1)S(1)}, bf16[4,96,640]{2,1,0:T(8,128)(2,1)S(1)}, u32[]{:S(2)}, u32[]{:S(2)}) collective-permute-start(bf16[4,96,640]{2,1,0:T(8,128)(2,1)S(1)} %get-tuple-element.475), channel_id=1, source_target_pairs={{0,1},{1,0},{2,3},{3,2},{4,5},{5,4},{6,7},{7,6},{8,9},{9,8},{10,11... | collective-permute-start | bytes 1474568 | tf_op jit(solution)/shard_map/ppermute | solution.py:117
  176.8 21.3 %collective-permute-start.59 = (bf16[4,96,768]{2,1,0:T(8,128)(2,1)S(1)}, bf16[4,96,768]{2,1,0:T(8,128)(2,1)S(1)}, u32[]{:S(2)}, u32[]{:S(2)}) collective-permute-start(bf16[4,96,768]{2,1,0:T(8,128)(2,1)S(1)} %get-tuple-element.495), channel_id=1, source_target_pairs={{0,1},{1,0},{2,3},{3,2},{4,5},{5,4},{6,7},{7,6},{8,9},{9,8},{10,11... | collective-permute-start | bytes 1769480 | tf_op jit(solution)/shard_map/ppermute | solution.py:117
  183.8 19.8 %collective-permute-start.55 = (bf16[4,2,96,384]{3,2,1,0:T(8,128)(2,1)S(1)}, bf16[4,2,96,384]{3,2,1,0:T(8,128)(2,1)S(1)}, u32[]{:S(2)}, u32[]{:S(2)}) collective-permute-start(bf16[4,2,96,384]{3,2,1,0:T(8,128)(2,1)S(1)} %get-tuple-element.479), channel_id=1, source_target_pairs={{0,16},{8,24},{16,0},{24,8},{1,17},{9,25},{17,1},{25,9},{2,18},{10... | collective-permute-start | bytes 1769480 | tf_op jit(solution)/shard_map/ppermute | solution.py:111
  185.6 15.5 %collective-permute-start.56 = (bf16[4,96,384]{2,1,0:T(8,128)(2,1)S(1)}, bf16[4,96,384]{2,1,0:T(8,128)(2,1)S(1)}, u32[]{:S(2)}, u32[]{:S(2)}) collective-permute-start(bf16[4,96,384]{2,1,0:T(8,128)(2,1)S(1)} %get-tuple-element.490), channel_id=1, source_target_pairs={{0,1},{1,0},{2,3},{3,2},{4,5},{5,4},{6,7},{7,6},{8,9},{9,8},{10,11... | collective-permute-start | bytes 884744 | tf_op jit(solution)/shard_map/ppermute | solution.py:117
  205.6 18.2 %collective-permute-start.66 = (bf16[4,96,768]{2,1,0:T(8,128)(2,1)S(1)}, bf16[4,96,768]{2,1,0:T(8,128)(2,1)S(1)}, u32[]{:S(2)}, u32[]{:S(2)}) collective-permute-start(bf16[4,96,768]{2,1,0:T(8,128)(2,1)S(1)} %get-tuple-element.522), channel_id=1, source_target_pairs={{0,16},{8,24},{16,0},{24,8},{1,17},{9,25},{17,1},{25,9},{2,18},{10... | collective-permute-start | bytes 1769480 | tf_op jit(solution)/shard_map/ppermute | solution.py:111
  224.6 16.1 %collective-permute-start.73 = (bf16[96,2176]{1,0:T(8,128)(2,1)S(1)}, bf16[96,2176]{1,0:T(8,128)(2,1)S(1)}, u32[]{:S(2)}, u32[]{:S(2)}) collective-permute-start(bf16[96,2176]{1,0:T(8,128)(2,1)S(1)} %get-tuple-element.531.refs_0_), channel_id=1, source_target_pairs={{0,8},{8,0},{16,24},{24,16},{1,9},{9,1},{17,25},{25,17},{2,10},{10... | collective-permute-start | bytes 1253384 | tf_op jit(solution)/shard_map/ppermute | solution.py:108
  228.7 12.0 %collective-permute-start.74 = (bf16[96,2176]{1,0:T(8,128)(2,1)S(1)}, bf16[96,2176]{1,0:T(8,128)(2,1)S(1)}, u32[]{:S(2)}, u32[]{:S(2)}) collective-permute-start(bf16[96,2176]{1,0:T(8,128)(2,1)S(1)} %collective-permute-done.72.refs_1_), channel_id=1, source_target_pairs={{0,8},{8,0},{16,24},{24,16},{1,9},{9,1},{17,25},{25,17},{2,10},{10... | collective-permute-start | bytes 1253384 | tf_op jit(solution)/shard_map/ppermute | solution.py:108
  (66 other events, 538.2 us)
